TPU v7x, 256 devices: a whole 4x4x8 slice. The times are simulated.
256 devices in a mesh: grp: 8 (over z), dev: 32 (over x, y, core).
Axes of the slice: x: 4, y: 4, z: 8, core: 2. Of those that a mesh axis runs over, the one named last changes fastest.
Arguments:
- incident: bfloat16 [1024, 128, 128], P(('grp', 'dev')), may hold values from -6 to 6
- tmatrix: bfloat16 [1024, 128, 128], P(('grp', 'dev')), may hold values from -0.5 to 0.5
- blocks: bfloat16 [32768, 128, 128], P(('grp', 'dev')), may hold values from -0.09375 to 0.09375
- need: int32 [256, 32, 4], P(('grp', 'dev')), may hold values from 0 to 3, as said below
- pair_src: int32 [256, 512], P(('grp', 'dev')), may hold values from 0 to 127
- pair_tgt: int32 [256, 512], P(('grp', 'dev')), may hold values from 0 to 3
- pair_blk: int32 [256, 512], P(('grp', 'dev')), may hold values from 0 to 127
- pair_count: int32 [256], P(('grp', 'dev')), may hold values from 128 to 512, as said below
- factor: float32 [1024, 2048], P(('grp', 'dev')), may hold values from -24 to 24
- harmonics: bfloat16 [2048, 128], replicated, may hold values from -0.015625 to 0.015625
- owner: int32 [2048], replicated, may hold values from 0 to 2047, each once
Outputs:
- amplitudes: float32 [2048, 128], P(('grp', 'dev'))
Inputs may be any that keep to these rules, and one draw needn't show every extreme that they name: Each row need[k, j] lists 4 distinct local spheres of peer j. `pair_count`: some device has exactly 512 live pairs.
All inputs are finite; a program needn't handle non-finite values.
Results may differ from a plain program's by a relative error of at most 0.0075.
Values may be sent and summed in bfloat16 or wider, within the bound.
No kernel may reach another device: no remote copies, remote signals or barrier semaphores. Data moves between devices by JAX's collectives and lax.ppermute only.
A program may use at most 128 MiB of HBM per device.

v0:
```python
import jax
import jax.numpy as jnp
from jax import lax
from jax.sharding import PartitionSpec as P

SWEEPS = 2


def apply_tmatrix(tmatrix, field):
    return jnp.einsum("skl,slq->skq", tmatrix, field, preferred_element_type=jnp.float32).astype(
        jnp.bfloat16
    )


def scatter_pairs(sources, blocks, source_ids, target_ids, block_ids, live_count, spheres):
    pair_total = source_ids.shape[0]
    block_rows = pair_total // 4
    sphere_ids = jnp.arange(spheres, dtype=jnp.int32)

    def advance(running, offset):
        chosen_src = lax.dynamic_slice_in_dim(source_ids, offset, block_rows)
        chosen_tgt = lax.dynamic_slice_in_dim(target_ids, offset, block_rows)
        chosen_blk = lax.dynamic_slice_in_dim(block_ids, offset, block_rows)
        source_tiles = jnp.take(sources, chosen_src, axis=0)
        operators = jnp.take(blocks, chosen_blk, axis=0)
        contrib = jnp.einsum(
            "pkl,plq->pkq", operators, source_tiles, preferred_element_type=jnp.float32
        )
        pair_live = offset + jnp.arange(block_rows, dtype=jnp.int32) < live_count
        selector = ((chosen_tgt[None, :] == sphere_ids[:, None]) & pair_live[None, :]).astype(
            jnp.float32
        )
        added = jnp.einsum("sp,pkq->skq", selector, contrib, precision=lax.Precision.HIGHEST)
        return (running + added, None)

    start_rows = jnp.arange(4, dtype=jnp.int32) * block_rows
    initial = jnp.zeros((spheres, sources.shape[1], sources.shape[2]), jnp.float32)
    result, unused = lax.scan(advance, initial, start_rows)
    return result


def body(
    incident,
    tmatrix,
    blocks,
    need,
    pair_src,
    pair_tgt,
    pair_blk,
    pair_count,
    factor,
    harmonics,
    owner,
):
    spheres, coeff_rows, columns = incident.shape
    n_dev = lax.axis_size("dev")
    needed = need[0]
    incident_wide = incident.astype(jnp.float32)
    coeff = apply_tmatrix(tmatrix, incident)
    group_ids = (jnp.arange(n_dev, dtype=jnp.int32)[:, None] * spheres + needed).reshape(-1)
    source_ids = jnp.take(group_ids, pair_src[0])
    for sweep_index in range(SWEEPS):
        sources = lax.all_gather(coeff, "dev", axis=0, tiled=True)
        scattered = scatter_pairs(
            sources, blocks, source_ids, pair_tgt[0], pair_blk[0], pair_count[0], spheres
        )
        field = (incident_wide + scattered).astype(jnp.bfloat16)
        coeff = apply_tmatrix(tmatrix, field)
    table = jnp.take(harmonics, owner, axis=0).astype(jnp.float32)
    phases = jnp.take(factor, owner, axis=1)
    weighted = (phases[:, :, None] * table[None]).astype(jnp.bfloat16)
    amplitude = jnp.einsum("sdl,slq->dq", weighted, coeff, preferred_element_type=jnp.float32)
    return lax.psum_scatter(amplitude, ("grp", "dev"), scatter_dimension=0, tiled=True)


def solution(mesh):
    return jax.shard_map(
        body,
        mesh=mesh,
        in_specs=(
            P(("grp", "dev"), None, None),
            P(("grp", "dev"), None, None),
            P(("grp", "dev"), None, None),
            P(("grp", "dev"), None, None),
            P(("grp", "dev"), None),
            P(("grp", "dev"), None),
            P(("grp", "dev"), None),
            P(("grp", "dev")),
            P(("grp", "dev"), None),
            P(),
            P(),
        ),
        out_specs=P(("grp", "dev"), None),
        check_vma=False,
    )
```

profile of v0, /device:TPU:1, one launch (start us, length us, event | category | flops | bytes accessed | tf_op | source)
XLA Modules:
  0.0 660.5 jit_solution(9000928349111691345)
XLA Ops:
  6.5 1.9 convolution_convert_fusion.2
  10.3 3.3 gather_fusion.6
  14.3 50.8 %all-gather.3.cloned.1.call-done = bf16[128,128,128]{2,1,0:T(8,128)(2,1)} async-done(((bf16[4,128,128]{2,1,0:T(8,128)(2,1)}), bf16[128,128,128]{2,1,0:T(8,128)(2,1)}) %all-gather.3.cloned.1.call-update) | async-done | bytes 4194320 | tf_op jit(solution)/shard_map/all_gather | solution.py:63
  65.1 138.4 %while.22 = (s32[]{:T(128)}, f32[4,128,128]{2,0,1:T(4,128)S(1)}, s32[4]{0:T(128)S(1)}, s32[512]{0:T(512)}, s32[]{:T(128)}, /*index=5*/s32[512]{0:T(512)}, bf16[1...) while((s32[]{:T(128)}, f32[4,128,128]{2,0,1:T(4,128)S(1)}, ...), condition=%wide.region_1.3_spmd.clone, body=%wide.region_0.0_spmd.clone.sunk | while | flops 641864448 | bytes 42482108 | solution.py:38
  68.7 5.2 gather_fusion
  73.9 5.2 gather_fusion.1
  79.1 8.0 %fusion.68 = f32[128,128,128]{2,1,0:T(8,128)} fusion(bf16[128,128,128]{2,1,0:T(8,128)(2,1)} %gather_fusion, bf16[128,128,128]{2,1,0:T(8,128)(2,1)} %gather_fusion.1, pred[128]{0:T(512)(128)(4,1)S(1)} %get-tuple-element.335, pred[128]{0:T(512)(128)(4,1)S(1)} %get-tuple-element.336), kind=kOutput, calls=%fused_computation.11.clone.1 | convolution fusion | flops 541065216 | bytes 16777472 | tf_op jit(solution)/shard_map/while/body/eval_jaxpr/pkl,plq->pkq/dot_general | solution.py:26
  87.9 1.3 add_compare_fusion.4
  89.2 10.5 %fusion.69 = f32[4,128,128]{2,0,1:T(4,128)S(1)} fusion(f32[128,128,128]{2,1,0:T(8,128)} %fusion.68, f32[4,128,128]{2,0,1:T(4,128)S(1)} %get-tuple-element.363, pred[]{:T(512)S(6)} %compare.6, s32[128]{0:T(128)S(1)} %dynamic_slice.46, pred[128]{0:T(512)(128)(4,1)S(1)} %add_compare_fusion.4), kind=kOutput, calls=%fused_computation.17.clone.1 | convolution fusion | flops 100795392 | bytes 8913537 | tf_op jit(solution)/shard_map/while/body/eval_jaxpr/sp,pkq->skq/dot_general | solution.py:33
  103.3 5.2 gather_fusion
  108.5 5.2 gather_fusion.1
  113.7 8.0 %fusion.68 = f32[128,128,128]{2,1,0:T(8,128)} fusion(bf16[128,128,128]{2,1,0:T(8,128)(2,1)} %gather_fusion, bf16[128,128,128]{2,1,0:T(8,128)(2,1)} %gather_fusion.1, pred[128]{0:T(512)(128)(4,1)S(1)} %get-tuple-element.335, pred[128]{0:T(512)(128)(4,1)S(1)} %get-tuple-element.336), kind=kOutput, calls=%fused_computation.11.clone.1 | convolution fusion | flops 541065216 | bytes 16777472 | tf_op jit(solution)/shard_map/while/body/eval_jaxpr/pkl,plq->pkq/dot_general | solution.py:26
  122.4 1.3 add_compare_fusion.4
  123.8 10.5 %fusion.69 = f32[4,128,128]{2,0,1:T(4,128)S(1)} fusion(f32[128,128,128]{2,1,0:T(8,128)} %fusion.68, f32[4,128,128]{2,0,1:T(4,128)S(1)} %get-tuple-element.363, pred[]{:T(512)S(6)} %compare.6, s32[128]{0:T(128)S(1)} %dynamic_slice.46, pred[128]{0:T(512)(128)(4,1)S(1)} %add_compare_fusion.4), kind=kOutput, calls=%fused_computation.17.clone.1 | convolution fusion | flops 100795392 | bytes 8913537 | tf_op jit(solution)/shard_map/while/body/eval_jaxpr/sp,pkq->skq/dot_general | solution.py:33
  137.8 5.2 gather_fusion
  143.0 5.2 gather_fusion.1
  148.3 8.0 %fusion.68 = f32[128,128,128]{2,1,0:T(8,128)} fusion(bf16[128,128,128]{2,1,0:T(8,128)(2,1)} %gather_fusion, bf16[128,128,128]{2,1,0:T(8,128)(2,1)} %gather_fusion.1, pred[128]{0:T(512)(128)(4,1)S(1)} %get-tuple-element.335, pred[128]{0:T(512)(128)(4,1)S(1)} %get-tuple-element.336), kind=kOutput, calls=%fused_computation.11.clone.1 | convolution fusion | flops 541065216 | bytes 16777472 | tf_op jit(solution)/shard_map/while/body/eval_jaxpr/pkl,plq->pkq/dot_general | solution.py:26
  157.0 1.3 add_compare_fusion.4
  158.4 10.5 %fusion.69 = f32[4,128,128]{2,0,1:T(4,128)S(1)} fusion(f32[128,128,128]{2,1,0:T(8,128)} %fusion.68, f32[4,128,128]{2,0,1:T(4,128)S(1)} %get-tuple-element.363, pred[]{:T(512)S(6)} %compare.6, s32[128]{0:T(128)S(1)} %dynamic_slice.46, pred[128]{0:T(512)(128)(4,1)S(1)} %add_compare_fusion.4), kind=kOutput, calls=%fused_computation.17.clone.1 | convolution fusion | flops 100795392 | bytes 8913537 | tf_op jit(solution)/shard_map/while/body/eval_jaxpr/sp,pkq->skq/dot_general | solution.py:33
  172.4 5.2 gather_fusion
  177.6 5.2 gather_fusion.1
  182.8 8.0 %fusion.68 = f32[128,128,128]{2,1,0:T(8,128)} fusion(bf16[128,128,128]{2,1,0:T(8,128)(2,1)} %gather_fusion, bf16[128,128,128]{2,1,0:T(8,128)(2,1)} %gather_fusion.1, pred[128]{0:T(512)(128)(4,1)S(1)} %get-tuple-element.335, pred[128]{0:T(512)(128)(4,1)S(1)} %get-tuple-element.336), kind=kOutput, calls=%fused_computation.11.clone.1 | convolution fusion | flops 541065216 | bytes 16777472 | tf_op jit(solution)/shard_map/while/body/eval_jaxpr/pkl,plq->pkq/dot_general | solution.py:26
  191.6 1.3 add_compare_fusion.4
  193.0 10.5 %fusion.69 = f32[4,128,128]{2,0,1:T(4,128)S(1)} fusion(f32[128,128,128]{2,1,0:T(8,128)} %fusion.68, f32[4,128,128]{2,0,1:T(4,128)S(1)} %get-tuple-element.363, pred[]{:T(512)S(6)} %compare.6, s32[128]{0:T(128)S(1)} %dynamic_slice.46, pred[128]{0:T(512)(128)(4,1)S(1)} %add_compare_fusion.4), kind=kOutput, calls=%fused_computation.17.clone.1 | convolution fusion | flops 100795392 | bytes 8913537 | tf_op jit(solution)/shard_map/while/body/eval_jaxpr/sp,pkq->skq/dot_general | solution.py:33
  205.4 5.5 gather_fusion.4
  211.5 6.2 gather_fusion.5
  218.1 37.3 %all-gather.5.cloned.1.call-done = bf16[128,128,128]{2,1,0:T(8,128)(2,1)} async-done(((bf16[4,128,128]{2,1,0:T(8,128)(2,1)}), bf16[128,128,128]{2,1,0:T(8,128)(2,1)}) %all-gather.5.cloned.1.call-update) | async-done | bytes 4194320 | tf_op jit(solution)/shard_map/all_gather | solution.py:63
  255.4 138.3 %while.23 = (s32[]{:T(128)}, f32[4,128,128]{2,0,1:T(4,128)S(1)}, s32[4]{0:T(128)S(1)}, s32[512]{0:T(512)}, s32[]{:T(128)}, /*index=5*/s32[512]{0:T(512)}, bf16[1...) while((s32[]{:T(128)}, f32[4,128,128]{2,0,1:T(4,128)S(1)}, ...), condition=%wide.region_3.5_spmd.clone, body=%wide.region_2.4_spmd.clone.sunk | while | flops 641864448 | bytes 42482108 | solution.py:38
  258.9 5.2 gather_fusion.2
  264.1 5.2 gather_fusion.3
  269.3 8.0 %fusion.74 = f32[128,128,128]{2,1,0:T(8,128)} fusion(bf16[128,128,128]{2,1,0:T(8,128)(2,1)} %gather_fusion.2, bf16[128,128,128]{2,1,0:T(8,128)(2,1)} %gather_fusion.3, pred[128]{0:T(512)(128)(4,1)S(1)} %get-tuple-element.348, pred[128]{0:T(512)(128)(4,1)S(1)} %get-tuple-element.349), kind=kOutput, calls=%fused_computation.33.clone.1 | convolution fusion | flops 541065216 | bytes 16777472 | tf_op jit(solution)/shard_map/while/body/eval_jaxpr/pkl,plq->pkq/dot_general | solution.py:26
  278.1 1.3 add_compare_fusion.5
  279.4 10.5 %fusion.75 = f32[4,128,128]{2,0,1:T(4,128)S(1)} fusion(f32[128,128,128]{2,1,0:T(8,128)} %fusion.74, f32[4,128,128]{2,0,1:T(4,128)S(1)} %get-tuple-element.399, pred[]{:T(512)S(6)} %compare.7, s32[128]{0:T(128)S(1)} %dynamic_slice.48, pred[128]{0:T(512)(128)(4,1)S(1)} %add_compare_fusion.5), kind=kOutput, calls=%fused_computation.39.clone.1 | convolution fusion | flops 100795392 | bytes 8913537 | tf_op jit(solution)/shard_map/while/body/eval_jaxpr/sp,pkq->skq/dot_general | solution.py:33
  293.4 5.2 gather_fusion.2
  298.6 5.2 gather_fusion.3
  303.9 8.0 %fusion.74 = f32[128,128,128]{2,1,0:T(8,128)} fusion(bf16[128,128,128]{2,1,0:T(8,128)(2,1)} %gather_fusion.2, bf16[128,128,128]{2,1,0:T(8,128)(2,1)} %gather_fusion.3, pred[128]{0:T(512)(128)(4,1)S(1)} %get-tuple-element.348, pred[128]{0:T(512)(128)(4,1)S(1)} %get-tuple-element.349), kind=kOutput, calls=%fused_computation.33.clone.1 | convolution fusion | flops 541065216 | bytes 16777472 | tf_op jit(solution)/shard_map/while/body/eval_jaxpr/pkl,plq->pkq/dot_general | solution.py:26
  314.0 10.5 %fusion.75 = f32[4,128,128]{2,0,1:T(4,128)S(1)} fusion(f32[128,128,128]{2,1,0:T(8,128)} %fusion.74, f32[4,128,128]{2,0,1:T(4,128)S(1)} %get-tuple-element.399, pred[]{:T(512)S(6)} %compare.7, s32[128]{0:T(128)S(1)} %dynamic_slice.48, pred[128]{0:T(512)(128)(4,1)S(1)} %add_compare_fusion.5), kind=kOutput, calls=%fused_computation.39.clone.1 | convolution fusion | flops 100795392 | bytes 8913537 | tf_op jit(solution)/shard_map/while/body/eval_jaxpr/sp,pkq->skq/dot_general | solution.py:33
  328.0 5.2 gather_fusion.2
  333.2 5.2 gather_fusion.3
  338.4 8.0 %fusion.74 = f32[128,128,128]{2,1,0:T(8,128)} fusion(bf16[128,128,128]{2,1,0:T(8,128)(2,1)} %gather_fusion.2, bf16[128,128,128]{2,1,0:T(8,128)(2,1)} %gather_fusion.3, pred[128]{0:T(512)(128)(4,1)S(1)} %get-tuple-element.348, pred[128]{0:T(512)(128)(4,1)S(1)} %get-tuple-element.349), kind=kOutput, calls=%fused_computation.33.clone.1 | convolution fusion | flops 541065216 | bytes 16777472 | tf_op jit(solution)/shard_map/while/body/eval_jaxpr/pkl,plq->pkq/dot_general | solution.py:26
  347.2 1.3 add_compare_fusion.5
  348.6 10.5 %fusion.75 = f32[4,128,128]{2,0,1:T(4,128)S(1)} fusion(f32[128,128,128]{2,1,0:T(8,128)} %fusion.74, f32[4,128,128]{2,0,1:T(4,128)S(1)} %get-tuple-element.399, pred[]{:T(512)S(6)} %compare.7, s32[128]{0:T(128)S(1)} %dynamic_slice.48, pred[128]{0:T(512)(128)(4,1)S(1)} %add_compare_fusion.5), kind=kOutput, calls=%fused_computation.39.clone.1 | convolution fusion | flops 100795392 | bytes 8913537 | tf_op jit(solution)/shard_map/while/body/eval_jaxpr/sp,pkq->skq/dot_general | solution.py:33
  362.6 5.2 gather_fusion.2
  367.8 5.2 gather_fusion.3
  373.0 8.0 %fusion.74 = f32[128,128,128]{2,1,0:T(8,128)} fusion(bf16[128,128,128]{2,1,0:T(8,128)(2,1)} %gather_fusion.2, bf16[128,128,128]{2,1,0:T(8,128)(2,1)} %gather_fusion.3, pred[128]{0:T(512)(128)(4,1)S(1)} %get-tuple-element.348, pred[128]{0:T(512)(128)(4,1)S(1)} %get-tuple-element.349), kind=kOutput, calls=%fused_computation.33.clone.1 | convolution fusion | flops 541065216 | bytes 16777472 | tf_op jit(solution)/shard_map/while/body/eval_jaxpr/pkl,plq->pkq/dot_general | solution.py:26
  383.1 10.5 %fusion.75 = f32[4,128,128]{2,0,1:T(4,128)S(1)} fusion(f32[128,128,128]{2,1,0:T(8,128)} %fusion.74, f32[4,128,128]{2,0,1:T(4,128)S(1)} %get-tuple-element.399, pred[]{:T(512)S(6)} %compare.7, s32[128]{0:T(128)S(1)} %dynamic_slice.48, pred[128]{0:T(512)(128)(4,1)S(1)} %add_compare_fusion.5), kind=kOutput, calls=%fused_computation.39.clone.1 | convolution fusion | flops 100795392 | bytes 8913537 | tf_op jit(solution)/shard_map/while/body/eval_jaxpr/sp,pkq->skq/dot_general | solution.py:33
  393.8 2.3 convolution_bitcast_fusion
  396.2 256.5 %all-reduce.3.cloned.1.call-done = f32[2048,128]{1,0:T(8,128)} async-done(((f32[2048,128]{1,0:T(8,128)}), f32[2048,128]{1,0:T(8,128)}) %all-reduce.3.cloned.1.call-update) | async-done | bytes 1048592
  (81 shorter events, 26.9 us)
Async XLA Ops:
  6.5 205.0 %copy-start = (bf16[2048,128]{1,0:T(8,128)(2,1)S(1)}, bf16[2048,128]{1,0:T(8,128)(2,1)}, u32[]{:S(2)}) copy-start(bf16[2048,128]{1,0:T(8,128)(2,1)} %param.26) | copy-start | bytes 1572868
  6.5 58.6 %all-gather.3.cloned.1.call-start = ((), (), s32[]{:S(2)}) async-start(), calls=%async_computation | async-start | bytes 4325376 | tf_op jit(solution)/shard_map/all_gather | solution.py:63
  8.4 247.0 %all-gather.5.cloned.1.call-start = ((), (), s32[]{:S(2)}) async-start(), calls=%async_computation.1 | async-start | bytes 4325376 | tf_op jit(solution)/shard_map/all_gather | solution.py:63
  65.1 138.4 %copy-start.1 = (bf16[4,128,128]{2,1,0:T(8,128)(2,1)S(1)}, bf16[4,128,128]{2,1,0:T(8,128)(2,1)}, u32[]{:S(2)}) copy-start(bf16[4,128,128]{2,1,0:T(8,128)(2,1)} %param.17) | copy-start | bytes 393220
  65.1 138.5 %copy-start.2 = (bf16[4,128,128]{2,1,0:T(8,128)(2,1)S(1)}, bf16[4,128,128]{2,1,0:T(8,128)(2,1)}, u32[]{:S(2)}) copy-start(bf16[4,128,128]{2,1,0:T(8,128)(2,1)} %param.18) | copy-start | bytes 393220
  65.1 139.8 %copy-start.3 = (f32[4,2048]{1,0:T(4,128)S(1)}, f32[4,2048]{1,0:T(4,128)}, u32[]{:S(2)}) copy-start(f32[4,2048]{1,0:T(4,128)} %param.25) | copy-start | bytes 98308
  65.1 140.2 %copy-start.4 = (s32[2048]{0:T(1024)S(1)}, s32[2048]{0:T(1024)}, u32[]{:S(2)}) copy-start(s32[2048]{0:T(1024)} %param.27) | copy-start | bytes 24580
  204.7 448.0 %all-reduce.3.cloned.1.call-start = ((), (), s32[]{:S(2)}) async-start(), calls=%async_computation.2 | async-start | bytes 2097152
Sparse Core Ops, SparseCore 0:
  9.9 55.2 all-gather.2
  204.8 50.4 all-gather.4
  396.3 256.3 all-reduce.2
where the time goes:
time: 663 us; the launch traced here: 660 us
  waiting for transfers between devices  345 us (52%)
  matrix products  153 us (23%)
  local copies, waits for them, and re-layouts  113 us (17%)
  other arithmetic  19.3 us (3%)
  loops' own time  16.8 us (3%)
  between operations  13.3 us (2%)
    unnamed x4, waiting for transfers between devices  257 us
    all_gather x2, waiting for transfers between devices, body(): sources = lax.all_gather(coeff, 'dev', axis=0, tiled=True)  88.1 us
    dot_general x8, matrix products, advance(): jnp.einsum('sp,pkq->skq', selector, contrib, precision=lax.Precision.HIGH...  84.1 us
    dot_general x8, matrix products, advance(): jnp.einsum('pkl,plq->pkq', operators, source_tiles, preferred_element_typ...  64.2 us
    gather x8, local copies, waits for them, and re-layouts, advance(): operators = jnp.take(blocks, chosen_blk, axis=0)  41.7 us
    gather x8, local copies, waits for them, and re-layouts, advance(): source_tiles = jnp.take(sources, chosen_src, axis=0)  41.6 us
    another operation x2, loops' own time, scatter_pairs(): result, unused = lax.scan(advance, initial, start_rows)  16.8 us
  transfers between devices with their start and end apart: 3, of which 3 were waited for; matrix products, arithmetic and copies ran while one was open for 3% of the time, Pallas kernels for 0%

commit v1 on v0

v1 whole, which is shorter than its diff:
```python
import jax
import jax.numpy as jnp
from jax import lax
from jax.experimental import pallas as pl
from jax.experimental.pallas import tpu as pltpu
from jax.sharding import PartitionSpec as P

SIDE = 4
OWN = 4
SOURCES = 2 * SIDE * SIDE * OWN
BLOCKS = 128
PAIRS = 512
TILE = 128
JOIN = 8
WIDE = 4
ROOM = PAIRS + JOIN
LISTS = 2 * OWN
GROUPS = PAIRS // JOIN + OWN + WIDE

SMEM = pl.BlockSpec(memory_space=pltpu.SMEM)
VMEM = pl.BlockSpec(memory_space=pltpu.VMEM)
ANY = pl.BlockSpec(memory_space=pl.ANY)


def device_of(x, y, core):
    return ((x % SIDE) * SIDE + y % SIDE) * 2 + core


def moves(step):
    spots = [(x, y, c) for x in range(SIDE) for y in range(SIDE) for c in range(2)]
    return [(device_of(*spot), device_of(*step(*spot))) for spot in spots]


def along_first(shift):
    return moves(lambda x, y, c: (x + shift, y, c) if c == 0 else (x, y + shift, c))


def along_second(shift):
    return moves(lambda x, y, c: (x, y + shift, c) if c == 0 else (x + shift, y, c))


SWAP = moves(lambda x, y, c: (x, y, 1 - c))


def send(values, pairs):
    return lax.ppermute(values, "dev", pairs)


def spread(coeff):
    half = OWN // 2
    first3 = send(coeff, along_first(1))
    first1 = send(coeff, along_first(-1))
    first2a = send(first3[:half], along_first(1))
    first2b = send(first1[half:], along_first(-1))
    row = jnp.concatenate([coeff, first1, first2a, first2b, first3])
    half = SIDE * OWN // 2
    second3 = send(row, along_second(1))
    second1 = send(row, along_second(-1))
    other0 = send(row, SWAP)
    second2a = send(second3[:half], along_second(1))
    second2b = send(second1[half:], along_second(-1))
    other3 = send(second3, SWAP)
    other1 = send(second1, SWAP)
    other2a = send(second2a, SWAP)
    other2b = send(second2b, SWAP)
    early = (row, second1, second3, other0, other1, other3)
    late = (second2a, second2b, other2a, other2b)
    return early, late


EARLY_AT = (0, 16, 48, 64, 80, 112)
LATE_AT = (32, 40, 96, 104)


def source_table(need):
    me = lax.axis_index("dev")
    peer = jnp.arange(2 * SIDE * SIDE, dtype=jnp.int32)
    core = peer & 1
    dx = ((peer >> 3) - (me >> 3)) & 3
    dy = (((peer >> 1) & 3) - ((me >> 1) & 3)) & 3
    first = jnp.where(core == 0, dx, dy)
    second = jnp.where(core == 0, dy, dx)
    slot = ((core ^ (me & 1)) << 6) + (second << 4) + (first << 2)
    late = jnp.where(second == 2, 1 << 20, 0)
    return ((slot + late)[:, None] + need).reshape(-1)


def plan_kernel(table, src, operand, count, lists, groups, sizes, filled):
    for k in range(LISTS):
        filled[k] = k * ROOM

    def place(p, carry):
        word = table[src[p]]
        tail = operand[p]
        which = (tail & 3) | (word >> 18)
        at = filled[which]
        lists[at] = word + (tail & 0x7F00)
        filled[which] = at + 1
        return carry

    lax.fori_loop(0, count[0], place, 0)
    for u in range(JOIN):
        lists[LISTS * ROOM + u] = SOURCES
    for part in range(2):
        total = jnp.int32(0)
        for k in range(part * OWN, (part + 1) * OWN):
            end = filled[k]
            for u in range(JOIN):
                lists[end + u] = SOURCES
            several = (end - k * ROOM + (JOIN - 1)) // JOIN

            def enter(g, carry, k=k, part=part, total=total):
                groups[part * GROUPS + total + g] = (k * ROOM + g * JOIN) | ((k % OWN) << 16)
                return carry

            lax.fori_loop(0, several, enter, 0)
            total = total + several
        for w in range(WIDE):
            groups[part * GROUPS + total + w] = LISTS * ROOM
        sizes[part] = (total + (WIDE - 1)) // WIDE


def plan(table, src, operand, count):
    return pl.pallas_call(
        plan_kernel,
        out_shape=(
            jax.ShapeDtypeStruct(((LISTS + 1) * ROOM,), jnp.int32),
            jax.ShapeDtypeStruct((2 * GROUPS,), jnp.int32),
            jax.ShapeDtypeStruct((2,), jnp.int32),
        ),
        in_specs=[SMEM] * 4,
        out_specs=(SMEM,) * 3,
        scratch_shapes=[pltpu.SMEM((LISTS,), jnp.int32)],
        cost_estimate=pl.CostEstimate(flops=5_000_000_000, bytes_accessed=16384, transcendentals=0),
        name="plan",
    )(table, src, operand, count)


def add_pairs(part, lists, groups, sizes, blocks, sources, total):
    def step(i, carry):
        made = []
        for w in range(WIDE):
            group = groups[part * GROUPS + i * WIDE + w]
            base = group & 0xFFFF
            left, right = [], []
            for u in range(JOIN):
                word = lists[base + u]
                left.append(blocks[(word >> 8) & 0x7F])
                right.append(sources[word & 0xFF])
            product = jnp.dot(
                jnp.concatenate(left, axis=1),
                jnp.concatenate(right, axis=0),
                preferred_element_type=jnp.float32,
            )
            made.append((group >> 16, product))
        for target, product in made:
            total[target] += product
        return carry

    lax.fori_loop(0, sizes[part], step, 0)


def fetch(pieces, places, sources, sems):
    copies = []
    for n, (piece, place) in enumerate(zip(pieces, places)):
        copy = pltpu.make_async_copy(piece, sources.at[pl.ds(place, piece.shape[0])], sems.at[n])
        copy.start()
        copies.append(copy)
    sources[SOURCES] = jnp.zeros((TILE, TILE), jnp.bfloat16)
    for copy in copies:
        copy.wait()


def early_kernel(lists, groups, sizes, blocks, incident, *rest):
    pieces, (total, sources, sems) = rest[:-3], rest[-3:]
    fetch(pieces, EARLY_AT, sources, sems)
    total[...] = incident[...].astype(jnp.float32)
    add_pairs(0, lists, groups, sizes, blocks, sources, total)


def finish(tmatrix, total, t):
    field = total[t].astype(jnp.bfloat16)
    return jnp.dot(tmatrix[t], field, preferred_element_type=jnp.float32).astype(jnp.bfloat16)


def late_kernel(lists, groups, sizes, blocks, before, tmatrix, *rest):
    pieces, (coeff, sources, total, sems) = rest[:-4], rest[-4:]
    fetch(pieces, LATE_AT, sources, sems)
    total[...] = before[...]
    add_pairs(1, lists, groups, sizes, blocks, sources, total)
    for t in range(OWN):
        coeff[t] = finish(tmatrix, total, t)


FAR_ROWS = 256


def last_kernel(lists, groups, sizes, blocks, before, tmatrix, weighted, *rest):
    pieces, (far, sources, total, coeff, sems) = rest[:-5], rest[-5:]
    fetch(pieces, LATE_AT, sources, sems)
    total[...] = before[...]
    add_pairs(1, lists, groups, sizes, blocks, sources, total)
    for t in range(OWN):
        coeff[pl.ds(t * TILE, TILE), :] = finish(tmatrix, total, t)

    def chunk(i, carry):
        rows = pl.ds(pl.multiple_of(i * FAR_ROWS, FAR_ROWS), FAR_ROWS)
        far[rows, :] = jnp.dot(weighted[rows, :], coeff[...], preferred_element_type=jnp.float32)
        return carry

    lax.fori_loop(0, far.shape[0] // FAR_ROWS, chunk, 0)


SCRATCH = pltpu.VMEM((SOURCES + 1, TILE, TILE), jnp.bfloat16)
TOTAL = (OWN, TILE, TILE)


def early_pairs(made, blocks, incident, pieces):
    return pl.pallas_call(
        early_kernel,
        out_shape=jax.ShapeDtypeStruct(TOTAL, jnp.float32),
        in_specs=[SMEM] * 3 + [VMEM] * 2 + [ANY] * len(pieces),
        out_specs=VMEM,
        scratch_shapes=[SCRATCH, pltpu.SemaphoreType.DMA((len(pieces),))],
        cost_estimate=pl.CostEstimate(
            flops=2_000_000_000, bytes_accessed=8_000_000, transcendentals=0
        ),
        name="early",
    )(*made, blocks, incident, *pieces)


def late_pairs(made, blocks, before, tmatrix, pieces):
    return pl.pallas_call(
        late_kernel,
        out_shape=jax.ShapeDtypeStruct(TOTAL, jnp.bfloat16),
        in_specs=[SMEM] * 3 + [VMEM] * 3 + [ANY] * len(pieces),
        out_specs=VMEM,
        scratch_shapes=[
            SCRATCH,
            pltpu.VMEM(TOTAL, jnp.float32),
            pltpu.SemaphoreType.DMA((len(pieces),)),
        ],
        name="late",
    )(*made, blocks, before, tmatrix, *pieces)


def last_pairs(made, blocks, before, tmatrix, weighted, pieces):
    return pl.pallas_call(
        last_kernel,
        out_shape=jax.ShapeDtypeStruct((weighted.shape[0], TILE), jnp.float32),
        in_specs=[SMEM] * 3 + [VMEM] * 4 + [ANY] * len(pieces),
        out_specs=VMEM,
        scratch_shapes=[
            SCRATCH,
            pltpu.VMEM(TOTAL, jnp.float32),
            pltpu.VMEM((OWN * TILE, TILE), jnp.bfloat16),
            pltpu.SemaphoreType.DMA((len(pieces),)),
        ],
        name="last",
    )(*made, blocks, before, tmatrix, weighted, *pieces)


def apply_tmatrix(tmatrix, field):
    product = jnp.einsum("skl,slq->skq", tmatrix, field, preferred_element_type=jnp.float32)
    return product.astype(jnp.bfloat16)


def body(
    incident,
    tmatrix,
    blocks,
    need,
    pair_src,
    pair_tgt,
    pair_blk,
    pair_count,
    factor,
    harmonics,
    owner,
):
    n_grp, n_dev = lax.axis_size("grp"), lax.axis_size("dev")
    coeff = apply_tmatrix(tmatrix, incident)
    made = plan(source_table(need[0]), pair_src[0], pair_tgt[0] | (pair_blk[0] << 8), pair_count)
    early, late = spread(coeff)
    before = early_pairs(made, blocks, incident, early)
    coeff = late_pairs(made, blocks, before, tmatrix, late)

    rows = owner.shape[0] // (n_grp * n_dev)
    order = owner.reshape(n_grp, n_dev, rows).transpose(1, 0, 2).reshape(-1)
    table = jnp.take(harmonics, order, axis=0).astype(jnp.float32)
    phases = jnp.take(factor, order, axis=1)
    weighted = (phases.T[:, :, None] * table[:, None, :]).astype(jnp.bfloat16)
    weighted = weighted.reshape(owner.shape[0], -1)

    early, late = spread(coeff)
    before = early_pairs(made, blocks, incident, early)
    far = last_pairs(made, blocks, before, tmatrix, weighted, late)

    far = far.reshape(n_dev, n_grp * rows, TILE)
    far = lax.all_to_all(far, "dev", 0, 0).sum(axis=0)
    far = far.reshape(n_grp, rows, TILE)
    return lax.all_to_all(far, "grp", 0, 0).sum(axis=0)


def solution(mesh):
    both = ("grp", "dev")
    return jax.shard_map(
        body,
        mesh=mesh,
        in_specs=(
            P(both, None, None),
            P(both, None, None),
            P(both, None, None),
            P(both, None, None),
            P(both, None),
            P(both, None),
            P(both, None),
            P(both),
            P(both, None),
            P(),
            P(),
        ),
        out_specs=P(both, None),
        check_vma=False,
    )
```

time: 663 us -> 167 us (0.25)
  waiting for transfers between devices: 345 us -> 8.37 us
  matrix products: 153 us -> 1.2 us
  local copies, waits for them, and re-layouts: 113 us -> 25.8 us
  blocking collectives: 0 us -> 44.8 us
  starting transfers between devices: 0.27 us -> 42.1 us
  Pallas kernels: 0 us -> 31.3 us
  loops' own time: 16.8 us -> 0 us
  between operations: 13.3 us -> 1.08 us
  other arithmetic: 19.3 us -> 10.9 us
    unnamed x4 -> x0, waiting for transfers between devices: 257 us -> none
    dot_general x17 -> x0, matrix products: 151 us -> none  [the longest x8 84.1 us: advance(): jnp.einsum('sp,pkq->skq', selector, contrib, precision=lax.Precision.HIGH...]
    all_gather x2 -> x0, waiting for transfers between devices: 88.1 us -> none  [body(): sources = lax.all_gather(coeff, 'dev', axis=0, tiled=True)]
    gather x19 -> x2, local copies, waits for them, and re-layouts: 98.3 us -> 13.7 us  [the longest x1 7.56 us: body(): phases = jnp.take(factor, order, axis=1)]
    all_to_all x0 -> x2, blocking collectives: none -> 44.8 us  [the longest x1 25.3 us: body(): far = lax.all_to_all(far, 'dev', 0, 0).sum(axis=0)]
    ppermute x0 -> x26, starting transfers between devices: none -> 42.1 us  [send(): return lax.ppermute(values, 'dev', pairs)]
    pallas_call x0 -> x5, Pallas kernels: none -> 31.3 us  [the longest x2 13.9 us: early_pairs(): pl.pallas_call(early_kernel, out_shape=jax.ShapeDtypeStruct(TOTAL, jnp.fl...]
    another operation x2 -> x0, loops' own time: 16.8 us -> none  [scatter_pairs(): result, unused = lax.scan(advance, initial, start_rows)]
  transfers between devices with their start and end apart: 3 -> 26, of which waited for: 3 -> 4; matrix products, arithmetic and copies ran while one was open for 3% -> 19% of each run, Pallas kernels for 0% -> 11%
where the time goes in v1:
time: 167 us; the launch traced here: 166 us
  blocking collectives  44.8 us (27%)
  starting transfers between devices  42.1 us (25%)
  Pallas kernels  31.3 us (19%)
  local copies, waits for them, and re-layouts  25.8 us (15%)
  other arithmetic  10.9 us (7%)
  waiting for transfers between devices  8.37 us (5%)
    ppermute x26, starting transfers between devices, send(): return lax.ppermute(values, 'dev', pairs)  42.1 us
    all_to_all x1, blocking collectives, body(): far = lax.all_to_all(far, 'dev', 0, 0).sum(axis=0)  25.3 us
    all_to_all x1, blocking collectives, body(): return lax.all_to_all(far, 'grp', 0, 0).sum(axis=0)  19.6 us
    pallas_call x2, Pallas kernels, early_pairs(): pl.pallas_call(early_kernel, out_shape=jax.ShapeDtypeStruct(TOTAL, jnp.fl...  13.9 us
    unnamed x40, local copies, waits for them, and re-layouts  9.13 us
    ppermute x26, waiting for transfers between devices, send(): return lax.ppermute(values, 'dev', pairs)  8.37 us
    pallas_call x1, Pallas kernels, last_pairs(): pl.pallas_call(last_kernel, out_shape=jax.ShapeDtypeStruct((weighted.shap...  8 us
    convert_element_type x1, other arithmetic, body(): weighted = (phases.T[:, :, None] * table[:, None, :]).astype(jnp.bfloat16)  7.71 us
  transfers between devices with their start and end apart: 26, of which 4 were waited for; matrix products, arithmetic and copies ran while one was open for 19% of the time, Pallas kernels for 11%

profile of v1, /device:TPU:1, one launch (start us, length us, event | category | flops | bytes accessed | tf_op | source)
XLA Modules:
  0.0 165.6 jit_solution(8099411795126701828)
XLA Ops:
  0.0 1.2 constant_dynamic-update-slice_fusion.4
  1.2 2.2 %collective-permute-start.1 = (bf16[4,128,128]{2,1,0:T(8,128)(2,1)S(1)}, bf16[4,128,128]{2,1,0:T(8,128)(2,1)S(1)}, u32[]{:S(2)}, u32[]{:S(2)}) collective-permute-start(bf16[4,128,128]{2,1,0:T(8,128)(2,1)S(1)} %get-tuple-element.12), channel_id=1, source_target_pairs={{0,8},{1,3},{2,10},{3,5},{4,12},{5,7},{6,14},{7,1},{8,16},{9,11},{... | collective-permute-start | bytes 393224 | tf_op jit(solution)/shard_map/ppermute | solution.py:46
  3.4 1.5 collective-permute-start
  4.9 2.3 %collective-permute-done.1 = bf16[4,128,128]{2,1,0:T(8,128)(2,1)S(1)} collective-permute-done((bf16[4,128,128]{2,1,0:T(8,128)(2,1)S(1)}, bf16[4,128,128]{2,1,0:T(8,128)(2,1)S(1)}, u32[]{:S(2)}, u32[]{:S(2)}) %collective-permute-start.1) | collective-permute-done | bytes 131104 | tf_op jit(solution)/shard_map/ppermute | solution.py:46
  7.2 3.0 %collective-permute-start.3 = (bf16[2,128,128]{2,1,0:T(8,128)(2,1)S(1)}, bf16[2,128,128]{2,1,0:T(8,128)(2,1)S(1)}, u32[]{:S(2)}, u32[]{:S(2)}) collective-permute-start(bf16[2,128,128]{2,1,0:T(8,128)(2,1)S(1)} %slice.37), channel_id=1, source_target_pairs={{0,24},{1,7},{2,26},{3,1},{4,28},{5,3},{6,30},{7,5},{8,0},{9,15},{... | collective-permute-start | bytes 196616 | tf_op jit(solution)/shard_map/ppermute | solution.py:46
  10.3 1.2 collective-permute-done.2
  11.6 1.3 collective-permute-start.5
  12.9 1.5 collective-permute-start.4
  14.6 0.8 copy.18
  16.1 0.6 add.62.table
  16.7 1.3 shift-left_or_fusion
  18.0 5.3 %collective-permute-start.6 = (bf16[16,128,128]{2,1,0:T(8,128)(2,1)S(1)}, bf16[16,128,128]{2,1,0:T(8,128)(2,1)S(1)}, u32[]{:S(2)}, u32[]{:S(2)}) collective-permute-start(bf16[16,128,128]{2,1,0:T(8,128)(2,1)S(1)} %constant_dynamic-update-slice_fusion.rest_0_), channel_id=1, source_target_pairs={{0,1},{1,0},{2,3},{3,2},{4,5},{5,4},{6,7},{7,6},{8,9},{9,8},{10,11... | collective-permute-start | bytes 1572872 | tf_op jit(solution)/shard_map/ppermute | solution.py:46
  23.2 0.8 slice.38
  24.0 0.8 slice.39
  24.8 3.4 %collective-permute-start.10 = (bf16[8,128,128]{2,1,0:T(8,128)(2,1)}, bf16[8,128,128]{2,1,0:T(8,128)(2,1)}, u32[]{:S(2)}, u32[]{:S(2)}) collective-permute-start(bf16[8,128,128]{2,1,0:T(8,128)(2,1)} %slice.39), channel_id=1, source_target_pairs={{0,6},{1,25},{2,0},{3,27},{4,2},{5,29},{6,4},{7,31},{8,14},{9,1},{... | collective-permute-start | bytes 786440 | tf_op jit(solution)/shard_map/ppermute | solution.py:46
  28.2 3.4 %collective-permute-start.7 = (bf16[16,128,128]{2,1,0:T(8,128)(2,1)S(1)}, bf16[16,128,128]{2,1,0:T(8,128)(2,1)S(1)}, u32[]{:S(2)}, u32[]{:S(2)}) collective-permute-start(bf16[16,128,128]{2,1,0:T(8,128)(2,1)S(1)} %collective-permute-done.4.rest_1_), channel_id=1, source_target_pairs={{0,1},{1,0},{2,3},{3,2},{4,5},{5,4},{6,7},{7,6},{8,9},{9,8},{10,11... | collective-permute-start | bytes 1572872 | tf_op jit(solution)/shard_map/ppermute | solution.py:46
  31.6 4.2 %plan.1 = (s32[4680]{0:T(1024)}, s32[144]{0:T(256)}, s32[2]{0:T(128)}) custom-call(s32[128]{0:T(128)} %add.62.table, s32[512]{0:T(512)} %bitcast.19, s32[512]{0:T(512)} %bitcast.18, s32[1]{0:T(128)S(6)} %copy.33.count), custom_call_target="tpu_custom_call" | custom-call | flops 5000000000 | bytes 16384 | tf_op jit(solution)/shard_map/plan/pallas_call | solution.py:124
  36.1 1.2 collective-permute-start.11
  37.5 0.8 copy-done.7
  38.4 7.0 %early.2.before = f32[4,128,128]{2,1,0:T(8,128)} custom-call(s32[4680]{0:T(1024)} %get-tuple-element.8.lists, s32[144]{0:T(256)} %get-tuple-element.9.groups, s32[2]{0:T(128)} %get-tuple-element.10.sizes, bf16[128,128,128]{2,1,0:T(8,128)(2,1)} %blocks.7, bf16[4,128,128]{2,1,0:T(8,128)(2,1)} %incident.3, bf16[16,128,128]{2,1,0:T(8,128)(2,1)} %copy-done.6, ...), custom_call_target="tpu_custom_call" | custom-call | flops 2000000000 | bytes 8000000 | tf_op jit(solution)/shard_map/early/pallas_call | solution.py:219
  45.5 5.2 %late.1 = bf16[4,128,128]{2,1,0:T(8,128)(2,1)} custom-call(s32[4680]{0:T(1024)} %get-tuple-element.8.lists, s32[144]{0:T(256)} %get-tuple-element.9.groups, s32[2]{0:T(128)} %get-tuple-element.10.sizes, bf16[128,128,128]{2,1,0:T(8,128)(2,1)} %blocks.7, f32[4,128,128]{2,1,0:T(8,128)} %early.2.before, bf16[4,128,128]{2,1,0:T(8,128)(2,1)} %tmatrix.3, ...), custom_call_target="tpu_custom_call" | custom-call | tf_op jit(solution)/shard_map/late/pallas_call | solution.py:233
  50.7 3.2 %collective-permute-start.13 = (bf16[4,128,128]{2,1,0:T(8,128)(2,1)}, bf16[4,128,128]{2,1,0:T(8,128)(2,1)S(1)}, u32[]{:S(2)}, u32[]{:S(2)}) collective-permute-start(bf16[4,128,128]{2,1,0:T(8,128)(2,1)} %late.1), channel_id=1, source_target_pairs={{0,24},{1,7},{2,26},{3,1},{4,28},{5,3},{6,30},{7,5},{8,0},{9,15},{... | collective-permute-start | bytes 393224 | tf_op jit(solution)/shard_map/ppermute | solution.py:46
  54.0 1.6 constant_dynamic-update-slice_fusion.9
  55.5 3.9 %collective-permute-done.14 = bf16[4,128,128]{2,1,0:T(8,128)(2,1)S(1)} collective-permute-done((bf16[4,128,128]{2,1,0:T(8,128)(2,1)}, bf16[4,128,128]{2,1,0:T(8,128)(2,1)S(1)}, u32[]{:S(2)}, u32[]{:S(2)}) %collective-permute-start.14) | collective-permute-done | bytes 131104 | tf_op jit(solution)/shard_map/ppermute | solution.py:46
  59.4 2.7 %collective-permute-start.16 = (bf16[2,128,128]{2,1,0:T(8,128)(2,1)S(1)}, bf16[2,128,128]{2,1,0:T(8,128)(2,1)S(1)}, u32[]{:S(2)}, u32[]{:S(2)}) collective-permute-start(bf16[2,128,128]{2,1,0:T(8,128)(2,1)S(1)} %slice.41), channel_id=1, source_target_pairs={{0,24},{1,7},{2,26},{3,1},{4,28},{5,3},{6,30},{7,5},{8,0},{9,15},{... | collective-permute-start | bytes 196616 | tf_op jit(solution)/shard_map/ppermute | solution.py:46
  62.2 0.7 constant_dynamic-update-slice_fusion.8
  62.8 0.9 collective-permute-done.15
  63.7 0.6 constant_dynamic-update-slice_fusion.7
  64.4 0.6 constant_dynamic-update-slice_fusion.6
  65.0 0.7 constant_dynamic-update-slice_fusion.5.rest_0_
  65.7 3.1 %collective-permute-start.17 = (bf16[16,128,128]{2,1,0:T(8,128)(2,1)}, bf16[16,128,128]{2,1,0:T(8,128)(2,1)S(1)}, u32[]{:S(2)}, u32[]{:S(2)}) collective-permute-start(bf16[16,128,128]{2,1,0:T(8,128)(2,1)} %constant_dynamic-update-slice_fusion.5.rest_0_), channel_id=1, source_target_pairs={{0,6},{1,25},{2,0},{3,27},{4,2},{5,29},{6,4},{7,31},{8,14},{9,1},{... | collective-permute-start | bytes 1572872 | tf_op jit(solution)/shard_map/ppermute | solution.py:46
  68.8 0.4 copy.21
  69.1 7.6 %gather_fusion = f32[2048,4]{1,0:T(8,128)} fusion(f32[4,2048]{0,1:T(8,128)S(1)} %copy.21, s32[2048]{0:T(1024)S(1)} %broadcast_clamp_fusion), kind=kCustom, calls=%fused_computation | custom fusion | bytes 73728 | tf_op jit(solution)/shard_map/jit(_take)/gather | solution.py:291
  76.7 6.2 %gather_fusion.1 = bf16[2048,128]{1,0:T(8,128)(2,1)S(1)} fusion(bf16[2048,128]{1,0:T(8,128)(2,1)S(1)} %copy-done, s32[2048]{0:T(1024)S(1)} %broadcast_clamp_fusion), kind=kCustom, calls=%fused_computation.1 | custom fusion | bytes 1056768 | tf_op jit(solution)/shard_map/jit(_take)/gather | solution.py:290
  83.4 2.7 %collective-permute-start.23 = (bf16[8,128,128]{2,1,0:T(8,128)(2,1)S(1)}, bf16[8,128,128]{2,1,0:T(8,128)(2,1)}, u32[]{:S(2)}, u32[]{:S(2)}) collective-permute-start(bf16[8,128,128]{2,1,0:T(8,128)(2,1)S(1)} %slice.43), channel_id=1, source_target_pairs={{0,6},{1,25},{2,0},{3,27},{4,2},{5,29},{6,4},{7,31},{8,14},{9,1},{... | collective-permute-start | bytes 786440 | tf_op jit(solution)/shard_map/ppermute | solution.py:46
  86.2 0.3 select_convert_fusion
  86.5 3.5 %collective-permute-start.19 = (bf16[16,128,128]{2,1,0:T(8,128)(2,1)}, bf16[16,128,128]{2,1,0:T(8,128)(2,1)S(1)}, u32[]{:S(2)}, u32[]{:S(2)}) collective-permute-start(bf16[16,128,128]{2,1,0:T(8,128)(2,1)} %constant_dynamic-update-slice_fusion.5.rest_0_), channel_id=1, source_target_pairs={{0,1},{1,0},{2,3},{3,2},{4,5},{5,4},{6,7},{7,6},{8,9},{9,8},{10,11... | collective-permute-start | bytes 1572872 | tf_op jit(solution)/shard_map/ppermute | solution.py:46
  90.1 0.4 collective-permute-start.21
  90.5 3.3 %collective-permute-start.24 = (bf16[8,128,128]{2,1,0:T(8,128)(2,1)S(1)}, bf16[8,128,128]{2,1,0:T(8,128)(2,1)}, u32[]{:S(2)}, u32[]{:S(2)}) collective-permute-start(bf16[8,128,128]{2,1,0:T(8,128)(2,1)S(1)} %collective-permute-done.22.rest_0_), channel_id=1, source_target_pairs={{0,1},{1,0},{2,3},{3,2},{4,5},{5,4},{6,7},{7,6},{8,9},{9,8},{10,11... | collective-permute-start | bytes 786440 | tf_op jit(solution)/shard_map/ppermute | solution.py:46
  93.9 7.7 %multiply_convert_fusion = bf16[2048,4,128]{2,1,0:T(4,128)(2,1)S(1)} fusion(f32[2048,128]{1,0:T(8,128)S(1)} %select_convert_fusion, f32[2048,4]{1,0:T(8,128)S(1)} %broadcast_select_fusion), kind=kLoop, calls=%fused_computation.2 | loop fusion | flops 2097152 | bytes 3178496 | tf_op jit(solution)/shard_map/convert_element_type | solution.py:292
  101.6 1.7 %copy.24 = bf16[256,8,4,128]{3,1,2,0:T(8,128)(2,1)} copy(bf16[256,8,4,128]{3,2,1,0:T(4,128)(2,1)S(1)} %bitcast.12) | data formatting | bytes 4194304
  103.4 0.8 copy-done.9
  104.3 0.8 copy-done.11
  105.2 7.0 %early.3.before = f32[4,128,128]{2,1,0:T(8,128)} custom-call(s32[4680]{0:T(1024)} %get-tuple-element.8.lists, s32[144]{0:T(256)} %get-tuple-element.9.groups, s32[2]{0:T(128)} %get-tuple-element.10.sizes, bf16[128,128,128]{2,1,0:T(8,128)(2,1)} %blocks.7, bf16[4,128,128]{2,1,0:T(8,128)(2,1)} %incident.3, ...), custom_call_target="tpu_custom_call" | custom-call | flops 2000000000 | bytes 8000000 | tf_op jit(solution)/shard_map/early/pallas_call | solution.py:219
  112.1 8.0 %last.1 = f32[2048,128]{1,0:T(8,128)} custom-call(s32[4680]{0:T(1024)} %get-tuple-element.8.lists, s32[144]{0:T(256)} %get-tuple-element.9.groups, s32[2]{0:T(128)} %get-tuple-element.10.sizes, bf16[128,128,128]{2,1,0:T(8,128)(2,1)} %blocks.7, f32[4,128,128]{2,1,0:T(8,128)} %early.3.before, bf16[4,128,128]{2,1,0:T(8,128)(2,1)} %tmatrix.3, ...), custom_call_target="tpu_custom_call" | custom-call | tf_op jit(solution)/shard_map/last/pallas_call | solution.py:248
  120.2 25.3 %all_to_all.10 = f32[32,64,128]{2,1,0:T(8,128)S(1)} all-to-all(f32[32,64,128]{2,1,0:T(8,128)} %bitcast.14), channel_id=1, replica_groups=mesh['grp'=8,'dev'=32] {'dev'}, dimensions={0} | all-to-all | bytes 2097152 | tf_op jit(solution)/shard_map/all_to_all | solution.py:300
  145.5 19.6 %all_to_all.11 = f32[8,8,128]{2,1,0:T(8,128)S(1)} all-to-all(f32[8,8,128]{2,1,0:T(8,128)S(1)} %bitcast.16), channel_id=1, replica_groups=mesh['grp'=8,'dev'=32] {'grp'}, dimensions={0} | all-to-all | bytes 65536 | tf_op jit(solution)/shard_map/all_to_all | solution.py:302
  165.0 0.6 reduce_sum.19
  (82 shorter events, 2.2 us)
Async XLA Ops:
  0.0 76.7 %copy-start = (bf16[2048,128]{1,0:T(8,128)(2,1)S(1)}, bf16[2048,128]{1,0:T(8,128)(2,1)}, u32[]{:S(2)}) copy-start(bf16[2048,128]{1,0:T(8,128)(2,1)} %param.20) | copy-start | bytes 1572868
  1.2 6.0 %collective-permute-start.1 = (bf16[4,128,128]{2,1,0:T(8,128)(2,1)S(1)}, bf16[4,128,128]{2,1,0:T(8,128)(2,1)S(1)}, u32[]{:S(2)}, u32[]{:S(2)}) collective-permute-start(bf16[4,128,128]{2,1,0:T(8,128)(2,1)S(1)} %get-tuple-element.12), channel_id=1, source_target_pairs={{0,8},{1,3},{2,10},{3,5},{4,12},{5,7},{6,14},{7,1},{8,16},{9,11},{... | collective-permute-start | bytes 393224 | tf_op jit(solution)/shard_map/ppermute | solution.py:46
  3.4 3.8 %collective-permute-start = (bf16[4,128,128]{2,1,0:T(8,128)(2,1)S(1)}, bf16[4,128,128]{2,1,0:T(8,128)(2,1)S(1)}, u32[]{:S(2)}, u32[]{:S(2)}) collective-permute-start(bf16[4,128,128]{2,1,0:T(8,128)(2,1)S(1)} %get-tuple-element.12), channel_id=1, source_target_pairs={{0,24},{1,7},{2,26},{3,1},{4,28},{5,3},{6,30},{7,5},{8,0},{9,15},{... | collective-permute-start | bytes 393224 | tf_op jit(solution)/shard_map/ppermute | solution.py:46
  7.2 4.3 %collective-permute-start.2 = (bf16[2,128,128]{2,1,0:T(8,128)(2,1)S(1)}, bf16[2,128,128]{2,1,0:T(8,128)(2,1)S(1)}, u32[]{:S(2)}, u32[]{:S(2)}) collective-permute-start(bf16[2,128,128]{2,1,0:T(8,128)(2,1)S(1)} %slice.36), channel_id=1, source_target_pairs={{0,8},{1,3},{2,10},{3,5},{4,12},{5,7},{6,14},{7,1},{8,16},{9,11},{... | collective-permute-start | bytes 196616 | tf_op jit(solution)/shard_map/ppermute | solution.py:46
  7.2 4.4 %collective-permute-start.3 = (bf16[2,128,128]{2,1,0:T(8,128)(2,1)S(1)}, bf16[2,128,128]{2,1,0:T(8,128)(2,1)S(1)}, u32[]{:S(2)}, u32[]{:S(2)}) collective-permute-start(bf16[2,128,128]{2,1,0:T(8,128)(2,1)S(1)} %slice.37), channel_id=1, source_target_pairs={{0,24},{1,7},{2,26},{3,1},{4,28},{5,3},{6,30},{7,5},{8,0},{9,15},{... | collective-permute-start | bytes 196616 | tf_op jit(solution)/shard_map/ppermute | solution.py:46
  11.6 24.1 %copy-start.6 = (bf16[16,128,128]{2,1,0:T(8,128)(2,1)}, bf16[16,128,128]{2,1,0:T(8,128)(2,1)S(1)}, u32[]{:S(2)}) copy-start(bf16[16,128,128]{2,1,0:T(8,128)(2,1)S(1)} %constant_dynamic-update-slice_fusion.rest_0_) | copy-start | bytes 1572868
  11.6 11.6 %collective-permute-start.5 = (bf16[16,128,128]{2,1,0:T(8,128)(2,1)S(1)}, bf16[16,128,128]{2,1,0:T(8,128)(2,1)S(1)}, u32[]{:S(2)}, u32[]{:S(2)}) collective-permute-start(bf16[16,128,128]{2,1,0:T(8,128)(2,1)S(1)} %constant_dynamic-update-slice_fusion.rest_0_), channel_id=1, source_target_pairs={{0,2},{1,9},{2,4},{3,11},{4,6},{5,13},{6,0},{7,15},{8,10},{9,17},{... | collective-permute-start | bytes 1572872 | tf_op jit(solution)/shard_map/ppermute | solution.py:46
  12.9 11.1 %collective-permute-start.4 = (bf16[16,128,128]{2,1,0:T(8,128)(2,1)S(1)}, bf16[16,128,128]{2,1,0:T(8,128)(2,1)S(1)}, u32[]{:S(2)}, u32[]{:S(2)}) collective-permute-start(bf16[16,128,128]{2,1,0:T(8,128)(2,1)S(1)} %constant_dynamic-update-slice_fusion.rest_0_), channel_id=1, source_target_pairs={{0,6},{1,25},{2,0},{3,27},{4,2},{5,29},{6,4},{7,31},{8,14},{9,1},{... | collective-permute-start | bytes 1572872 | tf_op jit(solution)/shard_map/ppermute | solution.py:46
  18.0 19.5 %collective-permute-start.6 = (bf16[16,128,128]{2,1,0:T(8,128)(2,1)S(1)}, bf16[16,128,128]{2,1,0:T(8,128)(2,1)S(1)}, u32[]{:S(2)}, u32[]{:S(2)}) collective-permute-start(bf16[16,128,128]{2,1,0:T(8,128)(2,1)S(1)} %constant_dynamic-update-slice_fusion.rest_0_), channel_id=1, source_target_pairs={{0,1},{1,0},{2,3},{3,2},{4,5},{5,4},{6,7},{7,6},{8,9},{9,8},{10,11... | collective-permute-start | bytes 1572872 | tf_op jit(solution)/shard_map/ppermute | solution.py:46
  23.2 12.5 %copy-start.1 = (bf16[16,128,128]{2,1,0:T(8,128)(2,1)}, bf16[16,128,128]{2,1,0:T(8,128)(2,1)S(1)}, u32[]{:S(2)}) copy-start(bf16[16,128,128]{2,1,0:T(8,128)(2,1)S(1)} %collective-permute-done.5.rest_2_) | copy-start | bytes 1572868
  24.0 12.1 %collective-permute-start.9 = (bf16[8,128,128]{2,1,0:T(8,128)(2,1)}, bf16[8,128,128]{2,1,0:T(8,128)(2,1)}, u32[]{:S(2)}, u32[]{:S(2)}) collective-permute-start(bf16[8,128,128]{2,1,0:T(8,128)(2,1)} %slice.38), channel_id=1, source_target_pairs={{0,2},{1,9},{2,4},{3,11},{4,6},{5,13},{6,0},{7,15},{8,10},{9,17},{... | collective-permute-start | bytes 786440 | tf_op jit(solution)/shard_map/ppermute | solution.py:46
  24.0 11.8 %copy-start.2 = (bf16[16,128,128]{2,1,0:T(8,128)(2,1)}, bf16[16,128,128]{2,1,0:T(8,128)(2,1)S(1)}, u32[]{:S(2)}) copy-start(bf16[16,128,128]{2,1,0:T(8,128)(2,1)S(1)} %collective-permute-done.4.rest_1_) | copy-start | bytes 1572868
  24.8 12.5 %collective-permute-start.10 = (bf16[8,128,128]{2,1,0:T(8,128)(2,1)}, bf16[8,128,128]{2,1,0:T(8,128)(2,1)}, u32[]{:S(2)}, u32[]{:S(2)}) collective-permute-start(bf16[8,128,128]{2,1,0:T(8,128)(2,1)} %slice.39), channel_id=1, source_target_pairs={{0,6},{1,25},{2,0},{3,27},{4,2},{5,29},{6,4},{7,31},{8,14},{9,1},{... | collective-permute-start | bytes 786440 | tf_op jit(solution)/shard_map/ppermute | solution.py:46
  28.2 9.3 %collective-permute-start.7 = (bf16[16,128,128]{2,1,0:T(8,128)(2,1)S(1)}, bf16[16,128,128]{2,1,0:T(8,128)(2,1)S(1)}, u32[]{:S(2)}, u32[]{:S(2)}) collective-permute-start(bf16[16,128,128]{2,1,0:T(8,128)(2,1)S(1)} %collective-permute-done.4.rest_1_), channel_id=1, source_target_pairs={{0,1},{1,0},{2,3},{3,2},{4,5},{5,4},{6,7},{7,6},{8,9},{9,8},{10,11... | collective-permute-start | bytes 1572872 | tf_op jit(solution)/shard_map/ppermute | solution.py:46
  31.6 5.9 %collective-permute-start.8 = (bf16[16,128,128]{2,1,0:T(8,128)(2,1)S(1)}, bf16[16,128,128]{2,1,0:T(8,128)(2,1)}, u32[]{:S(2)}, u32[]{:S(2)}) collective-permute-start(bf16[16,128,128]{2,1,0:T(8,128)(2,1)S(1)} %collective-permute-done.5.rest_2_), channel_id=1, source_target_pairs={{0,1},{1,0},{2,3},{3,2},{4,5},{5,4},{6,7},{7,6},{8,9},{9,8},{10,11... | collective-permute-start | bytes 1572872 | tf_op jit(solution)/shard_map/ppermute | solution.py:46
  31.6 4.2 %copy-start.14 = (s32[2048]{0:T(1024)S(1)}, s32[2048]{0:T(1024)}, u32[]{:S(2)}) copy-start(s32[2048]{0:T(1024)} %param.21) | copy-start | bytes 24580
  36.1 9.3 %collective-permute-start.11 = (bf16[8,128,128]{2,1,0:T(8,128)(2,1)}, bf16[8,128,128]{2,1,0:T(8,128)(2,1)}, u32[]{:S(2)}, u32[]{:S(2)}) collective-permute-start(bf16[8,128,128]{2,1,0:T(8,128)(2,1)} %collective-permute-done.9.rest_0_), channel_id=1, source_target_pairs={{0,1},{1,0},{2,3},{3,2},{4,5},{5,4},{6,7},{7,6},{8,9},{9,8},{10,11... | collective-permute-start | bytes 786440 | tf_op jit(solution)/shard_map/ppermute | solution.py:46
  37.3 8.1 %collective-permute-start.12 = (bf16[8,128,128]{2,1,0:T(8,128)(2,1)}, bf16[8,128,128]{2,1,0:T(8,128)(2,1)}, u32[]{:S(2)}, u32[]{:S(2)}) collective-permute-start(bf16[8,128,128]{2,1,0:T(8,128)(2,1)} %collective-permute-done.10.rest_1_), channel_id=1, source_target_pairs={{0,1},{1,0},{2,3},{3,2},{4,5},{5,4},{6,7},{7,6},{8,9},{9,8},{10,11... | collective-permute-start | bytes 786440 | tf_op jit(solution)/shard_map/ppermute | solution.py:46
  37.5 0.8 copy-start.7
  37.5 1.0 copy-start.8
  45.4 23.3 %copy-start.13 = (f32[4,2048]{1,0:T(4,128)S(1)}, f32[4,2048]{1,0:T(4,128)}, u32[]{:S(2)}) copy-start(f32[4,2048]{1,0:T(4,128)} %param.19) | copy-start | bytes 98308
  50.7 8.7 %collective-permute-start.13 = (bf16[4,128,128]{2,1,0:T(8,128)(2,1)}, bf16[4,128,128]{2,1,0:T(8,128)(2,1)S(1)}, u32[]{:S(2)}, u32[]{:S(2)}) collective-permute-start(bf16[4,128,128]{2,1,0:T(8,128)(2,1)} %late.1), channel_id=1, source_target_pairs={{0,24},{1,7},{2,26},{3,1},{4,28},{5,3},{6,30},{7,5},{8,0},{9,15},{... | collective-permute-start | bytes 393224 | tf_op jit(solution)/shard_map/ppermute | solution.py:46
  53.9 5.5 %collective-permute-start.14 = (bf16[4,128,128]{2,1,0:T(8,128)(2,1)}, bf16[4,128,128]{2,1,0:T(8,128)(2,1)S(1)}, u32[]{:S(2)}, u32[]{:S(2)}) collective-permute-start(bf16[4,128,128]{2,1,0:T(8,128)(2,1)} %late.1), channel_id=1, source_target_pairs={{0,8},{1,3},{2,10},{3,5},{4,12},{5,7},{6,14},{7,1},{8,16},{9,11},{... | collective-permute-start | bytes 393224 | tf_op jit(solution)/shard_map/ppermute | solution.py:46
  59.4 4.3 %collective-permute-start.15 = (bf16[2,128,128]{2,1,0:T(8,128)(2,1)S(1)}, bf16[2,128,128]{2,1,0:T(8,128)(2,1)S(1)}, u32[]{:S(2)}, u32[]{:S(2)}) collective-permute-start(bf16[2,128,128]{2,1,0:T(8,128)(2,1)S(1)} %slice.40), channel_id=1, source_target_pairs={{0,8},{1,3},{2,10},{3,5},{4,12},{5,7},{6,14},{7,1},{8,16},{9,11},{... | collective-permute-start | bytes 196616 | tf_op jit(solution)/shard_map/ppermute | solution.py:46
  59.4 4.9 %collective-permute-start.16 = (bf16[2,128,128]{2,1,0:T(8,128)(2,1)S(1)}, bf16[2,128,128]{2,1,0:T(8,128)(2,1)S(1)}, u32[]{:S(2)}, u32[]{:S(2)}) collective-permute-start(bf16[2,128,128]{2,1,0:T(8,128)(2,1)S(1)} %slice.41), channel_id=1, source_target_pairs={{0,24},{1,7},{2,26},{3,1},{4,28},{5,3},{6,30},{7,5},{8,0},{9,15},{... | collective-permute-start | bytes 196616 | tf_op jit(solution)/shard_map/ppermute | solution.py:46
  65.7 17.7 %collective-permute-start.17 = (bf16[16,128,128]{2,1,0:T(8,128)(2,1)}, bf16[16,128,128]{2,1,0:T(8,128)(2,1)S(1)}, u32[]{:S(2)}, u32[]{:S(2)}) collective-permute-start(bf16[16,128,128]{2,1,0:T(8,128)(2,1)} %constant_dynamic-update-slice_fusion.5.rest_0_), channel_id=1, source_target_pairs={{0,6},{1,25},{2,0},{3,27},{4,2},{5,29},{6,4},{7,31},{8,14},{9,1},{... | collective-permute-start | bytes 1572872 | tf_op jit(solution)/shard_map/ppermute | solution.py:46
  68.7 14.5 %collective-permute-start.18 = (bf16[16,128,128]{2,1,0:T(8,128)(2,1)}, bf16[16,128,128]{2,1,0:T(8,128)(2,1)S(1)}, u32[]{:S(2)}, u32[]{:S(2)}) collective-permute-start(bf16[16,128,128]{2,1,0:T(8,128)(2,1)} %constant_dynamic-update-slice_fusion.5.rest_0_), channel_id=1, source_target_pairs={{0,2},{1,9},{2,4},{3,11},{4,6},{5,13},{6,0},{7,15},{8,10},{9,17},{... | collective-permute-start | bytes 1572872 | tf_op jit(solution)/shard_map/ppermute | solution.py:46
  76.7 6.2 %copy-start.5 = (f32[2048,4]{1,0:T(8,128)S(1)}, f32[2048,4]{1,0:T(8,128)}, u32[]{:S(2)}) copy-start(f32[2048,4]{1,0:T(8,128)} %gather_fusion) | copy-start | bytes 98308
  83.2 20.1 %copy-start.4 = (bf16[16,128,128]{2,1,0:T(8,128)(2,1)}, bf16[16,128,128]{2,1,0:T(8,128)(2,1)S(1)}, u32[]{:S(2)}) copy-start(bf16[16,128,128]{2,1,0:T(8,128)(2,1)S(1)} %collective-permute-done.18.rest_2_) | copy-start | bytes 1572868
  83.3 7.3 %collective-permute-start.22 = (bf16[8,128,128]{2,1,0:T(8,128)(2,1)S(1)}, bf16[8,128,128]{2,1,0:T(8,128)(2,1)S(1)}, u32[]{:S(2)}, u32[]{:S(2)}) collective-permute-start(bf16[8,128,128]{2,1,0:T(8,128)(2,1)S(1)} %slice.42), channel_id=1, source_target_pairs={{0,2},{1,9},{2,4},{3,11},{4,6},{5,13},{6,0},{7,15},{8,10},{9,17},{... | collective-permute-start | bytes 786440 | tf_op jit(solution)/shard_map/ppermute | solution.py:46
  83.4 20.0 %copy-start.3 = (bf16[16,128,128]{2,1,0:T(8,128)(2,1)}, bf16[16,128,128]{2,1,0:T(8,128)(2,1)S(1)}, u32[]{:S(2)}) copy-start(bf16[16,128,128]{2,1,0:T(8,128)(2,1)S(1)} %collective-permute-done.17.rest_1_) | copy-start | bytes 1572868
  83.4 10.4 %collective-permute-start.23 = (bf16[8,128,128]{2,1,0:T(8,128)(2,1)S(1)}, bf16[8,128,128]{2,1,0:T(8,128)(2,1)}, u32[]{:S(2)}, u32[]{:S(2)}) collective-permute-start(bf16[8,128,128]{2,1,0:T(8,128)(2,1)S(1)} %slice.43), channel_id=1, source_target_pairs={{0,6},{1,25},{2,0},{3,27},{4,2},{5,29},{6,4},{7,31},{8,14},{9,1},{... | collective-permute-start | bytes 786440 | tf_op jit(solution)/shard_map/ppermute | solution.py:46
  86.5 16.8 %collective-permute-start.19 = (bf16[16,128,128]{2,1,0:T(8,128)(2,1)}, bf16[16,128,128]{2,1,0:T(8,128)(2,1)S(1)}, u32[]{:S(2)}, u32[]{:S(2)}) collective-permute-start(bf16[16,128,128]{2,1,0:T(8,128)(2,1)} %constant_dynamic-update-slice_fusion.5.rest_0_), channel_id=1, source_target_pairs={{0,1},{1,0},{2,3},{3,2},{4,5},{5,4},{6,7},{7,6},{8,9},{9,8},{10,11... | collective-permute-start | bytes 1572872 | tf_op jit(solution)/shard_map/ppermute | solution.py:46
  90.0 13.3 %collective-permute-start.20 = (bf16[16,128,128]{2,1,0:T(8,128)(2,1)S(1)}, bf16[16,128,128]{2,1,0:T(8,128)(2,1)S(1)}, u32[]{:S(2)}, u32[]{:S(2)}) collective-permute-start(bf16[16,128,128]{2,1,0:T(8,128)(2,1)S(1)} %collective-permute-done.17.rest_1_), channel_id=1, source_target_pairs={{0,1},{1,0},{2,3},{3,2},{4,5},{5,4},{6,7},{7,6},{8,9},{9,8},{10,11... | collective-permute-start | bytes 1572872 | tf_op jit(solution)/shard_map/ppermute | solution.py:46
  90.1 13.3 %collective-permute-start.21 = (bf16[16,128,128]{2,1,0:T(8,128)(2,1)S(1)}, bf16[16,128,128]{2,1,0:T(8,128)(2,1)S(1)}, u32[]{:S(2)}, u32[]{:S(2)}) collective-permute-start(bf16[16,128,128]{2,1,0:T(8,128)(2,1)S(1)} %collective-permute-done.18.rest_2_), channel_id=1, source_target_pairs={{0,1},{1,0},{2,3},{3,2},{4,5},{5,4},{6,7},{7,6},{8,9},{9,8},{10,11... | collective-permute-start | bytes 1572872 | tf_op jit(solution)/shard_map/ppermute | solution.py:46
  90.5 12.8 %copy-start.12 = (bf16[8,128,128]{2,1,0:T(8,128)(2,1)}, bf16[8,128,128]{2,1,0:T(8,128)(2,1)S(1)}, u32[]{:S(2)}) copy-start(bf16[8,128,128]{2,1,0:T(8,128)(2,1)S(1)} %collective-permute-done.22.rest_0_) | copy-start | bytes 786436
  90.5 21.6 %collective-permute-start.24 = (bf16[8,128,128]{2,1,0:T(8,128)(2,1)S(1)}, bf16[8,128,128]{2,1,0:T(8,128)(2,1)}, u32[]{:S(2)}, u32[]{:S(2)}) collective-permute-start(bf16[8,128,128]{2,1,0:T(8,128)(2,1)S(1)} %collective-permute-done.22.rest_0_), channel_id=1, source_target_pairs={{0,1},{1,0},{2,3},{3,2},{4,5},{5,4},{6,7},{7,6},{8,9},{9,8},{10,11... | collective-permute-start | bytes 786440 | tf_op jit(solution)/shard_map/ppermute | solution.py:46
  93.8 18.3 %collective-permute-start.25 = (bf16[8,128,128]{2,1,0:T(8,128)(2,1)}, bf16[8,128,128]{2,1,0:T(8,128)(2,1)}, u32[]{:S(2)}, u32[]{:S(2)}) collective-permute-start(bf16[8,128,128]{2,1,0:T(8,128)(2,1)} %collective-permute-done.23.rest_1_), channel_id=1, source_target_pairs={{0,1},{1,0},{2,3},{3,2},{4,5},{5,4},{6,7},{7,6},{8,9},{9,8},{10,11... | collective-permute-start | bytes 786440 | tf_op jit(solution)/shard_map/ppermute | solution.py:46
  103.4 0.8 copy-start.9
  103.4 1.0 copy-start.10
  104.3 0.8 copy-start.11

commit v2 on v1

--- a/solution.py
+++ b/solution.py
@@ -17,6 +17,7 @@
 LISTS = 2 * OWN
 GROUPS = PAIRS // JOIN + OWN + WIDE
 
+LIMIT = pltpu.CompilerParams(vmem_limit_bytes=16 << 20)
 SMEM = pl.BlockSpec(memory_space=pltpu.SMEM)
 VMEM = pl.BlockSpec(memory_space=pltpu.VMEM)
 ANY = pl.BlockSpec(memory_space=pl.ANY)
@@ -46,30 +47,40 @@
     return lax.ppermute(values, "dev", pairs)
 
 
-def spread(coeff):
+def together(values, *fillers):
+    return lax.optimization_barrier((values, fillers))[0]
+
+
+def spread(coeff, fill_first, fill_second):
     half = OWN // 2
     first3 = send(coeff, along_first(1))
     first1 = send(coeff, along_first(-1))
+    first3, first1 = together((first3, first1), fill_first)
     first2a = send(first3[:half], along_first(1))
     first2b = send(first1[half:], along_first(-1))
-    row = jnp.concatenate([coeff, first1, first2a, first2b, first3])
-    half = SIDE * OWN // 2
-    second3 = send(row, along_second(1))
-    second1 = send(row, along_second(-1))
-    other0 = send(row, SWAP)
-    second2a = send(second3[:half], along_second(1))
-    second2b = send(second1[half:], along_second(-1))
-    other3 = send(second3, SWAP)
-    other1 = send(second1, SWAP)
-    other2a = send(second2a, SWAP)
-    other2b = send(second2b, SWAP)
-    early = (row, second1, second3, other0, other1, other3)
-    late = (second2a, second2b, other2a, other2b)
-    return early, late
-
-
-EARLY_AT = (0, 16, 48, 64, 80, 112)
-LATE_AT = (32, 40, 96, 104)
+    first2a, first2b = together((first2a, first2b), fill_second)
+    low = jnp.concatenate([coeff, first1])
+    high = jnp.concatenate([first2a, first2b, first3])
+    low3 = send(low, along_second(1))
+    high1 = send(high, along_second(-1))
+    high3 = send(high, along_second(1))
+    low1 = send(low, along_second(-1))
+    low2 = send(low3, along_second(1))
+    high2 = send(high1, along_second(-1))
+    near = (low, high, low1, high1, low3, high3)
+    far = (low2, high2)
+    return near, tuple(send(piece, SWAP) for piece in near), far
+
+
+def swapped(pieces, before):
+    pieces = together(pieces, before)
+    return pieces + tuple(send(piece, SWAP) for piece in pieces)
+
+
+NEAR_AT = (0, 8, 16, 24, 48, 56)
+FAR_AT = (32, 40)
+EARLY_AT = NEAR_AT + tuple(place + SOURCES // 2 for place in NEAR_AT)
+LATE_AT = FAR_AT + tuple(place + SOURCES // 2 for place in FAR_AT)
 
 
 def source_table(need):
@@ -132,6 +143,7 @@
         out_specs=(SMEM,) * 3,
         scratch_shapes=[pltpu.SMEM((LISTS,), jnp.int32)],
         cost_estimate=pl.CostEstimate(flops=5_000_000_000, bytes_accessed=16384, transcendentals=0),
+        compiler_params=LIMIT,
         name="plan",
     )(table, src, operand, count)
 
@@ -195,7 +207,7 @@
 FAR_ROWS = 256
 
 
-def last_kernel(lists, groups, sizes, blocks, before, tmatrix, weighted, *rest):
+def last_kernel(lists, groups, sizes, blocks, before, tmatrix, weighted_a, weighted_b, *rest):
     pieces, (far, sources, total, coeff, sems) = rest[:-5], rest[-5:]
     fetch(pieces, LATE_AT, sources, sems)
     total[...] = before[...]
@@ -203,12 +215,73 @@
     for t in range(OWN):
         coeff[pl.ds(t * TILE, TILE), :] = finish(tmatrix, total, t)
 
+    for n, weighted in enumerate((weighted_a, weighted_b)):
+        size = weighted.shape[0]
+
+        def chunk(i, carry, weighted=weighted, first=n * size):
+            start = pl.multiple_of(i * FAR_ROWS, FAR_ROWS)
+            far[pl.ds(first + start, FAR_ROWS), :] = jnp.dot(
+                weighted[pl.ds(start, FAR_ROWS), :],
+                coeff[...],
+                preferred_element_type=jnp.float32,
+            )
+            return carry
+
+        lax.fori_loop(0, size // FAR_ROWS, chunk, 0)
+
+
+def table_kernel(phases, harmonics, table):
     def chunk(i, carry):
         rows = pl.ds(pl.multiple_of(i * FAR_ROWS, FAR_ROWS), FAR_ROWS)
-        far[rows, :] = jnp.dot(weighted[rows, :], coeff[...], preferred_element_type=jnp.float32)
+        modes = harmonics[rows, :].astype(jnp.float32)
+        for s in range(OWN):
+            phase = jnp.broadcast_to(phases[rows, s : s + 1], modes.shape)
+            table[rows, s * TILE : (s + 1) * TILE] = (phase * modes).astype(jnp.bfloat16)
         return carry
 
-    lax.fori_loop(0, far.shape[0] // FAR_ROWS, chunk, 0)
+    lax.fori_loop(0, table.shape[0] // FAR_ROWS, chunk, 0)
+
+
+def order_kernel(order, table, ordered):
+    def chunk(i, carry):
+        rows = pl.ds(pl.multiple_of(i * FAR_ROWS, FAR_ROWS), FAR_ROWS)
+        wanted = jnp.broadcast_to(order[rows, :], (FAR_ROWS, table.shape[0]))
+        place = lax.broadcasted_iota(jnp.int32, wanted.shape, 1)
+        pick = jnp.where(wanted == place, 1.0, 0.0).astype(jnp.bfloat16)
+        ordered[rows, :] = jnp.dot(pick, table[...], preferred_element_type=jnp.float32).astype(
+            jnp.bfloat16
+        )
+        return carry
+
+    lax.fori_loop(0, ordered.shape[0] // FAR_ROWS, chunk, 0)
+
+
+def make_table(factor, harmonics):
+    return pl.pallas_call(
+        table_kernel,
+        out_shape=jax.ShapeDtypeStruct((harmonics.shape[0], OWN * TILE), jnp.bfloat16),
+        in_specs=[VMEM] * 2,
+        out_specs=VMEM,
+        compiler_params=LIMIT,
+        cost_estimate=pl.CostEstimate(
+            flops=1_000_000_000, bytes_accessed=4_000_000, transcendentals=0
+        ),
+        name="table",
+    )(factor.T, harmonics)
+
+
+def in_order(order, table):
+    return pl.pallas_call(
+        order_kernel,
+        out_shape=jax.ShapeDtypeStruct((order.shape[0], OWN * TILE), jnp.bfloat16),
+        in_specs=[VMEM] * 2,
+        out_specs=VMEM,
+        compiler_params=LIMIT,
+        cost_estimate=pl.CostEstimate(
+            flops=2_000_000_000, bytes_accessed=4_000_000, transcendentals=0
+        ),
+        name="order",
+    )(order[:, None], table)
 
 
 SCRATCH = pltpu.VMEM((SOURCES + 1, TILE, TILE), jnp.bfloat16)
@@ -225,6 +298,7 @@
         cost_estimate=pl.CostEstimate(
             flops=2_000_000_000, bytes_accessed=8_000_000, transcendentals=0
         ),
+        compiler_params=LIMIT,
         name="early",
     )(*made, blocks, incident, *pieces)
 
@@ -240,15 +314,17 @@
             pltpu.VMEM(TOTAL, jnp.float32),
             pltpu.SemaphoreType.DMA((len(pieces),)),
         ],
+        compiler_params=LIMIT,
         name="late",
     )(*made, blocks, before, tmatrix, *pieces)
 
 
 def last_pairs(made, blocks, before, tmatrix, weighted, pieces):
+    rows = sum(part.shape[0] for part in weighted)
     return pl.pallas_call(
         last_kernel,
-        out_shape=jax.ShapeDtypeStruct((weighted.shape[0], TILE), jnp.float32),
-        in_specs=[SMEM] * 3 + [VMEM] * 4 + [ANY] * len(pieces),
+        out_shape=jax.ShapeDtypeStruct((rows, TILE), jnp.float32),
+        in_specs=[SMEM] * 3 + [VMEM] * 5 + [ANY] * len(pieces),
         out_specs=VMEM,
         scratch_shapes=[
             SCRATCH,
@@ -256,8 +332,9 @@
             pltpu.VMEM((OWN * TILE, TILE), jnp.bfloat16),
             pltpu.SemaphoreType.DMA((len(pieces),)),
         ],
+        compiler_params=LIMIT,
         name="last",
-    )(*made, blocks, before, tmatrix, weighted, *pieces)
+    )(*made, blocks, before, tmatrix, *weighted, *pieces)
 
 
 def apply_tmatrix(tmatrix, field):
@@ -281,20 +358,17 @@
     n_grp, n_dev = lax.axis_size("grp"), lax.axis_size("dev")
     coeff = apply_tmatrix(tmatrix, incident)
     made = plan(source_table(need[0]), pair_src[0], pair_tgt[0] | (pair_blk[0] << 8), pair_count)
-    early, late = spread(coeff)
-    before = early_pairs(made, blocks, incident, early)
-    coeff = late_pairs(made, blocks, before, tmatrix, late)
+    table = make_table(factor, harmonics)
+    near, other, far = spread(coeff, table, made)
+    before = early_pairs(made, blocks, incident, near + other)
+    coeff = late_pairs(made, blocks, before, tmatrix, swapped(far, before))
 
     rows = owner.shape[0] // (n_grp * n_dev)
-    order = owner.reshape(n_grp, n_dev, rows).transpose(1, 0, 2).reshape(-1)
-    table = jnp.take(harmonics, order, axis=0).astype(jnp.float32)
-    phases = jnp.take(factor, order, axis=1)
-    weighted = (phases.T[:, :, None] * table[:, None, :]).astype(jnp.bfloat16)
-    weighted = weighted.reshape(owner.shape[0], -1)
-
-    early, late = spread(coeff)
-    before = early_pairs(made, blocks, incident, early)
-    far = last_pairs(made, blocks, before, tmatrix, weighted, late)
+    order = owner.reshape(n_grp, n_dev, rows).transpose(1, 0, 2).reshape(2, -1)
+    weighted = tuple(in_order(part, table) for part in order)
+    near, other, far = spread(coeff, weighted[0], weighted[1])
+    before = early_pairs(made, blocks, incident, near + other)
+    far = last_pairs(made, blocks, before, tmatrix, weighted, swapped(far, before))
 
     far = far.reshape(n_dev, n_grp * rows, TILE)
     far = lax.all_to_all(far, "dev", 0, 0).sum(axis=0)

time: 167 us -> 135 us (0.81)
  local copies, waits for them, and re-layouts: 25.8 us -> 10.1 us
  other arithmetic: 10.9 us -> 1.45 us
  blocking collectives: 44.8 us -> 37.5 us
  starting transfers between devices: 42.1 us -> 47.7 us
  Pallas kernels: 31.3 us -> 27.8 us
  waiting for transfers between devices: 8.37 us -> 6.24 us
    gather x2 -> x0, local copies, waits for them, and re-layouts: 13.7 us -> none  [the longest x1 7.56 us: body(): phases = jnp.take(factor, order, axis=1)]
    convert_element_type x2 -> x0, other arithmetic: 8.04 us -> none  [the longest x1 7.71 us: body(): weighted = (phases.T[:, :, None] * table[:, None, :]).astype(jnp.bfloat16)]
    all_to_all x1, blocking collectives: 19.6 us -> 12.5 us  [body(): return lax.all_to_all(far, 'grp', 0, 0).sum(axis=0)]
    ppermute x26 -> x36, starting transfers between devices: 42.1 us -> 47.7 us  [send(): return lax.ppermute(values, 'dev', pairs)]
    pallas_call x2, Pallas kernels: 13.9 us -> 8.78 us  [early_pairs(): pl.pallas_call(early_kernel, out_shape=jax.ShapeDtypeStruct(TOTAL, jnp.fl...]
    pallas_call x1 -> x4, Pallas kernels: 8 us -> 11.9 us  [the longest x2 5.97 us: in_order(): pl.pallas_call(order_kernel, out_shape=jax.ShapeDtypeStruct((order.shape[...]
    pallas_call x1, Pallas kernels: 5.23 us -> 2.53 us  [late_pairs(): pl.pallas_call(late_kernel, out_shape=jax.ShapeDtypeStruct(TOTAL, jnp.bfl...]
    ppermute x26 -> x36, waiting for transfers between devices: 8.37 us -> 6.24 us  [send(): return lax.ppermute(values, 'dev', pairs)]
  transfers between devices with their start and end apart: 26 -> 36, of which waited for: 4 -> 8; matrix products, arithmetic and copies ran while one was open for 19% -> 3% of each run, Pallas kernels for 11% -> 16%
where the time goes in v2:
time: 135 us; the launch traced here: 133 us
  starting transfers between devices  47.7 us (35%)
  blocking collectives  37.5 us (28%)
  Pallas kernels  27.8 us (21%)
  local copies, waits for them, and re-layouts  10.1 us (7%)
  waiting for transfers between devices  6.24 us (5%)
  other arithmetic  1.45 us (1%)
    ppermute x36, starting transfers between devices, send(): return lax.ppermute(values, 'dev', pairs)  47.7 us
    all_to_all x1, blocking collectives, body(): far = lax.all_to_all(far, 'dev', 0, 0).sum(axis=0)  25 us
    all_to_all x1, blocking collectives, body(): return lax.all_to_all(far, 'grp', 0, 0).sum(axis=0)  12.5 us
    pallas_call x2, Pallas kernels, early_pairs(): pl.pallas_call(early_kernel, out_shape=jax.ShapeDtypeStruct(TOTAL, jnp.fl...  8.78 us
    unnamed x32, local copies, waits for them, and re-layouts  8.64 us
    ppermute x36, waiting for transfers between devices, send(): return lax.ppermute(values, 'dev', pairs)  6.24 us
    pallas_call x2, Pallas kernels, in_order(): pl.pallas_call(order_kernel, out_shape=jax.ShapeDtypeStruct((order.shape[...  5.97 us
    pallas_call x1, Pallas kernels, plan(): pl.pallas_call(plan_kernel, out_shape=(jax.ShapeDtypeStruct(((LISTS + 1)...  4.59 us
  transfers between devices with their start and end apart: 36, of which 8 were waited for; matrix products, arithmetic and copies ran while one was open for 3% of the time, Pallas kernels for 16%

profile of v2, /device:TPU:1, one launch (start us, length us, event | category | flops | bytes accessed | tf_op | source)
XLA Modules:
  0.0 133.0 jit_solution(8119288845213359096)
XLA Ops:
  0.0 1.1 convolution_convert_fusion
  1.1 2.2 %collective-permute-start = (bf16[4,128,128]{2,1,0:T(8,128)(2,1)S(1)}, bf16[4,128,128]{2,1,0:T(8,128)(2,1)S(1)}, u32[]{:S(2)}, u32[]{:S(2)}) collective-permute-start(bf16[4,128,128]{2,1,0:T(8,128)(2,1)S(1)} %convolution_convert_fusion), channel_id=1, source_target_pairs={{0,8},{1,3},{2,10},{3,5},{4,12},{5,7},{6,14},{7,1},{8,16},{9,11},{... | collective-permute-start | bytes 393224 | tf_op jit(solution)/shard_map/ppermute | solution.py:47
  3.3 1.5 %collective-permute-start.1 = (bf16[4,128,128]{2,1,0:T(8,128)(2,1)S(1)}, bf16[4,128,128]{2,1,0:T(8,128)(2,1)S(1)}, u32[]{:S(2)}, u32[]{:S(2)}) collective-permute-start(bf16[4,128,128]{2,1,0:T(8,128)(2,1)S(1)} %convolution_convert_fusion), channel_id=1, source_target_pairs={{0,24},{1,7},{2,26},{3,1},{4,28},{5,3},{6,30},{7,5},{8,0},{9,15},{... | collective-permute-start | bytes 393224 | tf_op jit(solution)/shard_map/ppermute | solution.py:47
  5.1 0.8 copy.20
  6.6 0.7 shift-left_or_fusion
  7.3 0.7 copy-done.7
  8.0 4.6 %plan.1 = (s32[4680]{0:T(1024)S(1)}, s32[144]{0:T(256)S(1)}, s32[2]{0:T(128)S(1)}) custom-call(s32[128]{0:T(128)S(1)} %add.37.table, s32[512]{0:T(512)S(1)} %bitcast.11, s32[512]{0:T(512)S(1)} %bitcast.10, s32[1]{0:T(128)S(6)} %copy.30.count), custom_call_target="tpu_custom_call" | custom-call | flops 5000000000 | bytes 16384 | tf_op jit(solution)/shard_map/plan/pallas_call | solution.py:135
  13.0 1.7 %table.1 = bf16[2048,512]{1,0:T(8,128)(2,1)S(1)} custom-call(f32[2048,4]{1,0:T(8,128)S(1)} %bitcast.9, bf16[2048,128]{1,0:T(8,128)(2,1)S(1)} %copy-done.6), custom_call_target="tpu_custom_call" | custom-call | flops 1000000000 | bytes 4000000 | tf_op jit(solution)/shard_map/table/pallas_call | solution.py:260
  14.7 1.3 %copy-done.8 = bf16[2048,512]{1,0:T(8,128)(2,1)} copy-done((bf16[2048,512]{1,0:T(8,128)(2,1)}, bf16[2048,512]{1,0:T(8,128)(2,1)S(1)}, u32[]{:S(2)}) %copy-start.8) | copy-done | bytes 2097176
  16.2 2.6 %collective-permute-start.3 = (bf16[2,128,128]{2,1,0:T(8,128)(2,1)S(1)}, bf16[2,128,128]{2,1,0:T(8,128)(2,1)S(1)}, u32[]{:S(2)}, u32[]{:S(2)}) collective-permute-start(bf16[2,128,128]{2,1,0:T(8,128)(2,1)S(1)} %slice.15), channel_id=1, source_target_pairs={{0,24},{1,7},{2,26},{3,1},{4,28},{5,3},{6,30},{7,5},{8,0},{9,15},{... | collective-permute-start | bytes 196616 | tf_op jit(solution)/shard_map/ppermute | solution.py:47
  18.8 2.2 %collective-permute-start.6 = (bf16[8,128,128]{2,1,0:T(8,128)(2,1)S(1)}, bf16[8,128,128]{2,1,0:T(8,128)(2,1)S(1)}, u32[]{:S(2)}, u32[]{:S(2)}) collective-permute-start(bf16[8,128,128]{2,1,0:T(8,128)(2,1)S(1)} %pad_maximum_fusion.rest_0_), channel_id=1, source_target_pairs={{0,2},{1,9},{2,4},{3,11},{4,6},{5,13},{6,0},{7,15},{8,10},{9,17},{... | collective-permute-start | bytes 786440 | tf_op jit(solution)/shard_map/ppermute | solution.py:47
  21.1 1.4 %collective-permute-start.4 = (bf16[8,128,128]{2,1,0:T(8,128)(2,1)S(1)}, bf16[8,128,128]{2,1,0:T(8,128)(2,1)S(1)}, u32[]{:S(2)}, u32[]{:S(2)}) collective-permute-start(bf16[8,128,128]{2,1,0:T(8,128)(2,1)S(1)} %pad_maximum_fusion.rest_0_), channel_id=1, source_target_pairs={{0,6},{1,25},{2,0},{3,27},{4,2},{5,29},{6,4},{7,31},{8,14},{9,1},{... | collective-permute-start | bytes 786440 | tf_op jit(solution)/shard_map/ppermute | solution.py:47
  22.4 3.6 %collective-permute-start.8 = (bf16[8,128,128]{2,1,0:T(8,128)(2,1)S(1)}, bf16[8,128,128]{2,1,0:T(8,128)(2,1)S(1)}, u32[]{:S(2)}, u32[]{:S(2)}) collective-permute-start(bf16[8,128,128]{2,1,0:T(8,128)(2,1)S(1)} %pad_maximum_fusion.rest_0_), channel_id=1, source_target_pairs={{0,1},{1,0},{2,3},{3,2},{4,5},{5,4},{6,7},{7,6},{8,9},{9,8},{10,11... | collective-permute-start | bytes 786440 | tf_op jit(solution)/shard_map/ppermute | solution.py:47
  26.1 1.7 %collective-permute-start.5 = (bf16[8,128,128]{2,1,0:T(8,128)(2,1)S(1)}, bf16[8,128,128]{2,1,0:T(8,128)(2,1)S(1)}, u32[]{:S(2)}, u32[]{:S(2)}) collective-permute-start(bf16[8,128,128]{2,1,0:T(8,128)(2,1)S(1)} %constant_dynamic-update-slice_fusion.rest_1_), channel_id=1, source_target_pairs={{0,6},{1,25},{2,0},{3,27},{4,2},{5,29},{6,4},{7,31},{8,14},{9,1},{... | collective-permute-start | bytes 786440 | tf_op jit(solution)/shard_map/ppermute | solution.py:47
  27.8 2.6 %collective-permute-start.9 = (bf16[8,128,128]{2,1,0:T(8,128)(2,1)S(1)}, bf16[8,128,128]{2,1,0:T(8,128)(2,1)S(1)}, u32[]{:S(2)}, u32[]{:S(2)}) collective-permute-start(bf16[8,128,128]{2,1,0:T(8,128)(2,1)S(1)} %constant_dynamic-update-slice_fusion.rest_1_), channel_id=1, source_target_pairs={{0,1},{1,0},{2,3},{3,2},{4,5},{5,4},{6,7},{7,6},{8,9},{9,8},{10,11... | collective-permute-start | bytes 786440 | tf_op jit(solution)/shard_map/ppermute | solution.py:47
  30.9 0.8 collective-permute-done.5.rest_3_
  31.7 1.0 collective-permute-start.11
  32.8 1.8 %collective-permute-done.7.rest_5_ = bf16[8,128,128]{2,1,0:T(8,128)(2,1)S(1)} collective-permute-done((bf16[8,128,128]{2,1,0:T(8,128)(2,1)S(1)}, bf16[8,128,128]{2,1,0:T(8,128)(2,1)S(1)}, u32[]{:S(2)}, u32[]{:S(2)}) %collective-permute-start.7) | collective-permute-done | bytes 262176 | tf_op jit(solution)/shard_map/ppermute | solution.py:47
  34.6 0.9 collective-permute-start.13
  35.4 1.4 %collective-permute-start.14 = (bf16[8,128,128]{2,1,0:T(8,128)(2,1)S(1)}, bf16[8,128,128]{2,1,0:T(8,128)(2,1)S(1)}, u32[]{:S(2)}, u32[]{:S(2)}) collective-permute-start(bf16[8,128,128]{2,1,0:T(8,128)(2,1)S(1)} %collective-permute-done.6.rest_4_), channel_id=1, source_target_pairs={{0,2},{1,9},{2,4},{3,11},{4,6},{5,13},{6,0},{7,15},{8,10},{9,17},{... | collective-permute-start | bytes 786440 | tf_op jit(solution)/shard_map/ppermute | solution.py:47
  36.8 1.9 %collective-permute-start.15 = (bf16[8,128,128]{2,1,0:T(8,128)(2,1)S(1)}, bf16[8,128,128]{2,1,0:T(8,128)(2,1)S(1)}, u32[]{:S(2)}, u32[]{:S(2)}) collective-permute-start(bf16[8,128,128]{2,1,0:T(8,128)(2,1)S(1)} %collective-permute-done.5.rest_3_), channel_id=1, source_target_pairs={{0,6},{1,25},{2,0},{3,27},{4,2},{5,29},{6,4},{7,31},{8,14},{9,1},{... | collective-permute-start | bytes 786440 | tf_op jit(solution)/shard_map/ppermute | solution.py:47
  38.7 0.7 reshape.45
  39.5 0.7 copy-done.4
  40.2 2.2 %copy-done = bf16[128,128,128]{2,1,0:T(8,128)(2,1)S(1)} copy-done((bf16[128,128,128]{2,1,0:T(8,128)(2,1)S(1)}, bf16[128,128,128]{2,1,0:T(8,128)(2,1)}, u32[]{:S(2)}) %copy-start) | copy-done | bytes 4194328
  42.4 0.9 copy-done.5
  43.3 4.9 %early.2.before = f32[4,128,128]{2,1,0:T(8,128)S(1)} custom-call(s32[4680]{0:T(1024)S(1)} %get-tuple-element.20.lists, s32[144]{0:T(256)S(1)} %get-tuple-element.21.groups, s32[2]{0:T(128)S(1)} %get-tuple-element.22.sizes, bf16[128,128,128]{2,1,0:T(8,128)(2,1)S(1)} %copy-done, bf16[4,128,128]{2,1,0:T(8,128)(2,1)S(1)} %copy-done.2, ...), custom_call_target="tpu_custom_call" | custom-call | flops 2000000000 | bytes 8000000 | tf_op jit(solution)/shard_map/early/pallas_call | solution.py:292
  49.3 1.6 %copy-done.9 = bf16[2048,512]{1,0:T(8,128)(2,1)S(1)} copy-done((bf16[2048,512]{1,0:T(8,128)(2,1)S(1)}, bf16[2048,512]{1,0:T(8,128)(2,1)}, u32[]{:S(2)}) %copy-start.9) | copy-done | bytes 2097176
  50.9 3.0 %order.2.weighted_a = bf16[1024,512]{1,0:T(8,128)(2,1)S(1)} custom-call(s32[1024,1]{1,0:T(8,128)S(1)} %broadcast_in_dim_unstack.8.order, bf16[2048,512]{1,0:T(8,128)(2,1)S(1)} %copy-done.9), custom_call_target="tpu_custom_call" | custom-call | flops 2000000000 | bytes 4000000 | tf_op jit(solution)/shard_map/order/pallas_call | solution.py:274
  53.9 2.5 %late.1 = bf16[4,128,128]{2,1,0:T(8,128)(2,1)S(1)} custom-call(s32[4680]{0:T(1024)S(1)} %get-tuple-element.20.lists, s32[144]{0:T(256)S(1)} %get-tuple-element.21.groups, s32[2]{0:T(128)S(1)} %get-tuple-element.22.sizes, bf16[128,128,128]{2,1,0:T(8,128)(2,1)S(1)} %copy-done.1, f32[4,128,128]{2,1,0:T(8,128)S(1)} %early.2.before, ...), custom_call_target="tpu_custom_call" | custom-call | tf_op jit(solution)/shard_map/late/pallas_call | solution.py:307
  56.6 2.7 %collective-permute-start.19 = (bf16[4,128,128]{2,1,0:T(8,128)(2,1)S(1)}, bf16[4,128,128]{2,1,0:T(8,128)(2,1)S(1)}, u32[]{:S(2)}, u32[]{:S(2)}) collective-permute-start(bf16[4,128,128]{2,1,0:T(8,128)(2,1)S(1)} %late.1), channel_id=1, source_target_pairs={{0,24},{1,7},{2,26},{3,1},{4,28},{5,3},{6,30},{7,5},{8,0},{9,15},{... | collective-permute-start | bytes 393224 | tf_op jit(solution)/shard_map/ppermute | solution.py:47
  59.2 3.0 %order.3.weighted_b = bf16[1024,512]{1,0:T(8,128)(2,1)S(1)} custom-call(s32[1024,1]{1,0:T(8,128)S(1)} %broadcast_in_dim_unstack.9.order, bf16[2048,512]{1,0:T(8,128)(2,1)S(1)} %copy-done.9), custom_call_target="tpu_custom_call" | custom-call | flops 2000000000 | bytes 4000000 | tf_op jit(solution)/shard_map/order/pallas_call | solution.py:274
  62.3 2.7 %collective-permute-start.21 = (bf16[2,128,128]{2,1,0:T(8,128)(2,1)S(1)}, bf16[2,128,128]{2,1,0:T(8,128)(2,1)S(1)}, u32[]{:S(2)}, u32[]{:S(2)}) collective-permute-start(bf16[2,128,128]{2,1,0:T(8,128)(2,1)S(1)} %slice.17), channel_id=1, source_target_pairs={{0,24},{1,7},{2,26},{3,1},{4,28},{5,3},{6,30},{7,5},{8,0},{9,15},{... | collective-permute-start | bytes 196616 | tf_op jit(solution)/shard_map/ppermute | solution.py:47
  65.0 5.3 %collective-permute-start.22 = (bf16[8,128,128]{2,1,0:T(8,128)(2,1)S(1)}, bf16[8,128,128]{2,1,0:T(8,128)(2,1)S(1)}, u32[]{:S(2)}, u32[]{:S(2)}) collective-permute-start(bf16[8,128,128]{2,1,0:T(8,128)(2,1)S(1)} %pad_maximum_fusion.1.rest_0_), channel_id=1, source_target_pairs={{0,6},{1,25},{2,0},{3,27},{4,2},{5,29},{6,4},{7,31},{8,14},{9,1},{... | collective-permute-start | bytes 786440 | tf_op jit(solution)/shard_map/ppermute | solution.py:47
  70.4 2.0 %collective-permute-start.26 = (bf16[8,128,128]{2,1,0:T(8,128)(2,1)S(1)}, bf16[8,128,128]{2,1,0:T(8,128)(2,1)S(1)}, u32[]{:S(2)}, u32[]{:S(2)}) collective-permute-start(bf16[8,128,128]{2,1,0:T(8,128)(2,1)S(1)} %pad_maximum_fusion.1.rest_0_), channel_id=1, source_target_pairs={{0,1},{1,0},{2,3},{3,2},{4,5},{5,4},{6,7},{7,6},{8,9},{9,8},{10,11... | collective-permute-start | bytes 786440 | tf_op jit(solution)/shard_map/ppermute | solution.py:47
  72.4 1.7 %collective-permute-start.23 = (bf16[8,128,128]{2,1,0:T(8,128)(2,1)S(1)}, bf16[8,128,128]{2,1,0:T(8,128)(2,1)S(1)}, u32[]{:S(2)}, u32[]{:S(2)}) collective-permute-start(bf16[8,128,128]{2,1,0:T(8,128)(2,1)S(1)} %constant_dynamic-update-slice_fusion.3.rest_1_), channel_id=1, source_target_pairs={{0,6},{1,25},{2,0},{3,27},{4,2},{5,29},{6,4},{7,31},{8,14},{9,1},{... | collective-permute-start | bytes 786440 | tf_op jit(solution)/shard_map/ppermute | solution.py:47
  74.4 2.4 %collective-permute-start.27 = (bf16[8,128,128]{2,1,0:T(8,128)(2,1)S(1)}, bf16[8,128,128]{2,1,0:T(8,128)(2,1)S(1)}, u32[]{:S(2)}, u32[]{:S(2)}) collective-permute-start(bf16[8,128,128]{2,1,0:T(8,128)(2,1)S(1)} %constant_dynamic-update-slice_fusion.3.rest_1_), channel_id=1, source_target_pairs={{0,1},{1,0},{2,3},{3,2},{4,5},{5,4},{6,7},{7,6},{8,9},{9,8},{10,11... | collective-permute-start | bytes 786440 | tf_op jit(solution)/shard_map/ppermute | solution.py:47
  77.1 0.9 collective-permute-start.28
  78.0 1.5 %collective-permute-start.29 = (bf16[8,128,128]{2,1,0:T(8,128)(2,1)S(1)}, bf16[8,128,128]{2,1,0:T(8,128)(2,1)S(1)}, u32[]{:S(2)}, u32[]{:S(2)}) collective-permute-start(bf16[8,128,128]{2,1,0:T(8,128)(2,1)S(1)} %collective-permute-done.23.rest_3_), channel_id=1, source_target_pairs={{0,1},{1,0},{2,3},{3,2},{4,5},{5,4},{6,7},{7,6},{8,9},{9,8},{10,11... | collective-permute-start | bytes 786440 | tf_op jit(solution)/shard_map/ppermute | solution.py:47
  79.5 1.3 collective-permute-done.25.rest_5_
  81.4 0.6 collective-permute-start.32
  82.0 2.1 %collective-permute-start.33 = (bf16[8,128,128]{2,1,0:T(8,128)(2,1)S(1)}, bf16[8,128,128]{2,1,0:T(8,128)(2,1)S(1)}, u32[]{:S(2)}, u32[]{:S(2)}) collective-permute-start(bf16[8,128,128]{2,1,0:T(8,128)(2,1)S(1)} %collective-permute-done.23.rest_3_), channel_id=1, source_target_pairs={{0,6},{1,25},{2,0},{3,27},{4,2},{5,29},{6,4},{7,31},{8,14},{9,1},{... | collective-permute-start | bytes 786440 | tf_op jit(solution)/shard_map/ppermute | solution.py:47
  84.1 3.9 %early.3.before = f32[4,128,128]{2,1,0:T(8,128)S(1)} custom-call(s32[4680]{0:T(1024)S(1)} %get-tuple-element.20.lists, s32[144]{0:T(256)S(1)} %get-tuple-element.21.groups, s32[2]{0:T(128)S(1)} %get-tuple-element.22.sizes, bf16[128,128,128]{2,1,0:T(8,128)(2,1)S(1)} %copy-done.1, bf16[4,128,128]{2,1,0:T(8,128)(2,1)S(1)} %copy-done.2, ...), custom_call_target="tpu_custom_call" | custom-call | flops 2000000000 | bytes 8000000 | tf_op jit(solution)/shard_map/early/pallas_call | solution.py:292
  88.1 0.9 collective-permute-start.34
  89.0 1.2 collective-permute-done.34.rest_2_
  90.5 4.2 %last.1 = f32[2048,128]{1,0:T(8,128)S(1)} custom-call(s32[4680]{0:T(1024)S(1)} %get-tuple-element.20.lists, s32[144]{0:T(256)S(1)} %get-tuple-element.21.groups, s32[2]{0:T(128)S(1)} %get-tuple-element.22.sizes, bf16[128,128,128]{2,1,0:T(8,128)(2,1)S(1)} %copy-done.1, f32[4,128,128]{2,1,0:T(8,128)S(1)} %early.3.before, bf16[4,128,128]{2,1,0:T(8,128)(2,1)S(1)} %copy-done.3, ...), custom_call_target="tpu_custom_call" | custom-call | tf_op jit(solution)/shard_map/last/pallas_call | solution.py:324
  94.8 25.0 %all_to_all.10 = f32[32,64,128]{2,1,0:T(8,128)S(1)} all-to-all(f32[32,64,128]{2,1,0:T(8,128)S(1)} %bitcast.8), channel_id=1, replica_groups=mesh['grp'=8,'dev'=32] {'dev'}, dimensions={0} | all-to-all | bytes 2097152 | tf_op jit(solution)/shard_map/all_to_all | solution.py:374
  119.9 12.5 %all_to_all.11 = f32[8,8,128]{2,1,0:T(8,128)S(1)} all-to-all(f32[8,8,128]{2,1,0:T(8,128)S(1)} %bitcast.13), channel_id=1, replica_groups=mesh['grp'=8,'dev'=32] {'grp'}, dimensions={0} | all-to-all | bytes 65536 | tf_op jit(solution)/shard_map/all_to_all | solution.py:376
  132.4 0.6 reduce_sum.19
  (89 shorter events, 4.5 us)
Async XLA Ops:
  1.1 14.9 %collective-permute-start = (bf16[4,128,128]{2,1,0:T(8,128)(2,1)S(1)}, bf16[4,128,128]{2,1,0:T(8,128)(2,1)S(1)}, u32[]{:S(2)}, u32[]{:S(2)}) collective-permute-start(bf16[4,128,128]{2,1,0:T(8,128)(2,1)S(1)} %convolution_convert_fusion), channel_id=1, source_target_pairs={{0,8},{1,3},{2,10},{3,5},{4,12},{5,7},{6,14},{7,1},{8,16},{9,11},{... | collective-permute-start | bytes 393224 | tf_op jit(solution)/shard_map/ppermute | solution.py:47
  3.3 12.7 %collective-permute-start.1 = (bf16[4,128,128]{2,1,0:T(8,128)(2,1)S(1)}, bf16[4,128,128]{2,1,0:T(8,128)(2,1)S(1)}, u32[]{:S(2)}, u32[]{:S(2)}) collective-permute-start(bf16[4,128,128]{2,1,0:T(8,128)(2,1)S(1)} %convolution_convert_fusion), channel_id=1, source_target_pairs={{0,24},{1,7},{2,26},{3,1},{4,28},{5,3},{6,30},{7,5},{8,0},{9,15},{... | collective-permute-start | bytes 393224 | tf_op jit(solution)/shard_map/ppermute | solution.py:47
  8.0 4.6 %copy-start.11 = (f32[4,2048]{1,0:T(4,128)S(1)}, f32[4,2048]{1,0:T(4,128)}, u32[]{:S(2)}) copy-start(f32[4,2048]{1,0:T(4,128)} %param.19) | copy-start | bytes 98308
  8.0 5.0 %copy-start.6 = (bf16[2048,128]{1,0:T(8,128)(2,1)S(1)}, bf16[2048,128]{1,0:T(8,128)(2,1)}, u32[]{:S(2)}) copy-start(bf16[2048,128]{1,0:T(8,128)(2,1)} %harmonics.1) | copy-start | bytes 1572868
  12.6 26.1 %copy-start.12 = (s32[2048]{0:T(1024)S(1)}, s32[2048]{0:T(1024)}, u32[]{:S(2)}) copy-start(s32[2048]{0:T(1024)} %param.21) | copy-start | bytes 24580
  12.6 27.6 %copy-start.2 = (bf16[4,128,128]{2,1,0:T(8,128)(2,1)S(1)}, bf16[4,128,128]{2,1,0:T(8,128)(2,1)}, u32[]{:S(2)}) copy-start(bf16[4,128,128]{2,1,0:T(8,128)(2,1)} %incident.3) | copy-start | bytes 393220
  14.7 1.4 %copy-start.8 = (bf16[2048,512]{1,0:T(8,128)(2,1)}, bf16[2048,512]{1,0:T(8,128)(2,1)S(1)}, u32[]{:S(2)}) copy-start(bf16[2048,512]{1,0:T(8,128)(2,1)S(1)} %table.1) | copy-start | bytes 6291460
  16.0 10.0 %collective-permute-start.2 = (bf16[2,128,128]{2,1,0:T(8,128)(2,1)S(1)}, bf16[2,128,128]{2,1,0:T(8,128)(2,1)S(1)}, u32[]{:S(2)}, u32[]{:S(2)}) collective-permute-start(bf16[2,128,128]{2,1,0:T(8,128)(2,1)S(1)} %slice.14), channel_id=1, source_target_pairs={{0,8},{1,3},{2,10},{3,5},{4,12},{5,7},{6,14},{7,1},{8,16},{9,11},{... | collective-permute-start | bytes 196616 | tf_op jit(solution)/shard_map/ppermute | solution.py:47
  16.2 9.9 %collective-permute-start.3 = (bf16[2,128,128]{2,1,0:T(8,128)(2,1)S(1)}, bf16[2,128,128]{2,1,0:T(8,128)(2,1)S(1)}, u32[]{:S(2)}, u32[]{:S(2)}) collective-permute-start(bf16[2,128,128]{2,1,0:T(8,128)(2,1)S(1)} %slice.15), channel_id=1, source_target_pairs={{0,24},{1,7},{2,26},{3,1},{4,28},{5,3},{6,30},{7,5},{8,0},{9,15},{... | collective-permute-start | bytes 196616 | tf_op jit(solution)/shard_map/ppermute | solution.py:47
  18.8 9.0 %collective-permute-start.6 = (bf16[8,128,128]{2,1,0:T(8,128)(2,1)S(1)}, bf16[8,128,128]{2,1,0:T(8,128)(2,1)S(1)}, u32[]{:S(2)}, u32[]{:S(2)}) collective-permute-start(bf16[8,128,128]{2,1,0:T(8,128)(2,1)S(1)} %pad_maximum_fusion.rest_0_), channel_id=1, source_target_pairs={{0,2},{1,9},{2,4},{3,11},{4,6},{5,13},{6,0},{7,15},{8,10},{9,17},{... | collective-permute-start | bytes 786440 | tf_op jit(solution)/shard_map/ppermute | solution.py:47
  21.1 9.3 %collective-permute-start.4 = (bf16[8,128,128]{2,1,0:T(8,128)(2,1)S(1)}, bf16[8,128,128]{2,1,0:T(8,128)(2,1)S(1)}, u32[]{:S(2)}, u32[]{:S(2)}) collective-permute-start(bf16[8,128,128]{2,1,0:T(8,128)(2,1)S(1)} %pad_maximum_fusion.rest_0_), channel_id=1, source_target_pairs={{0,6},{1,25},{2,0},{3,27},{4,2},{5,29},{6,4},{7,31},{8,14},{9,1},{... | collective-permute-start | bytes 786440 | tf_op jit(solution)/shard_map/ppermute | solution.py:47
  22.4 8.0 %collective-permute-start.8 = (bf16[8,128,128]{2,1,0:T(8,128)(2,1)S(1)}, bf16[8,128,128]{2,1,0:T(8,128)(2,1)S(1)}, u32[]{:S(2)}, u32[]{:S(2)}) collective-permute-start(bf16[8,128,128]{2,1,0:T(8,128)(2,1)S(1)} %pad_maximum_fusion.rest_0_), channel_id=1, source_target_pairs={{0,1},{1,0},{2,3},{3,2},{4,5},{5,4},{6,7},{7,6},{8,9},{9,8},{10,11... | collective-permute-start | bytes 786440 | tf_op jit(solution)/shard_map/ppermute | solution.py:47
  26.1 5.6 %collective-permute-start.5 = (bf16[8,128,128]{2,1,0:T(8,128)(2,1)S(1)}, bf16[8,128,128]{2,1,0:T(8,128)(2,1)S(1)}, u32[]{:S(2)}, u32[]{:S(2)}) collective-permute-start(bf16[8,128,128]{2,1,0:T(8,128)(2,1)S(1)} %constant_dynamic-update-slice_fusion.rest_1_), channel_id=1, source_target_pairs={{0,6},{1,25},{2,0},{3,27},{4,2},{5,29},{6,4},{7,31},{8,14},{9,1},{... | collective-permute-start | bytes 786440 | tf_op jit(solution)/shard_map/ppermute | solution.py:47
  27.8 6.7 %collective-permute-start.7 = (bf16[8,128,128]{2,1,0:T(8,128)(2,1)S(1)}, bf16[8,128,128]{2,1,0:T(8,128)(2,1)S(1)}, u32[]{:S(2)}, u32[]{:S(2)}) collective-permute-start(bf16[8,128,128]{2,1,0:T(8,128)(2,1)S(1)} %constant_dynamic-update-slice_fusion.rest_1_), channel_id=1, source_target_pairs={{0,2},{1,9},{2,4},{3,11},{4,6},{5,13},{6,0},{7,15},{8,10},{9,17},{... | collective-permute-start | bytes 786440 | tf_op jit(solution)/shard_map/ppermute | solution.py:47
  27.8 7.6 %collective-permute-start.9 = (bf16[8,128,128]{2,1,0:T(8,128)(2,1)S(1)}, bf16[8,128,128]{2,1,0:T(8,128)(2,1)S(1)}, u32[]{:S(2)}, u32[]{:S(2)}) collective-permute-start(bf16[8,128,128]{2,1,0:T(8,128)(2,1)S(1)} %constant_dynamic-update-slice_fusion.rest_1_), channel_id=1, source_target_pairs={{0,1},{1,0},{2,3},{3,2},{4,5},{5,4},{6,7},{7,6},{8,9},{9,8},{10,11... | collective-permute-start | bytes 786440 | tf_op jit(solution)/shard_map/ppermute | solution.py:47
  30.4 6.4 %collective-permute-start.12 = (bf16[8,128,128]{2,1,0:T(8,128)(2,1)S(1)}, bf16[8,128,128]{2,1,0:T(8,128)(2,1)S(1)}, u32[]{:S(2)}, u32[]{:S(2)}) collective-permute-start(bf16[8,128,128]{2,1,0:T(8,128)(2,1)S(1)} %collective-permute-done.6.rest_4_), channel_id=1, source_target_pairs={{0,1},{1,0},{2,3},{3,2},{4,5},{5,4},{6,7},{7,6},{8,9},{9,8},{10,11... | collective-permute-start | bytes 786440 | tf_op jit(solution)/shard_map/ppermute | solution.py:47
  30.4 9.1 %collective-permute-start.10 = (bf16[8,128,128]{2,1,0:T(8,128)(2,1)S(1)}, bf16[8,128,128]{2,1,0:T(8,128)(2,1)S(1)}, u32[]{:S(2)}, u32[]{:S(2)}) collective-permute-start(bf16[8,128,128]{2,1,0:T(8,128)(2,1)S(1)} %collective-permute-done.4.rest_2_), channel_id=1, source_target_pairs={{0,1},{1,0},{2,3},{3,2},{4,5},{5,4},{6,7},{7,6},{8,9},{9,8},{10,11... | collective-permute-start | bytes 786440 | tf_op jit(solution)/shard_map/ppermute | solution.py:47
  31.7 8.5 %collective-permute-start.11 = (bf16[8,128,128]{2,1,0:T(8,128)(2,1)S(1)}, bf16[8,128,128]{2,1,0:T(8,128)(2,1)}, u32[]{:S(2)}, u32[]{:S(2)}) collective-permute-start(bf16[8,128,128]{2,1,0:T(8,128)(2,1)S(1)} %collective-permute-done.5.rest_3_), channel_id=1, source_target_pairs={{0,1},{1,0},{2,3},{3,2},{4,5},{5,4},{6,7},{7,6},{8,9},{9,8},{10,11... | collective-permute-start | bytes 786440 | tf_op jit(solution)/shard_map/ppermute | solution.py:47
  34.6 5.6 %collective-permute-start.13 = (bf16[8,128,128]{2,1,0:T(8,128)(2,1)S(1)}, bf16[8,128,128]{2,1,0:T(8,128)(2,1)}, u32[]{:S(2)}, u32[]{:S(2)}) collective-permute-start(bf16[8,128,128]{2,1,0:T(8,128)(2,1)S(1)} %collective-permute-done.7.rest_5_), channel_id=1, source_target_pairs={{0,1},{1,0},{2,3},{3,2},{4,5},{5,4},{6,7},{7,6},{8,9},{9,8},{10,11... | collective-permute-start | bytes 786440 | tf_op jit(solution)/shard_map/ppermute | solution.py:47
  35.4 12.8 %collective-permute-start.14 = (bf16[8,128,128]{2,1,0:T(8,128)(2,1)S(1)}, bf16[8,128,128]{2,1,0:T(8,128)(2,1)S(1)}, u32[]{:S(2)}, u32[]{:S(2)}) collective-permute-start(bf16[8,128,128]{2,1,0:T(8,128)(2,1)S(1)} %collective-permute-done.6.rest_4_), channel_id=1, source_target_pairs={{0,2},{1,9},{2,4},{3,11},{4,6},{5,13},{6,0},{7,15},{8,10},{9,17},{... | collective-permute-start | bytes 786440 | tf_op jit(solution)/shard_map/ppermute | solution.py:47
  36.8 11.4 %collective-permute-start.15 = (bf16[8,128,128]{2,1,0:T(8,128)(2,1)S(1)}, bf16[8,128,128]{2,1,0:T(8,128)(2,1)S(1)}, u32[]{:S(2)}, u32[]{:S(2)}) collective-permute-start(bf16[8,128,128]{2,1,0:T(8,128)(2,1)S(1)} %collective-permute-done.5.rest_3_), channel_id=1, source_target_pairs={{0,6},{1,25},{2,0},{3,27},{4,2},{5,29},{6,4},{7,31},{8,14},{9,1},{... | collective-permute-start | bytes 786440 | tf_op jit(solution)/shard_map/ppermute | solution.py:47
  39.5 0.7 copy-start.4
  40.2 2.2 %copy-start = (bf16[128,128,128]{2,1,0:T(8,128)(2,1)S(1)}, bf16[128,128,128]{2,1,0:T(8,128)(2,1)}, u32[]{:S(2)}) copy-start(bf16[128,128,128]{2,1,0:T(8,128)(2,1)} %blocks.7) | copy-start | bytes 12582916
  42.4 0.9 copy-start.5
  43.3 5.5 %copy-start.10 = (s32[8,32,8]{2,1,0:T(8,128)S(1)}, s32[8,32,8]{2,1,0:T(8,128)}, u32[]{:S(2)}) copy-start(s32[8,32,8]{2,1,0:T(8,128)} %reshape.45) | copy-start | bytes 24580
  48.2 5.7 %collective-permute-start.16 = (bf16[8,128,128]{2,1,0:T(8,128)(2,1)S(1)}, bf16[8,128,128]{2,1,0:T(8,128)(2,1)S(1)}, u32[]{:S(2)}, u32[]{:S(2)}) collective-permute-start(bf16[8,128,128]{2,1,0:T(8,128)(2,1)S(1)} %collective-permute-done.14.rest_0_), channel_id=1, source_target_pairs={{0,1},{1,0},{2,3},{3,2},{4,5},{5,4},{6,7},{7,6},{8,9},{9,8},{10,11... | collective-permute-start | bytes 786440 | tf_op jit(solution)/shard_map/ppermute | solution.py:47
  48.3 5.6 %collective-permute-start.17 = (bf16[8,128,128]{2,1,0:T(8,128)(2,1)S(1)}, bf16[8,128,128]{2,1,0:T(8,128)(2,1)S(1)}, u32[]{:S(2)}, u32[]{:S(2)}) collective-permute-start(bf16[8,128,128]{2,1,0:T(8,128)(2,1)S(1)} %collective-permute-done.15.rest_1_), channel_id=1, source_target_pairs={{0,1},{1,0},{2,3},{3,2},{4,5},{5,4},{6,7},{7,6},{8,9},{9,8},{10,11... | collective-permute-start | bytes 786440 | tf_op jit(solution)/shard_map/ppermute | solution.py:47
  49.1 4.8 %copy-start.3 = (bf16[4,128,128]{2,1,0:T(8,128)(2,1)S(1)}, bf16[4,128,128]{2,1,0:T(8,128)(2,1)}, u32[]{:S(2)}) copy-start(bf16[4,128,128]{2,1,0:T(8,128)(2,1)} %tmatrix.3) | copy-start | bytes 393220
  49.3 1.6 %copy-start.9 = (bf16[2048,512]{1,0:T(8,128)(2,1)S(1)}, bf16[2048,512]{1,0:T(8,128)(2,1)}, u32[]{:S(2)}) copy-start(bf16[2048,512]{1,0:T(8,128)(2,1)} %copy-done.8) | copy-start | bytes 6291460
  50.9 3.0 %copy-start.1 = (bf16[128,128,128]{2,1,0:T(8,128)(2,1)S(1)}, bf16[128,128,128]{2,1,0:T(8,128)(2,1)}, u32[]{:S(2)}) copy-start(bf16[128,128,128]{2,1,0:T(8,128)(2,1)} %blocks.7) | copy-start | bytes 12582916
  56.5 5.7 %collective-permute-start.18 = (bf16[4,128,128]{2,1,0:T(8,128)(2,1)S(1)}, bf16[4,128,128]{2,1,0:T(8,128)(2,1)S(1)}, u32[]{:S(2)}, u32[]{:S(2)}) collective-permute-start(bf16[4,128,128]{2,1,0:T(8,128)(2,1)S(1)} %late.1), channel_id=1, source_target_pairs={{0,8},{1,3},{2,10},{3,5},{4,12},{5,7},{6,14},{7,1},{8,16},{9,11},{... | collective-permute-start | bytes 393224 | tf_op jit(solution)/shard_map/ppermute | solution.py:47
  56.6 5.7 %collective-permute-start.19 = (bf16[4,128,128]{2,1,0:T(8,128)(2,1)S(1)}, bf16[4,128,128]{2,1,0:T(8,128)(2,1)S(1)}, u32[]{:S(2)}, u32[]{:S(2)}) collective-permute-start(bf16[4,128,128]{2,1,0:T(8,128)(2,1)S(1)} %late.1), channel_id=1, source_target_pairs={{0,24},{1,7},{2,26},{3,1},{4,28},{5,3},{6,30},{7,5},{8,0},{9,15},{... | collective-permute-start | bytes 393224 | tf_op jit(solution)/shard_map/ppermute | solution.py:47
  62.2 10.1 %collective-permute-start.20 = (bf16[2,128,128]{2,1,0:T(8,128)(2,1)S(1)}, bf16[2,128,128]{2,1,0:T(8,128)(2,1)S(1)}, u32[]{:S(2)}, u32[]{:S(2)}) collective-permute-start(bf16[2,128,128]{2,1,0:T(8,128)(2,1)S(1)} %slice.16), channel_id=1, source_target_pairs={{0,8},{1,3},{2,10},{3,5},{4,12},{5,7},{6,14},{7,1},{8,16},{9,11},{... | collective-permute-start | bytes 196616 | tf_op jit(solution)/shard_map/ppermute | solution.py:47
  62.3 10.0 %collective-permute-start.21 = (bf16[2,128,128]{2,1,0:T(8,128)(2,1)S(1)}, bf16[2,128,128]{2,1,0:T(8,128)(2,1)S(1)}, u32[]{:S(2)}, u32[]{:S(2)}) collective-permute-start(bf16[2,128,128]{2,1,0:T(8,128)(2,1)S(1)} %slice.17), channel_id=1, source_target_pairs={{0,24},{1,7},{2,26},{3,1},{4,28},{5,3},{6,30},{7,5},{8,0},{9,15},{... | collective-permute-start | bytes 196616 | tf_op jit(solution)/shard_map/ppermute | solution.py:47
  65.0 9.3 %collective-permute-start.22 = (bf16[8,128,128]{2,1,0:T(8,128)(2,1)S(1)}, bf16[8,128,128]{2,1,0:T(8,128)(2,1)S(1)}, u32[]{:S(2)}, u32[]{:S(2)}) collective-permute-start(bf16[8,128,128]{2,1,0:T(8,128)(2,1)S(1)} %pad_maximum_fusion.1.rest_0_), channel_id=1, source_target_pairs={{0,6},{1,25},{2,0},{3,27},{4,2},{5,29},{6,4},{7,31},{8,14},{9,1},{... | collective-permute-start | bytes 786440 | tf_op jit(solution)/shard_map/ppermute | solution.py:47
  70.3 6.7 %collective-permute-start.24 = (bf16[8,128,128]{2,1,0:T(8,128)(2,1)S(1)}, bf16[8,128,128]{2,1,0:T(8,128)(2,1)S(1)}, u32[]{:S(2)}, u32[]{:S(2)}) collective-permute-start(bf16[8,128,128]{2,1,0:T(8,128)(2,1)S(1)} %pad_maximum_fusion.1.rest_0_), channel_id=1, source_target_pairs={{0,2},{1,9},{2,4},{3,11},{4,6},{5,13},{6,0},{7,15},{8,10},{9,17},{... | collective-permute-start | bytes 786440 | tf_op jit(solution)/shard_map/ppermute | solution.py:47
  70.4 7.7 %collective-permute-start.26 = (bf16[8,128,128]{2,1,0:T(8,128)(2,1)S(1)}, bf16[8,128,128]{2,1,0:T(8,128)(2,1)S(1)}, u32[]{:S(2)}, u32[]{:S(2)}) collective-permute-start(bf16[8,128,128]{2,1,0:T(8,128)(2,1)S(1)} %pad_maximum_fusion.1.rest_0_), channel_id=1, source_target_pairs={{0,1},{1,0},{2,3},{3,2},{4,5},{5,4},{6,7},{7,6},{8,9},{9,8},{10,11... | collective-permute-start | bytes 786440 | tf_op jit(solution)/shard_map/ppermute | solution.py:47
  72.4 5.6 %collective-permute-start.23 = (bf16[8,128,128]{2,1,0:T(8,128)(2,1)S(1)}, bf16[8,128,128]{2,1,0:T(8,128)(2,1)S(1)}, u32[]{:S(2)}, u32[]{:S(2)}) collective-permute-start(bf16[8,128,128]{2,1,0:T(8,128)(2,1)S(1)} %constant_dynamic-update-slice_fusion.3.rest_1_), channel_id=1, source_target_pairs={{0,6},{1,25},{2,0},{3,27},{4,2},{5,29},{6,4},{7,31},{8,14},{9,1},{... | collective-permute-start | bytes 786440 | tf_op jit(solution)/shard_map/ppermute | solution.py:47
  74.1 6.7 %collective-permute-start.25 = (bf16[8,128,128]{2,1,0:T(8,128)(2,1)S(1)}, bf16[8,128,128]{2,1,0:T(8,128)(2,1)S(1)}, u32[]{:S(2)}, u32[]{:S(2)}) collective-permute-start(bf16[8,128,128]{2,1,0:T(8,128)(2,1)S(1)} %constant_dynamic-update-slice_fusion.3.rest_1_), channel_id=1, source_target_pairs={{0,2},{1,9},{2,4},{3,11},{4,6},{5,13},{6,0},{7,15},{8,10},{9,17},{... | collective-permute-start | bytes 786440 | tf_op jit(solution)/shard_map/ppermute | solution.py:47
  74.4 7.0 %collective-permute-start.27 = (bf16[8,128,128]{2,1,0:T(8,128)(2,1)S(1)}, bf16[8,128,128]{2,1,0:T(8,128)(2,1)S(1)}, u32[]{:S(2)}, u32[]{:S(2)}) collective-permute-start(bf16[8,128,128]{2,1,0:T(8,128)(2,1)S(1)} %constant_dynamic-update-slice_fusion.3.rest_1_), channel_id=1, source_target_pairs={{0,1},{1,0},{2,3},{3,2},{4,5},{5,4},{6,7},{7,6},{8,9},{9,8},{10,11... | collective-permute-start | bytes 786440 | tf_op jit(solution)/shard_map/ppermute | solution.py:47
  77.1 4.9 %collective-permute-start.28 = (bf16[8,128,128]{2,1,0:T(8,128)(2,1)S(1)}, bf16[8,128,128]{2,1,0:T(8,128)(2,1)S(1)}, u32[]{:S(2)}, u32[]{:S(2)}) collective-permute-start(bf16[8,128,128]{2,1,0:T(8,128)(2,1)S(1)} %collective-permute-done.22.rest_2_), channel_id=1, source_target_pairs={{0,1},{1,0},{2,3},{3,2},{4,5},{5,4},{6,7},{7,6},{8,9},{9,8},{10,11... | collective-permute-start | bytes 786440 | tf_op jit(solution)/shard_map/ppermute | solution.py:47
  78.0 6.1 %collective-permute-start.30 = (bf16[8,128,128]{2,1,0:T(8,128)(2,1)S(1)}, bf16[8,128,128]{2,1,0:T(8,128)(2,1)S(1)}, u32[]{:S(2)}, u32[]{:S(2)}) collective-permute-start(bf16[8,128,128]{2,1,0:T(8,128)(2,1)S(1)} %collective-permute-done.24.rest_4_), channel_id=1, source_target_pairs={{0,1},{1,0},{2,3},{3,2},{4,5},{5,4},{6,7},{7,6},{8,9},{9,8},{10,11... | collective-permute-start | bytes 786440 | tf_op jit(solution)/shard_map/ppermute | solution.py:47
  78.0 6.1 %collective-permute-start.29 = (bf16[8,128,128]{2,1,0:T(8,128)(2,1)S(1)}, bf16[8,128,128]{2,1,0:T(8,128)(2,1)S(1)}, u32[]{:S(2)}, u32[]{:S(2)}) collective-permute-start(bf16[8,128,128]{2,1,0:T(8,128)(2,1)S(1)} %collective-permute-done.23.rest_3_), channel_id=1, source_target_pairs={{0,1},{1,0},{2,3},{3,2},{4,5},{5,4},{6,7},{7,6},{8,9},{9,8},{10,11... | collective-permute-start | bytes 786440 | tf_op jit(solution)/shard_map/ppermute | solution.py:47
  80.8 3.3 %collective-permute-start.31 = (bf16[8,128,128]{2,1,0:T(8,128)(2,1)S(1)}, bf16[8,128,128]{2,1,0:T(8,128)(2,1)S(1)}, u32[]{:S(2)}, u32[]{:S(2)}) collective-permute-start(bf16[8,128,128]{2,1,0:T(8,128)(2,1)S(1)} %collective-permute-done.25.rest_5_), channel_id=1, source_target_pairs={{0,1},{1,0},{2,3},{3,2},{4,5},{5,4},{6,7},{7,6},{8,9},{9,8},{10,11... | collective-permute-start | bytes 786440 | tf_op jit(solution)/shard_map/ppermute | solution.py:47
  81.4 6.7 %collective-permute-start.32 = (bf16[8,128,128]{2,1,0:T(8,128)(2,1)S(1)}, bf16[8,128,128]{2,1,0:T(8,128)(2,1)S(1)}, u32[]{:S(2)}, u32[]{:S(2)}) collective-permute-start(bf16[8,128,128]{2,1,0:T(8,128)(2,1)S(1)} %collective-permute-done.24.rest_4_), channel_id=1, source_target_pairs={{0,2},{1,9},{2,4},{3,11},{4,6},{5,13},{6,0},{7,15},{8,10},{9,17},{... | collective-permute-start | bytes 786440 | tf_op jit(solution)/shard_map/ppermute | solution.py:47
  82.0 6.1 %collective-permute-start.33 = (bf16[8,128,128]{2,1,0:T(8,128)(2,1)S(1)}, bf16[8,128,128]{2,1,0:T(8,128)(2,1)S(1)}, u32[]{:S(2)}, u32[]{:S(2)}) collective-permute-start(bf16[8,128,128]{2,1,0:T(8,128)(2,1)S(1)} %collective-permute-done.23.rest_3_), channel_id=1, source_target_pairs={{0,6},{1,25},{2,0},{3,27},{4,2},{5,29},{6,4},{7,31},{8,14},{9,1},{... | collective-permute-start | bytes 786440 | tf_op jit(solution)/shard_map/ppermute | solution.py:47
  88.1 2.0 %collective-permute-start.34 = (bf16[8,128,128]{2,1,0:T(8,128)(2,1)S(1)}, bf16[8,128,128]{2,1,0:T(8,128)(2,1)S(1)}, u32[]{:S(2)}, u32[]{:S(2)}) collective-permute-start(bf16[8,128,128]{2,1,0:T(8,128)(2,1)S(1)} %collective-permute-done.32.rest_0_), channel_id=1, source_target_pairs={{0,1},{1,0},{2,3},{3,2},{4,5},{5,4},{6,7},{7,6},{8,9},{9,8},{10,11... | collective-permute-start | bytes 786440 | tf_op jit(solution)/shard_map/ppermute | solution.py:47
  89.0 1.5 %collective-permute-start.35 = (bf16[8,128,128]{2,1,0:T(8,128)(2,1)S(1)}, bf16[8,128,128]{2,1,0:T(8,128)(2,1)S(1)}, u32[]{:S(2)}, u32[]{:S(2)}) collective-permute-start(bf16[8,128,128]{2,1,0:T(8,128)(2,1)S(1)} %collective-permute-done.33.rest_1_), channel_id=1, source_target_pairs={{0,1},{1,0},{2,3},{3,2},{4,5},{5,4},{6,7},{7,6},{8,9},{9,8},{10,11... | collective-permute-start | bytes 786440 | tf_op jit(solution)/shard_map/ppermute | solution.py:47
  (1 other events, 0.7 us)

commit v3 on v2

--- a/solution.py
+++ b/solution.py
@@ -13,9 +13,8 @@
 TILE = 128
 JOIN = 8
 WIDE = 4
-ROOM = PAIRS + JOIN
-LISTS = 2 * OWN
-GROUPS = PAIRS // JOIN + OWN + WIDE
+LATE_GROUP = 72
+GROUPS = 2 * LATE_GROUP
 
 LIMIT = pltpu.CompilerParams(vmem_limit_bytes=16 << 20)
 SMEM = pl.BlockSpec(memory_space=pltpu.SMEM)
@@ -41,6 +40,7 @@
 
 
 SWAP = moves(lambda x, y, c: (x, y, 1 - c))
+SAME_CORE = [[device_of(x, y, c) for x in range(SIDE) for y in range(SIDE)] for c in range(2)]
 
 
 def send(values, pairs):
@@ -52,21 +52,19 @@
 
 
 def spread(coeff, fill_first, fill_second):
-    half = OWN // 2
+    first2 = send(coeff, along_first(2))
     first3 = send(coeff, along_first(1))
     first1 = send(coeff, along_first(-1))
-    first3, first1 = together((first3, first1), fill_first)
-    first2a = send(first3[:half], along_first(1))
-    first2b = send(first1[half:], along_first(-1))
-    first2a, first2b = together((first2a, first2b), fill_second)
+    first2, first3, first1 = together((first2, first3, first1), *fill_first)
     low = jnp.concatenate([coeff, first1])
-    high = jnp.concatenate([first2a, first2b, first3])
+    high = jnp.concatenate([first2, first3])
     low3 = send(low, along_second(1))
     high1 = send(high, along_second(-1))
     high3 = send(high, along_second(1))
     low1 = send(low, along_second(-1))
     low2 = send(low3, along_second(1))
     high2 = send(high1, along_second(-1))
+    high3, low1 = together((high3, low1), *fill_second)
     near = (low, high, low1, high1, low3, high3)
     far = (low2, high2)
     return near, tuple(send(piece, SWAP) for piece in near), far
@@ -83,81 +81,107 @@
 LATE_AT = FAR_AT + tuple(place + SOURCES // 2 for place in FAR_AT)
 
 
-def source_table(need):
-    me = lax.axis_index("dev")
-    peer = jnp.arange(2 * SIDE * SIDE, dtype=jnp.int32)
+def ones_where(mask):
+    return jnp.where(mask, 1.0, 0.0).astype(jnp.bfloat16)
+
+
+def counted(shape, axis):
+    return lax.broadcasted_iota(jnp.int32, shape, axis)
+
+
+def dot(left, right, contract=((1,), (0,))):
+    return lax.dot_general(left, right, (contract, ((), ())), preferred_element_type=jnp.float32)
+
+
+def plan_kernel(me, count, need, src, tgt, blk, blocks, words, groups, sizes, near, sem):
+    copy = pltpu.make_async_copy(blocks, near, sem)
+    copy.start()
+    source = src[...]
+    peer, request = source >> 2, source & 3
+    from_peer = ones_where(counted((need.shape[0], PAIRS), 0) == peer)
+    choices = dot(need[...].astype(jnp.float32).astype(jnp.bfloat16), from_peer, ((0,), (0,)))
+    sphere = jnp.zeros((1, PAIRS), jnp.float32)
+    for k in range(OWN):
+        sphere = jnp.where(request == k, choices[k : k + 1, :], sphere)
     core = peer & 1
-    dx = ((peer >> 3) - (me >> 3)) & 3
-    dy = (((peer >> 1) & 3) - ((me >> 1) & 3)) & 3
+    dx = ((peer >> 3) - (me[0] >> 3)) & 3
+    dy = (((peer >> 1) & 3) - ((me[0] >> 1) & 3)) & 3
     first = jnp.where(core == 0, dx, dy)
     second = jnp.where(core == 0, dy, dx)
-    slot = ((core ^ (me & 1)) << 6) + (second << 4) + (first << 2)
-    late = jnp.where(second == 2, 1 << 20, 0)
-    return ((slot + late)[:, None] + need).reshape(-1)
-
-
-def plan_kernel(table, src, operand, count, lists, groups, sizes, filled):
-    for k in range(LISTS):
-        filled[k] = k * ROOM
-
-    def place(p, carry):
-        word = table[src[p]]
-        tail = operand[p]
-        which = (tail & 3) | (word >> 18)
-        at = filled[which]
-        lists[at] = word + (tail & 0x7F00)
-        filled[which] = at + 1
-        return carry
-
-    lax.fori_loop(0, count[0], place, 0)
-    for u in range(JOIN):
-        lists[LISTS * ROOM + u] = SOURCES
-    for part in range(2):
-        total = jnp.int32(0)
-        for k in range(part * OWN, (part + 1) * OWN):
-            end = filled[k]
-            for u in range(JOIN):
-                lists[end + u] = SOURCES
-            several = (end - k * ROOM + (JOIN - 1)) // JOIN
-
-            def enter(g, carry, k=k, part=part, total=total):
-                groups[part * GROUPS + total + g] = (k * ROOM + g * JOIN) | ((k % OWN) << 16)
-                return carry
-
-            lax.fori_loop(0, several, enter, 0)
-            total = total + several
-        for w in range(WIDE):
-            groups[part * GROUPS + total + w] = LISTS * ROOM
-        sizes[part] = (total + (WIDE - 1)) // WIDE
-
-
-def plan(table, src, operand, count):
-    return pl.pallas_call(
+    slot = ((core ^ (me[0] & 1)) << 6) + (second << 4) + (first << 2) + sphere.astype(jnp.int32)
+    which = tgt[...] + jnp.where(second == 2, OWN, 0)
+    live = counted((1, PAIRS), 1) < count[0]
+
+    rows = 16
+    row = counted((rows, PAIRS), 0)
+    member = (row == which) & live
+    ahead = ones_where(counted((PAIRS, PAIRS), 0) < counted((PAIRS, PAIRS), 1))
+    rank = dot(ones_where(member), ahead)
+    many = jnp.sum(jnp.where(member, 1.0, 0.0), axis=1, keepdims=True).astype(jnp.int32)
+    several = (many + (JOIN - 1)) // JOIN
+    r, c = counted((rows, rows), 0), counted((rows, rows), 1)
+    below = ones_where((c < r) & ((c < OWN) == (r < OWN)))
+    wide = jnp.broadcast_to(several, (rows, TILE)).astype(jnp.float32).astype(jnp.bfloat16)
+    begin = dot(below, wide)[:, :1].astype(jnp.int32)
+    begin = begin + jnp.where(counted((rows, 1), 0) < OWN, 0, LATE_GROUP)
+
+    at = rank.astype(jnp.int32) + begin * JOIN
+    at = jnp.sum(jnp.where(member, at, 0).astype(jnp.float32), axis=0, keepdims=True)
+    at = jnp.where(live, at.astype(jnp.int32), -1)
+    placed = ones_where(counted((GROUPS * JOIN, PAIRS), 0) == at)
+    values = jnp.where(row == 0, slot - SOURCES, jnp.where(row == 1, blk[...], 0))
+    values = values.astype(jnp.float32).astype(jnp.bfloat16)
+    listed = dot(values, placed, ((1,), (1,))).astype(jnp.int32)
+    words[...] = (listed[0:1, :] + SOURCES) | (listed[1:2, :] << 8)
+
+    group = counted((rows, 2 * TILE), 1)
+    passed = (group >= begin) & (counted((rows, 2 * TILE), 0) < 2 * OWN)
+    owner = jnp.sum(jnp.where(passed, 1.0, 0.0), axis=0, keepdims=True).astype(jnp.int32) - 1
+    groups[...] = (group[0:1, :] * JOIN) | ((owner & (OWN - 1)) << 16)
+
+    lane = counted((1, TILE), 1)
+    part = counted((rows, 1), 0) // OWN
+    steps = jnp.zeros((1, TILE), jnp.int32)
+    for k in range(2):
+        total = jnp.sum(jnp.where(part == k, several, 0).astype(jnp.float32), axis=0, keepdims=True)
+        needed = (total.astype(jnp.int32) + (WIDE - 1)) // WIDE
+        steps = jnp.where(lane == k, needed, steps)
+    sizes[...] = steps
+    copy.wait()
+
+
+def plan(need, src, tgt, blk, count, blocks):
+    me = lax.axis_index("dev").reshape(1)
+    words, groups, sizes, near = pl.pallas_call(
         plan_kernel,
         out_shape=(
-            jax.ShapeDtypeStruct(((LISTS + 1) * ROOM,), jnp.int32),
-            jax.ShapeDtypeStruct((2 * GROUPS,), jnp.int32),
-            jax.ShapeDtypeStruct((2,), jnp.int32),
-        ),
-        in_specs=[SMEM] * 4,
-        out_specs=(SMEM,) * 3,
-        scratch_shapes=[pltpu.SMEM((LISTS,), jnp.int32)],
-        cost_estimate=pl.CostEstimate(flops=5_000_000_000, bytes_accessed=16384, transcendentals=0),
-        compiler_params=LIMIT,
+            jax.ShapeDtypeStruct((1, GROUPS * JOIN), jnp.int32),
+            jax.ShapeDtypeStruct((1, 2 * TILE), jnp.int32),
+            jax.ShapeDtypeStruct((1, TILE), jnp.int32),
+            jax.ShapeDtypeStruct(blocks.shape, blocks.dtype),
+        ),
+        in_specs=[SMEM] * 2 + [VMEM] * 4 + [ANY],
+        out_specs=(VMEM,) * 4,
+        scratch_shapes=[pltpu.SemaphoreType.DMA],
+        compiler_params=LIMIT,
+        cost_estimate=pl.CostEstimate(
+            flops=1_000_000_000, bytes_accessed=8_000_000, transcendentals=0
+        ),
         name="plan",
-    )(table, src, operand, count)
+    )(me, count, need, src, tgt, blk, blocks)
+    return (words, groups, sizes), near
 
 
 def add_pairs(part, lists, groups, sizes, blocks, sources, total):
     def step(i, carry):
         made = []
         for w in range(WIDE):
-            group = groups[part * GROUPS + i * WIDE + w]
+            group = groups[0, part * LATE_GROUP + i * WIDE + w]
             base = group & 0xFFFF
             left, right = [], []
             for u in range(JOIN):
-                word = lists[base + u]
-                left.append(blocks[(word >> 8) & 0x7F])
+                word = lists[0, base + u]
+                left.append(blocks[word >> 8])
                 right.append(sources[word & 0xFF])
             product = jnp.dot(
                 jnp.concatenate(left, axis=1),
@@ -169,7 +193,7 @@
             total[target] += product
         return carry
 
-    lax.fori_loop(0, sizes[part], step, 0)
+    lax.fori_loop(0, sizes[0, part], step, 0)
 
 
 def fetch(pieces, places, sources, sems):
@@ -207,27 +231,24 @@
 FAR_ROWS = 256
 
 
-def last_kernel(lists, groups, sizes, blocks, before, tmatrix, weighted_a, weighted_b, *rest):
-    pieces, (far, sources, total, coeff, sems) = rest[:-5], rest[-5:]
-    fetch(pieces, LATE_AT, sources, sems)
-    total[...] = before[...]
-    add_pairs(1, lists, groups, sizes, blocks, sources, total)
-    for t in range(OWN):
-        coeff[pl.ds(t * TILE, TILE), :] = finish(tmatrix, total, t)
-
-    for n, weighted in enumerate((weighted_a, weighted_b)):
-        size = weighted.shape[0]
-
-        def chunk(i, carry, weighted=weighted, first=n * size):
-            start = pl.multiple_of(i * FAR_ROWS, FAR_ROWS)
-            far[pl.ds(first + start, FAR_ROWS), :] = jnp.dot(
-                weighted[pl.ds(start, FAR_ROWS), :],
-                coeff[...],
-                preferred_element_type=jnp.float32,
-            )
-            return carry
-
-        lax.fori_loop(0, size // FAR_ROWS, chunk, 0)
+def far_kernel(mine, other, coeff, arrived, far):
+    def chunk(i, carry):
+        rows = pl.ds(pl.multiple_of(i * FAR_ROWS, FAR_ROWS), FAR_ROWS)
+        far[rows, :] = dot(mine[rows, :], coeff[...]) + dot(other[rows, :], arrived[...])
+        return carry
+
+    lax.fori_loop(0, far.shape[0] // FAR_ROWS, chunk, 0)
+
+
+def far_field(mine, other, coeff, arrived):
+    return pl.pallas_call(
+        far_kernel,
+        out_shape=jax.ShapeDtypeStruct((mine.shape[0], TILE), jnp.float32),
+        in_specs=[VMEM] * 4,
+        out_specs=VMEM,
+        compiler_params=LIMIT,
+        name="far",
+    )(mine, other, coeff.reshape(-1, TILE), arrived.reshape(-1, TILE))
 
 
 def table_kernel(phases, harmonics, table):
@@ -317,24 +338,6 @@
         compiler_params=LIMIT,
         name="late",
     )(*made, blocks, before, tmatrix, *pieces)
-
-
-def last_pairs(made, blocks, before, tmatrix, weighted, pieces):
-    rows = sum(part.shape[0] for part in weighted)
-    return pl.pallas_call(
-        last_kernel,
-        out_shape=jax.ShapeDtypeStruct((rows, TILE), jnp.float32),
-        in_specs=[SMEM] * 3 + [VMEM] * 5 + [ANY] * len(pieces),
-        out_specs=VMEM,
-        scratch_shapes=[
-            SCRATCH,
-            pltpu.VMEM(TOTAL, jnp.float32),
-            pltpu.VMEM((OWN * TILE, TILE), jnp.bfloat16),
-            pltpu.SemaphoreType.DMA((len(pieces),)),
-        ],
-        compiler_params=LIMIT,
-        name="last",
-    )(*made, blocks, before, tmatrix, *weighted, *pieces)
 
 
 def apply_tmatrix(tmatrix, field):
@@ -357,23 +360,30 @@
 ):
     n_grp, n_dev = lax.axis_size("grp"), lax.axis_size("dev")
     coeff = apply_tmatrix(tmatrix, incident)
-    made = plan(source_table(need[0]), pair_src[0], pair_tgt[0] | (pair_blk[0] << 8), pair_count)
+    made, blocks = plan(need[0], pair_src, pair_tgt, pair_blk, pair_count, blocks)
     table = make_table(factor, harmonics)
-    near, other, far = spread(coeff, table, made)
+
+    rows = owner.shape[0] // (n_grp * n_dev)
+    order = owner.reshape(n_grp, n_dev // 2, 2, rows).transpose(2, 1, 0, 3).reshape(2, -1)
+    core = lax.axis_index("dev") % 2
+    order_mine = jnp.where(core == 0, order[0], order[1])
+    order_other = jnp.where(core == 0, order[1], order[0])
+    for_other = in_order(order_other, table)
+    near, other, far = spread(coeff, (made, table), (for_other,))
     before = early_pairs(made, blocks, incident, near + other)
     coeff = late_pairs(made, blocks, before, tmatrix, swapped(far, before))
 
-    rows = owner.shape[0] // (n_grp * n_dev)
-    order = owner.reshape(n_grp, n_dev, rows).transpose(1, 0, 2).reshape(2, -1)
-    weighted = tuple(in_order(part, table) for part in order)
-    near, other, far = spread(coeff, weighted[0], weighted[1])
+    mine = in_order(order_mine, table)
+    near, other, far = spread(coeff, (mine,), ())
+    weighted_other = send(for_other, SWAP)
     before = early_pairs(made, blocks, incident, near + other)
-    far = last_pairs(made, blocks, before, tmatrix, weighted, swapped(far, before))
-
-    far = far.reshape(n_dev, n_grp * rows, TILE)
-    far = lax.all_to_all(far, "dev", 0, 0).sum(axis=0)
-    far = far.reshape(n_grp, rows, TILE)
-    return lax.all_to_all(far, "grp", 0, 0).sum(axis=0)
+    coeff = late_pairs(made, blocks, before, tmatrix, swapped(far, before))
+
+    amplitude = far_field(mine, weighted_other, coeff, send(coeff, SWAP))
+    amplitude = amplitude.reshape(n_dev // 2, n_grp * rows, TILE)
+    amplitude = lax.all_to_all(amplitude, "dev", 0, 0, axis_index_groups=SAME_CORE).sum(axis=0)
+    amplitude = amplitude.reshape(n_grp, rows, TILE)
+    return lax.all_to_all(amplitude, "grp", 0, 0).sum(axis=0)
 
 
 def solution(mesh):

time: 135 us -> 117 us (0.87)
  starting transfers between devices: 47.7 us -> 38.3 us
  Pallas kernels: 27.8 us -> 19 us
  blocking collectives: 37.5 us -> 31.7 us
  waiting for transfers between devices: 6.24 us -> 11.1 us
  local copies, waits for them, and re-layouts: 10.1 us -> 12.3 us
    ppermute x36, starting transfers between devices: 47.7 us -> 38.3 us  [send(): return lax.ppermute(values, 'dev', pairs)]
    pallas_call x2, Pallas kernels: 8.83 us -> 2.27 us  [the longest x1 1.14 us: far_field(): pl.pallas_call(far_kernel, out_shape=jax.ShapeDtypeStruct((mine.shape[0],...]
    all_to_all x2, blocking collectives: 37.5 us -> 31.7 us  [the longest x1 16.9 us: body(): lax.all_to_all(amplitude, 'dev', 0, 0, axis_index_groups=SAME_CORE)]
    ppermute x36, waiting for transfers between devices: 6.24 us -> 11.1 us  [send(): return lax.ppermute(values, 'dev', pairs)]
    pallas_call x2, Pallas kernels: 8.78 us -> 5.47 us  [early_pairs(): pl.pallas_call(early_kernel, out_shape=jax.ShapeDtypeStruct(TOTAL, jnp.fl...]
    unnamed x32 -> x35, local copies, waits for them, and re-layouts: 8.64 us -> 11.5 us
    pallas_call x1 -> x2, Pallas kernels: 2.53 us -> 3.62 us  [late_pairs(): pl.pallas_call(late_kernel, out_shape=jax.ShapeDtypeStruct(TOTAL, jnp.bfl...]
  transfers between devices with their start and end apart: 36 -> 36, of which waited for: 8 -> 12; matrix products, arithmetic and copies ran while one was open for 3% -> 2% of each run, Pallas kernels for 16% -> 14%
where the time goes in v3:
time: 117 us; the launch traced here: 115 us
  starting transfers between devices  38.3 us (33%)
  blocking collectives  31.7 us (27%)
  Pallas kernels  19 us (16%)
  local copies, waits for them, and re-layouts  12.3 us (11%)
  waiting for transfers between devices  11.1 us (9%)
  matrix products  1.19 us (1%)
    ppermute x36, starting transfers between devices, send(): return lax.ppermute(values, 'dev', pairs)  38.3 us
    all_to_all x1, blocking collectives, body(): lax.all_to_all(amplitude, 'dev', 0, 0, axis_index_groups=SAME_CORE)  16.9 us
    all_to_all x1, blocking collectives, body(): return lax.all_to_all(amplitude, 'grp', 0, 0).sum(axis=0)  14.8 us
    unnamed x35, local copies, waits for them, and re-layouts  11.5 us
    ppermute x36, waiting for transfers between devices, send(): return lax.ppermute(values, 'dev', pairs)  11.1 us
    pallas_call x2, Pallas kernels, in_order(): pl.pallas_call(order_kernel, out_shape=jax.ShapeDtypeStruct((order.shape[...  5.97 us
    pallas_call x2, Pallas kernels, early_pairs(): pl.pallas_call(early_kernel, out_shape=jax.ShapeDtypeStruct(TOTAL, jnp.fl...  5.47 us
    pallas_call x2, Pallas kernels, late_pairs(): pl.pallas_call(late_kernel, out_shape=jax.ShapeDtypeStruct(TOTAL, jnp.bfl...  3.62 us
  transfers between devices with their start and end apart: 36, of which 12 were waited for; matrix products, arithmetic and copies ran while one was open for 2% of the time, Pallas kernels for 14%

profile of v3, /device:TPU:1, one launch (start us, length us, event | category | flops | bytes accessed | tf_op | source)
XLA Modules:
  0.0 115.3 jit_solution(6086557230580268768)
XLA Ops:
  0.0 1.2 %convolution_convert_fusion = bf16[4,128,128]{2,1,0:T(8,128)(2,1)S(1)} fusion(bf16[4,128,128]{2,1,0:T(8,128)(2,1)} %tmatrix.3, bf16[4,128,128]{2,1,0:T(8,128)(2,1)} %incident.3), kind=kOutput, calls=%fused_computation | convolution fusion | flops 16842752 | bytes 393216 | tf_op jit(solution)/shard_map/skl,slq->skq/dot_general | solution.py:344
  1.2 3.8 %collective-permute-start.1 = (bf16[4,128,128]{2,1,0:T(8,128)(2,1)S(1)}, bf16[4,128,128]{2,1,0:T(8,128)(2,1)S(1)}, u32[]{:S(2)}, u32[]{:S(2)}) collective-permute-start(bf16[4,128,128]{2,1,0:T(8,128)(2,1)S(1)} %convolution_convert_fusion), channel_id=1, source_target_pairs={{0,16},{1,5},{2,18},{3,7},{4,20},{5,1},{6,22},{7,3},{8,24},{9,13},... | collective-permute-start | bytes 393224 | tf_op jit(solution)/shard_map/ppermute | solution.py:47
  5.4 2.3 %collective-permute-start.3 = (bf16[4,128,128]{2,1,0:T(8,128)(2,1)S(1)}, bf16[4,128,128]{2,1,0:T(8,128)(2,1)S(1)}, u32[]{:S(2)}, u32[]{:S(2)}) collective-permute-start(bf16[4,128,128]{2,1,0:T(8,128)(2,1)S(1)} %convolution_convert_fusion), channel_id=1, source_target_pairs={{0,24},{1,7},{2,26},{3,1},{4,28},{5,3},{6,30},{7,5},{8,0},{9,15},{... | collective-permute-start | bytes 393224 | tf_op jit(solution)/shard_map/ppermute | solution.py:47
  7.7 1.1 copy.21
  8.9 1.0 copy-done.10
  9.9 1.7 %table.1 = bf16[2048,512]{1,0:T(8,128)(2,1)S(1)} custom-call(f32[2048,4]{1,0:T(8,128)S(1)} %bitcast.15, bf16[2048,128]{1,0:T(8,128)(2,1)S(1)} %copy-done.10), custom_call_target="tpu_custom_call" | custom-call | flops 1000000000 | bytes 4000000 | tf_op jit(solution)/shard_map/table/pallas_call | solution.py:281
  11.6 1.4 %copy-done.11 = bf16[2048,512]{1,0:T(8,128)(2,1)} copy-done((bf16[2048,512]{1,0:T(8,128)(2,1)}, bf16[2048,512]{1,0:T(8,128)(2,1)S(1)}, u32[]{:S(2)}) %copy-start.11) | copy-done | bytes 2097176
  13.9 2.2 %copy-done.4 = bf16[128,128,128]{2,1,0:T(8,128)(2,1)S(1)} copy-done((bf16[128,128,128]{2,1,0:T(8,128)(2,1)S(1)}, bf16[128,128,128]{2,1,0:T(8,128)(2,1)}, u32[]{:S(2)}) %copy-start.4) | copy-done | bytes 4194328
  16.1 1.1 plan.1
  17.3 2.0 %copy-done = bf16[128,128,128]{2,1,0:T(8,128)(2,1)} copy-done((bf16[128,128,128]{2,1,0:T(8,128)(2,1)}, bf16[128,128,128]{2,1,0:T(8,128)(2,1)S(1)}, u32[]{:S(2)}) %copy-start) | copy-done | bytes 4194328
  19.3 1.3 %collective-permute-start.4 = (bf16[8,128,128]{2,1,0:T(8,128)(2,1)S(1)}, bf16[8,128,128]{2,1,0:T(8,128)(2,1)S(1)}, u32[]{:S(2)}, u32[]{:S(2)}) collective-permute-start(bf16[8,128,128]{2,1,0:T(8,128)(2,1)S(1)} %constant_dynamic-update-slice_fusion.rest_1_), channel_id=1, source_target_pairs={{0,2},{1,9},{2,4},{3,11},{4,6},{5,13},{6,0},{7,15},{8,10},{9,17},{... | collective-permute-start | bytes 786440 | tf_op jit(solution)/shard_map/ppermute | solution.py:47
  20.6 1.5 %collective-permute-start.5 = (bf16[8,128,128]{2,1,0:T(8,128)(2,1)S(1)}, bf16[8,128,128]{2,1,0:T(8,128)(2,1)S(1)}, u32[]{:S(2)}, u32[]{:S(2)}) collective-permute-start(bf16[8,128,128]{2,1,0:T(8,128)(2,1)S(1)} %pad_maximum_fusion.rest_0_), channel_id=1, source_target_pairs={{0,6},{1,25},{2,0},{3,27},{4,2},{5,29},{6,4},{7,31},{8,14},{9,1},{... | collective-permute-start | bytes 786440 | tf_op jit(solution)/shard_map/ppermute | solution.py:47
  22.4 1.3 %collective-permute-start.6 = (bf16[8,128,128]{2,1,0:T(8,128)(2,1)S(1)}, bf16[8,128,128]{2,1,0:T(8,128)(2,1)S(1)}, u32[]{:S(2)}, u32[]{:S(2)}) collective-permute-start(bf16[8,128,128]{2,1,0:T(8,128)(2,1)S(1)} %constant_dynamic-update-slice_fusion.rest_1_), channel_id=1, source_target_pairs={{0,6},{1,25},{2,0},{3,27},{4,2},{5,29},{6,4},{7,31},{8,14},{9,1},{... | collective-permute-start | bytes 786440 | tf_op jit(solution)/shard_map/ppermute | solution.py:47
  23.9 2.5 %collective-permute-start.8 = (bf16[8,128,128]{2,1,0:T(8,128)(2,1)S(1)}, bf16[8,128,128]{2,1,0:T(8,128)(2,1)S(1)}, u32[]{:S(2)}, u32[]{:S(2)}) collective-permute-start(bf16[8,128,128]{2,1,0:T(8,128)(2,1)S(1)} %pad_maximum_fusion.rest_0_), channel_id=1, source_target_pairs={{0,1},{1,0},{2,3},{3,2},{4,5},{5,4},{6,7},{7,6},{8,9},{9,8},{10,11... | collective-permute-start | bytes 786440 | tf_op jit(solution)/shard_map/ppermute | solution.py:47
  26.4 1.6 %copy-done.12 = bf16[2048,512]{1,0:T(8,128)(2,1)S(1)} copy-done((bf16[2048,512]{1,0:T(8,128)(2,1)S(1)}, bf16[2048,512]{1,0:T(8,128)(2,1)}, u32[]{:S(2)}) %copy-start.12) | copy-done | bytes 2097176
  28.0 3.0 %order.3 = bf16[1024,512]{1,0:T(8,128)(2,1)S(1)} custom-call(s32[1024,1]{1,0:T(8,128)S(1)} %select_n.46.order, bf16[2048,512]{1,0:T(8,128)(2,1)S(1)} %copy-done.12), custom_call_target="tpu_custom_call" | custom-call | flops 2000000000 | bytes 4000000 | tf_op jit(solution)/shard_map/order/pallas_call | solution.py:295
  31.7 2.1 %collective-permute-start.12 = (bf16[8,128,128]{2,1,0:T(8,128)(2,1)S(1)}, bf16[8,128,128]{2,1,0:T(8,128)(2,1)S(1)}, u32[]{:S(2)}, u32[]{:S(2)}) collective-permute-start(bf16[8,128,128]{2,1,0:T(8,128)(2,1)S(1)} %collective-permute-done.7.rest_4_), channel_id=1, source_target_pairs={{0,1},{1,0},{2,3},{3,2},{4,5},{5,4},{6,7},{7,6},{8,9},{9,8},{10,11... | collective-permute-start | bytes 786440 | tf_op jit(solution)/shard_map/ppermute | solution.py:47
  33.9 2.7 %collective-permute-start.15 = (bf16[8,128,128]{2,1,0:T(8,128)(2,1)S(1)}, bf16[8,128,128]{2,1,0:T(8,128)(2,1)S(1)}, u32[]{:S(2)}, u32[]{:S(2)}) collective-permute-start(bf16[8,128,128]{2,1,0:T(8,128)(2,1)S(1)} %collective-permute-done.6.rest_3_), channel_id=1, source_target_pairs={{0,6},{1,25},{2,0},{3,27},{4,2},{5,29},{6,4},{7,31},{8,14},{9,1},{... | collective-permute-start | bytes 786440 | tf_op jit(solution)/shard_map/ppermute | solution.py:47
  36.6 2.7 %early.2.before = f32[4,128,128]{2,1,0:T(8,128)S(1)} custom-call(s32[1,1152]{1,0:T(1,128)S(1)} %get-tuple-element.23.lists, s32[1,256]{1,0:T(1,128)S(1)} %get-tuple-element.24.groups, s32[1,128]{1,0:T(1,128)S(1)} %get-tuple-element.25.sizes, bf16[128,128,128]{2,1,0:T(8,128)(2,1)S(1)} %copy-done.1, bf16[4,128,128]{2,1,0:T(8,128)(2,1)S(1)} %copy-done.5, ...), custom_call_target="tpu_custom_call" | custom-call | flops 2000000000 | bytes 8000000 | tf_op jit(solution)/shard_map/early/pallas_call | solution.py:313
  39.3 1.3 %collective-permute-done.14.rest_0_ = bf16[8,128,128]{2,1,0:T(8,128)(2,1)S(1)} collective-permute-done((bf16[8,128,128]{2,1,0:T(8,128)(2,1)S(1)}, bf16[8,128,128]{2,1,0:T(8,128)(2,1)S(1)}, u32[]{:S(2)}, u32[]{:S(2)}) %collective-permute-start.14) | collective-permute-done | bytes 262176 | tf_op jit(solution)/shard_map/ppermute | solution.py:47
  40.6 1.3 %collective-permute-start.16 = (bf16[8,128,128]{2,1,0:T(8,128)(2,1)S(1)}, bf16[8,128,128]{2,1,0:T(8,128)(2,1)S(1)}, u32[]{:S(2)}, u32[]{:S(2)}) collective-permute-start(bf16[8,128,128]{2,1,0:T(8,128)(2,1)S(1)} %collective-permute-done.14.rest_0_), channel_id=1, source_target_pairs={{0,1},{1,0},{2,3},{3,2},{4,5},{5,4},{6,7},{7,6},{8,9},{9,8},{10,11... | collective-permute-start | bytes 786440 | tf_op jit(solution)/shard_map/ppermute | solution.py:47
  42.1 0.9 collective-permute-done.16.rest_2_
  43.4 2.2 %copy-done.2 = bf16[128,128,128]{2,1,0:T(8,128)(2,1)S(1)} copy-done((bf16[128,128,128]{2,1,0:T(8,128)(2,1)S(1)}, bf16[128,128,128]{2,1,0:T(8,128)(2,1)}, u32[]{:S(2)}) %copy-start.2) | copy-done | bytes 4194328
  45.6 1.8 %late.2 = bf16[4,128,128]{2,1,0:T(8,128)(2,1)S(1)} custom-call(s32[1,1152]{1,0:T(1,128)S(1)} %get-tuple-element.23.lists, s32[1,256]{1,0:T(1,128)S(1)} %get-tuple-element.24.groups, s32[1,128]{1,0:T(1,128)S(1)} %get-tuple-element.25.sizes, bf16[128,128,128]{2,1,0:T(8,128)(2,1)S(1)} %copy-done.2, f32[4,128,128]{2,1,0:T(8,128)S(1)} %early.2.before, ...), custom_call_target="tpu_custom_call" | custom-call | tf_op jit(solution)/shard_map/late/pallas_call | solution.py:328
  47.4 1.5 %collective-permute-start.18 = (bf16[4,128,128]{2,1,0:T(8,128)(2,1)S(1)}, bf16[4,128,128]{2,1,0:T(8,128)(2,1)S(1)}, u32[]{:S(2)}, u32[]{:S(2)}) collective-permute-start(bf16[4,128,128]{2,1,0:T(8,128)(2,1)S(1)} %late.2), channel_id=1, source_target_pairs={{0,16},{1,5},{2,18},{3,7},{4,20},{5,1},{6,22},{7,3},{8,24},{9,13},... | collective-permute-start | bytes 393224 | tf_op jit(solution)/shard_map/ppermute | solution.py:47
  49.0 3.4 %collective-permute-start.19 = (bf16[4,128,128]{2,1,0:T(8,128)(2,1)S(1)}, bf16[4,128,128]{2,1,0:T(8,128)(2,1)S(1)}, u32[]{:S(2)}, u32[]{:S(2)}) collective-permute-start(bf16[4,128,128]{2,1,0:T(8,128)(2,1)S(1)} %late.2), channel_id=1, source_target_pairs={{0,8},{1,3},{2,10},{3,5},{4,12},{5,7},{6,14},{7,1},{8,16},{9,11},{... | collective-permute-start | bytes 393224 | tf_op jit(solution)/shard_map/ppermute | solution.py:47
  52.3 3.0 %order.2.mine = bf16[1024,512]{1,0:T(8,128)(2,1)S(1)} custom-call(s32[1024,1]{1,0:T(8,128)S(1)} %select_n.45.order, bf16[2048,512]{1,0:T(8,128)(2,1)S(1)} %copy-done.13), custom_call_target="tpu_custom_call" | custom-call | flops 2000000000 | bytes 4000000 | tf_op jit(solution)/shard_map/order/pallas_call | solution.py:295
  55.4 0.8 collective-permute-done.20
  56.3 2.7 %collective-permute-start.22 = (bf16[8,128,128]{2,1,0:T(8,128)(2,1)S(1)}, bf16[8,128,128]{2,1,0:T(8,128)(2,1)S(1)}, u32[]{:S(2)}, u32[]{:S(2)}) collective-permute-start(bf16[8,128,128]{2,1,0:T(8,128)(2,1)S(1)} %pad_maximum_fusion.1.rest_0_), channel_id=1, source_target_pairs={{0,6},{1,25},{2,0},{3,27},{4,2},{5,29},{6,4},{7,31},{8,14},{9,1},{... | collective-permute-start | bytes 786440 | tf_op jit(solution)/shard_map/ppermute | solution.py:47
  59.2 1.4 %collective-permute-start.24 = (bf16[8,128,128]{2,1,0:T(8,128)(2,1)S(1)}, bf16[8,128,128]{2,1,0:T(8,128)(2,1)S(1)}, u32[]{:S(2)}, u32[]{:S(2)}) collective-permute-start(bf16[8,128,128]{2,1,0:T(8,128)(2,1)S(1)} %pad_maximum_fusion.1.rest_0_), channel_id=1, source_target_pairs={{0,2},{1,9},{2,4},{3,11},{4,6},{5,13},{6,0},{7,15},{8,10},{9,17},{... | collective-permute-start | bytes 786440 | tf_op jit(solution)/shard_map/ppermute | solution.py:47
  60.5 0.5 collective-permute-start.25
  61.1 1.8 %collective-permute-done.21.rest_5_ = bf16[8,128,128]{2,1,0:T(8,128)(2,1)S(1)} collective-permute-done((bf16[8,128,128]{2,1,0:T(8,128)(2,1)S(1)}, bf16[8,128,128]{2,1,0:T(8,128)(2,1)S(1)}, u32[]{:S(2)}, u32[]{:S(2)}) %collective-permute-start.21) | collective-permute-done | bytes 262176 | tf_op jit(solution)/shard_map/ppermute | solution.py:47
  63.4 1.8 %collective-permute-done.23.rest_3_ = bf16[8,128,128]{2,1,0:T(8,128)(2,1)S(1)} collective-permute-done((bf16[8,128,128]{2,1,0:T(8,128)(2,1)S(1)}, bf16[8,128,128]{2,1,0:T(8,128)(2,1)S(1)}, u32[]{:S(2)}, u32[]{:S(2)}) %collective-permute-start.23) | collective-permute-done | bytes 262176 | tf_op jit(solution)/shard_map/ppermute | solution.py:47
  65.2 0.6 collective-permute-start.27
  65.9 2.8 %collective-permute-start.28 = (bf16[8,128,128]{2,1,0:T(8,128)(2,1)S(1)}, bf16[8,128,128]{2,1,0:T(8,128)(2,1)S(1)}, u32[]{:S(2)}, u32[]{:S(2)}) collective-permute-start(bf16[8,128,128]{2,1,0:T(8,128)(2,1)S(1)} %collective-permute-done.23.rest_3_), channel_id=1, source_target_pairs={{0,1},{1,0},{2,3},{3,2},{4,5},{5,4},{6,7},{7,6},{8,9},{9,8},{10,11... | collective-permute-start | bytes 786440 | tf_op jit(solution)/shard_map/ppermute | solution.py:47
  68.6 0.5 collective-permute-start.30
  69.2 0.5 collective-permute-start.31
  69.8 2.0 %collective-permute-start.32 = (bf16[8,128,128]{2,1,0:T(8,128)(2,1)S(1)}, bf16[8,128,128]{2,1,0:T(8,128)(2,1)S(1)}, u32[]{:S(2)}, u32[]{:S(2)}) collective-permute-start(bf16[8,128,128]{2,1,0:T(8,128)(2,1)S(1)} %collective-permute-done.23.rest_3_), channel_id=1, source_target_pairs={{0,6},{1,25},{2,0},{3,27},{4,2},{5,29},{6,4},{7,31},{8,14},{9,1},{... | collective-permute-start | bytes 786440 | tf_op jit(solution)/shard_map/ppermute | solution.py:47
  71.8 2.7 %early.3.before = f32[4,128,128]{2,1,0:T(8,128)S(1)} custom-call(s32[1,1152]{1,0:T(1,128)S(1)} %get-tuple-element.23.lists, s32[1,256]{1,0:T(1,128)S(1)} %get-tuple-element.24.groups, s32[1,128]{1,0:T(1,128)S(1)} %get-tuple-element.25.sizes, bf16[128,128,128]{2,1,0:T(8,128)(2,1)S(1)} %copy-done.3, bf16[4,128,128]{2,1,0:T(8,128)(2,1)S(1)} %copy-done.5, ...), custom_call_target="tpu_custom_call" | custom-call | flops 2000000000 | bytes 8000000 | tf_op jit(solution)/shard_map/early/pallas_call | solution.py:313
  74.6 1.3 %collective-permute-done.31.rest_0_ = bf16[8,128,128]{2,1,0:T(8,128)(2,1)S(1)} collective-permute-done((bf16[8,128,128]{2,1,0:T(8,128)(2,1)S(1)}, bf16[8,128,128]{2,1,0:T(8,128)(2,1)S(1)}, u32[]{:S(2)}, u32[]{:S(2)}) %collective-permute-start.31) | collective-permute-done | bytes 262176 | tf_op jit(solution)/shard_map/ppermute | solution.py:47
  75.9 1.2 %collective-permute-start.33 = (bf16[8,128,128]{2,1,0:T(8,128)(2,1)S(1)}, bf16[8,128,128]{2,1,0:T(8,128)(2,1)S(1)}, u32[]{:S(2)}, u32[]{:S(2)}) collective-permute-start(bf16[8,128,128]{2,1,0:T(8,128)(2,1)S(1)} %collective-permute-done.31.rest_0_), channel_id=1, source_target_pairs={{0,1},{1,0},{2,3},{3,2},{4,5},{5,4},{6,7},{7,6},{8,9},{9,8},{10,11... | collective-permute-start | bytes 786440 | tf_op jit(solution)/shard_map/ppermute | solution.py:47
  77.1 1.2 %collective-permute-done.33.rest_2_ = bf16[8,128,128]{2,1,0:T(8,128)(2,1)S(1)} collective-permute-done((bf16[8,128,128]{2,1,0:T(8,128)(2,1)S(1)}, bf16[8,128,128]{2,1,0:T(8,128)(2,1)S(1)}, u32[]{:S(2)}, u32[]{:S(2)}) %collective-permute-start.33) | collective-permute-done | bytes 262176 | tf_op jit(solution)/shard_map/ppermute | solution.py:47
  78.6 1.8 %late.3 = bf16[4,128,128]{2,1,0:T(8,128)(2,1)S(1)} custom-call(s32[1,1152]{1,0:T(1,128)S(1)} %get-tuple-element.23.lists, s32[1,256]{1,0:T(1,128)S(1)} %get-tuple-element.24.groups, s32[1,128]{1,0:T(1,128)S(1)} %get-tuple-element.25.sizes, bf16[128,128,128]{2,1,0:T(8,128)(2,1)S(1)} %copy-done.3, f32[4,128,128]{2,1,0:T(8,128)S(1)} %early.3.before, ...), custom_call_target="tpu_custom_call" | custom-call | tf_op jit(solution)/shard_map/late/pallas_call | solution.py:328
  80.9 1.0 collective-permute-done.35
  81.8 1.1 far.1
  83.0 16.9 %all_to_all.10 = f32[16,64,128]{2,1,0:T(8,128)S(1)} all-to-all(f32[16,64,128]{2,1,0:T(8,128)S(1)} %bitcast.14), channel_id=1, replica_groups={{0,2,4,6,8,10,12,14,16,18,20,22,24,26,28,30},{1,3,5,7,9,11,13,15,17,19,..., dimensions={0} | all-to-all | bytes 1048576 | tf_op jit(solution)/shard_map/all_to_all | solution.py:384
  99.9 14.8 %all_to_all.11 = f32[8,8,128]{2,1,0:T(8,128)S(1)} all-to-all(f32[8,8,128]{2,1,0:T(8,128)S(1)} %bitcast.19), channel_id=1, replica_groups=mesh['grp'=8,'dev'=32] {'grp'}, dimensions={0} | all-to-all | bytes 65536 | tf_op jit(solution)/shard_map/all_to_all | solution.py:386
  114.7 0.6 reduce_sum.19
  (84 shorter events, 4.6 us)
Async XLA Ops:
  0.0 12.9 %copy-start.14 = (s32[2048]{0:T(1024)S(1)}, s32[2048]{0:T(1024)}, u32[]{:S(2)}) copy-start(s32[2048]{0:T(1024)} %param.21) | copy-start | bytes 24580
  0.0 13.8 %copy-start.15 = (s32[1,32,4]{1,2,0:T(4,128)S(1)}, s32[1,32,4]{1,2,0:T(4,128)}, u32[]{:S(2)}) copy-start(s32[1,32,4]{1,2,0:T(4,128)} %param.14) | copy-start | bytes 1540
  0.0 13.9 %copy-start.7 = (s32[1,512]{1,0:T(1,128)S(1)}, s32[1,512]{1,0:T(1,128)}, u32[]{:S(2)}) copy-start(s32[1,512]{1,0:T(1,128)} %src.1) | copy-start | bytes 6148
  0.0 13.9 %copy-start.8 = (s32[1,512]{1,0:T(1,128)S(1)}, s32[1,512]{1,0:T(1,128)}, u32[]{:S(2)}) copy-start(s32[1,512]{1,0:T(1,128)} %tgt.1) | copy-start | bytes 6148
  0.0 13.9 %copy-start.9 = (s32[1,512]{1,0:T(1,128)S(1)}, s32[1,512]{1,0:T(1,128)}, u32[]{:S(2)}) copy-start(s32[1,512]{1,0:T(1,128)} %blk.1) | copy-start | bytes 6148
  1.2 18.0 %collective-permute-start.1 = (bf16[4,128,128]{2,1,0:T(8,128)(2,1)S(1)}, bf16[4,128,128]{2,1,0:T(8,128)(2,1)S(1)}, u32[]{:S(2)}, u32[]{:S(2)}) collective-permute-start(bf16[4,128,128]{2,1,0:T(8,128)(2,1)S(1)} %convolution_convert_fusion), channel_id=1, source_target_pairs={{0,16},{1,5},{2,18},{3,7},{4,20},{5,1},{6,22},{7,3},{8,24},{9,13},... | collective-permute-start | bytes 393224 | tf_op jit(solution)/shard_map/ppermute | solution.py:47
  5.0 14.2 %collective-permute-start.2 = (bf16[4,128,128]{2,1,0:T(8,128)(2,1)S(1)}, bf16[4,128,128]{2,1,0:T(8,128)(2,1)S(1)}, u32[]{:S(2)}, u32[]{:S(2)}) collective-permute-start(bf16[4,128,128]{2,1,0:T(8,128)(2,1)S(1)} %convolution_convert_fusion), channel_id=1, source_target_pairs={{0,8},{1,3},{2,10},{3,5},{4,12},{5,7},{6,14},{7,1},{8,16},{9,11},{... | collective-permute-start | bytes 393224 | tf_op jit(solution)/shard_map/ppermute | solution.py:47
  5.4 13.8 %collective-permute-start.3 = (bf16[4,128,128]{2,1,0:T(8,128)(2,1)S(1)}, bf16[4,128,128]{2,1,0:T(8,128)(2,1)S(1)}, u32[]{:S(2)}, u32[]{:S(2)}) collective-permute-start(bf16[4,128,128]{2,1,0:T(8,128)(2,1)S(1)} %convolution_convert_fusion), channel_id=1, source_target_pairs={{0,24},{1,7},{2,26},{3,1},{4,28},{5,3},{6,30},{7,5},{8,0},{9,15},{... | collective-permute-start | bytes 393224 | tf_op jit(solution)/shard_map/ppermute | solution.py:47
  13.9 2.2 %copy-start.4 = (bf16[128,128,128]{2,1,0:T(8,128)(2,1)S(1)}, bf16[128,128,128]{2,1,0:T(8,128)(2,1)}, u32[]{:S(2)}) copy-start(bf16[128,128,128]{2,1,0:T(8,128)(2,1)} %blocks.1) | copy-start | bytes 12582916
  19.3 11.7 %collective-permute-start.4 = (bf16[8,128,128]{2,1,0:T(8,128)(2,1)S(1)}, bf16[8,128,128]{2,1,0:T(8,128)(2,1)S(1)}, u32[]{:S(2)}, u32[]{:S(2)}) collective-permute-start(bf16[8,128,128]{2,1,0:T(8,128)(2,1)S(1)} %constant_dynamic-update-slice_fusion.rest_1_), channel_id=1, source_target_pairs={{0,2},{1,9},{2,4},{3,11},{4,6},{5,13},{6,0},{7,15},{8,10},{9,17},{... | collective-permute-start | bytes 786440 | tf_op jit(solution)/shard_map/ppermute | solution.py:47
  20.6 10.5 %collective-permute-start.5 = (bf16[8,128,128]{2,1,0:T(8,128)(2,1)S(1)}, bf16[8,128,128]{2,1,0:T(8,128)(2,1)S(1)}, u32[]{:S(2)}, u32[]{:S(2)}) collective-permute-start(bf16[8,128,128]{2,1,0:T(8,128)(2,1)S(1)} %pad_maximum_fusion.rest_0_), channel_id=1, source_target_pairs={{0,6},{1,25},{2,0},{3,27},{4,2},{5,29},{6,4},{7,31},{8,14},{9,1},{... | collective-permute-start | bytes 786440 | tf_op jit(solution)/shard_map/ppermute | solution.py:47
  22.1 14.5 %copy-start.5 = (bf16[4,128,128]{2,1,0:T(8,128)(2,1)S(1)}, bf16[4,128,128]{2,1,0:T(8,128)(2,1)}, u32[]{:S(2)}) copy-start(bf16[4,128,128]{2,1,0:T(8,128)(2,1)} %incident.3) | copy-start | bytes 393220
  22.4 14.2 %copy-start.1 = (bf16[128,128,128]{2,1,0:T(8,128)(2,1)S(1)}, bf16[128,128,128]{2,1,0:T(8,128)(2,1)}, u32[]{:S(2)}) copy-start(bf16[128,128,128]{2,1,0:T(8,128)(2,1)} %copy-done) | copy-start | bytes 12582916
  22.4 9.2 %collective-permute-start.6 = (bf16[8,128,128]{2,1,0:T(8,128)(2,1)S(1)}, bf16[8,128,128]{2,1,0:T(8,128)(2,1)S(1)}, u32[]{:S(2)}, u32[]{:S(2)}) collective-permute-start(bf16[8,128,128]{2,1,0:T(8,128)(2,1)S(1)} %constant_dynamic-update-slice_fusion.rest_1_), channel_id=1, source_target_pairs={{0,6},{1,25},{2,0},{3,27},{4,2},{5,29},{6,4},{7,31},{8,14},{9,1},{... | collective-permute-start | bytes 786440 | tf_op jit(solution)/shard_map/ppermute | solution.py:47
  23.7 8.0 %collective-permute-start.7 = (bf16[8,128,128]{2,1,0:T(8,128)(2,1)S(1)}, bf16[8,128,128]{2,1,0:T(8,128)(2,1)S(1)}, u32[]{:S(2)}, u32[]{:S(2)}) collective-permute-start(bf16[8,128,128]{2,1,0:T(8,128)(2,1)S(1)} %pad_maximum_fusion.rest_0_), channel_id=1, source_target_pairs={{0,2},{1,9},{2,4},{3,11},{4,6},{5,13},{6,0},{7,15},{8,10},{9,17},{... | collective-permute-start | bytes 786440 | tf_op jit(solution)/shard_map/ppermute | solution.py:47
  23.9 9.8 %collective-permute-start.8 = (bf16[8,128,128]{2,1,0:T(8,128)(2,1)S(1)}, bf16[8,128,128]{2,1,0:T(8,128)(2,1)S(1)}, u32[]{:S(2)}, u32[]{:S(2)}) collective-permute-start(bf16[8,128,128]{2,1,0:T(8,128)(2,1)S(1)} %pad_maximum_fusion.rest_0_), channel_id=1, source_target_pairs={{0,1},{1,0},{2,3},{3,2},{4,5},{5,4},{6,7},{7,6},{8,9},{9,8},{10,11... | collective-permute-start | bytes 786440 | tf_op jit(solution)/shard_map/ppermute | solution.py:47
  31.0 2.8 %collective-permute-start.9 = (bf16[8,128,128]{2,1,0:T(8,128)(2,1)S(1)}, bf16[8,128,128]{2,1,0:T(8,128)(2,1)S(1)}, u32[]{:S(2)}, u32[]{:S(2)}) collective-permute-start(bf16[8,128,128]{2,1,0:T(8,128)(2,1)S(1)} %constant_dynamic-update-slice_fusion.rest_1_), channel_id=1, source_target_pairs={{0,1},{1,0},{2,3},{3,2},{4,5},{5,4},{6,7},{7,6},{8,9},{9,8},{10,11... | collective-permute-start | bytes 786440 | tf_op jit(solution)/shard_map/ppermute | solution.py:47
  31.1 2.8 %collective-permute-start.10 = (bf16[8,128,128]{2,1,0:T(8,128)(2,1)S(1)}, bf16[8,128,128]{2,1,0:T(8,128)(2,1)S(1)}, u32[]{:S(2)}, u32[]{:S(2)}) collective-permute-start(bf16[8,128,128]{2,1,0:T(8,128)(2,1)S(1)} %collective-permute-done.5.rest_2_), channel_id=1, source_target_pairs={{0,1},{1,0},{2,3},{3,2},{4,5},{5,4},{6,7},{7,6},{8,9},{9,8},{10,11... | collective-permute-start | bytes 786440 | tf_op jit(solution)/shard_map/ppermute | solution.py:47
  31.6 4.9 %collective-permute-start.11 = (bf16[8,128,128]{2,1,0:T(8,128)(2,1)S(1)}, bf16[8,128,128]{2,1,0:T(8,128)(2,1)S(1)}, u32[]{:S(2)}, u32[]{:S(2)}) collective-permute-start(bf16[8,128,128]{2,1,0:T(8,128)(2,1)S(1)} %collective-permute-done.6.rest_3_), channel_id=1, source_target_pairs={{0,1},{1,0},{2,3},{3,2},{4,5},{5,4},{6,7},{7,6},{8,9},{9,8},{10,11... | collective-permute-start | bytes 786440 | tf_op jit(solution)/shard_map/ppermute | solution.py:47
  31.7 4.8 %collective-permute-start.12 = (bf16[8,128,128]{2,1,0:T(8,128)(2,1)S(1)}, bf16[8,128,128]{2,1,0:T(8,128)(2,1)S(1)}, u32[]{:S(2)}, u32[]{:S(2)}) collective-permute-start(bf16[8,128,128]{2,1,0:T(8,128)(2,1)S(1)} %collective-permute-done.7.rest_4_), channel_id=1, source_target_pairs={{0,1},{1,0},{2,3},{3,2},{4,5},{5,4},{6,7},{7,6},{8,9},{9,8},{10,11... | collective-permute-start | bytes 786440 | tf_op jit(solution)/shard_map/ppermute | solution.py:47
  33.8 2.8 %collective-permute-start.13 = (bf16[8,128,128]{2,1,0:T(8,128)(2,1)S(1)}, bf16[8,128,128]{2,1,0:T(8,128)(2,1)S(1)}, u32[]{:S(2)}, u32[]{:S(2)}) collective-permute-start(bf16[8,128,128]{2,1,0:T(8,128)(2,1)S(1)} %collective-permute-done.4.rest_5_), channel_id=1, source_target_pairs={{0,1},{1,0},{2,3},{3,2},{4,5},{5,4},{6,7},{7,6},{8,9},{9,8},{10,11... | collective-permute-start | bytes 786440 | tf_op jit(solution)/shard_map/ppermute | solution.py:47
  33.8 6.8 %collective-permute-start.14 = (bf16[8,128,128]{2,1,0:T(8,128)(2,1)S(1)}, bf16[8,128,128]{2,1,0:T(8,128)(2,1)S(1)}, u32[]{:S(2)}, u32[]{:S(2)}) collective-permute-start(bf16[8,128,128]{2,1,0:T(8,128)(2,1)S(1)} %collective-permute-done.7.rest_4_), channel_id=1, source_target_pairs={{0,2},{1,9},{2,4},{3,11},{4,6},{5,13},{6,0},{7,15},{8,10},{9,17},{... | collective-permute-start | bytes 786440 | tf_op jit(solution)/shard_map/ppermute | solution.py:47
  33.9 6.7 %collective-permute-start.15 = (bf16[8,128,128]{2,1,0:T(8,128)(2,1)S(1)}, bf16[8,128,128]{2,1,0:T(8,128)(2,1)S(1)}, u32[]{:S(2)}, u32[]{:S(2)}) collective-permute-start(bf16[8,128,128]{2,1,0:T(8,128)(2,1)S(1)} %collective-permute-done.6.rest_3_), channel_id=1, source_target_pairs={{0,6},{1,25},{2,0},{3,27},{4,2},{5,29},{6,4},{7,31},{8,14},{9,1},{... | collective-permute-start | bytes 786440 | tf_op jit(solution)/shard_map/ppermute | solution.py:47
  36.6 6.8 %copy-start.6 = (bf16[4,128,128]{2,1,0:T(8,128)(2,1)S(1)}, bf16[4,128,128]{2,1,0:T(8,128)(2,1)}, u32[]{:S(2)}) copy-start(bf16[4,128,128]{2,1,0:T(8,128)(2,1)} %tmatrix.3) | copy-start | bytes 393220
  40.6 2.4 %collective-permute-start.16 = (bf16[8,128,128]{2,1,0:T(8,128)(2,1)S(1)}, bf16[8,128,128]{2,1,0:T(8,128)(2,1)S(1)}, u32[]{:S(2)}, u32[]{:S(2)}) collective-permute-start(bf16[8,128,128]{2,1,0:T(8,128)(2,1)S(1)} %collective-permute-done.14.rest_0_), channel_id=1, source_target_pairs={{0,1},{1,0},{2,3},{3,2},{4,5},{5,4},{6,7},{7,6},{8,9},{9,8},{10,11... | collective-permute-start | bytes 786440 | tf_op jit(solution)/shard_map/ppermute | solution.py:47
  41.9 1.5 %collective-permute-start.17 = (bf16[8,128,128]{2,1,0:T(8,128)(2,1)S(1)}, bf16[8,128,128]{2,1,0:T(8,128)(2,1)S(1)}, u32[]{:S(2)}, u32[]{:S(2)}) collective-permute-start(bf16[8,128,128]{2,1,0:T(8,128)(2,1)S(1)} %collective-permute-done.15.rest_1_), channel_id=1, source_target_pairs={{0,1},{1,0},{2,3},{3,2},{4,5},{5,4},{6,7},{7,6},{8,9},{9,8},{10,11... | collective-permute-start | bytes 786440 | tf_op jit(solution)/shard_map/ppermute | solution.py:47
  43.4 2.2 %copy-start.2 = (bf16[128,128,128]{2,1,0:T(8,128)(2,1)S(1)}, bf16[128,128,128]{2,1,0:T(8,128)(2,1)}, u32[]{:S(2)}) copy-start(bf16[128,128,128]{2,1,0:T(8,128)(2,1)} %copy-done) | copy-start | bytes 12582916
  45.6 6.8 %copy-start.13 = (bf16[2048,512]{1,0:T(8,128)(2,1)S(1)}, bf16[2048,512]{1,0:T(8,128)(2,1)}, u32[]{:S(2)}) copy-start(bf16[2048,512]{1,0:T(8,128)(2,1)} %copy-done.11) | copy-start | bytes 6291460
  47.4 24.4 %copy-start.3 = (bf16[128,128,128]{2,1,0:T(8,128)(2,1)S(1)}, bf16[128,128,128]{2,1,0:T(8,128)(2,1)}, u32[]{:S(2)}) copy-start(bf16[128,128,128]{2,1,0:T(8,128)(2,1)} %copy-done) | copy-start | bytes 12582916
  47.4 7.9 %collective-permute-start.18 = (bf16[4,128,128]{2,1,0:T(8,128)(2,1)S(1)}, bf16[4,128,128]{2,1,0:T(8,128)(2,1)S(1)}, u32[]{:S(2)}, u32[]{:S(2)}) collective-permute-start(bf16[4,128,128]{2,1,0:T(8,128)(2,1)S(1)} %late.2), channel_id=1, source_target_pairs={{0,16},{1,5},{2,18},{3,7},{4,20},{5,1},{6,22},{7,3},{8,24},{9,13},... | collective-permute-start | bytes 393224 | tf_op jit(solution)/shard_map/ppermute | solution.py:47
  49.0 6.4 %collective-permute-start.19 = (bf16[4,128,128]{2,1,0:T(8,128)(2,1)S(1)}, bf16[4,128,128]{2,1,0:T(8,128)(2,1)S(1)}, u32[]{:S(2)}, u32[]{:S(2)}) collective-permute-start(bf16[4,128,128]{2,1,0:T(8,128)(2,1)S(1)} %late.2), channel_id=1, source_target_pairs={{0,8},{1,3},{2,10},{3,5},{4,12},{5,7},{6,14},{7,1},{8,16},{9,11},{... | collective-permute-start | bytes 393224 | tf_op jit(solution)/shard_map/ppermute | solution.py:47
  52.3 3.8 %collective-permute-start.20 = (bf16[4,128,128]{2,1,0:T(8,128)(2,1)S(1)}, bf16[4,128,128]{2,1,0:T(8,128)(2,1)S(1)}, u32[]{:S(2)}, u32[]{:S(2)}) collective-permute-start(bf16[4,128,128]{2,1,0:T(8,128)(2,1)S(1)} %late.2), channel_id=1, source_target_pairs={{0,24},{1,7},{2,26},{3,1},{4,28},{5,3},{6,30},{7,5},{8,0},{9,15},{... | collective-permute-start | bytes 393224 | tf_op jit(solution)/shard_map/ppermute | solution.py:47
  56.2 6.7 %collective-permute-start.21 = (bf16[8,128,128]{2,1,0:T(8,128)(2,1)S(1)}, bf16[8,128,128]{2,1,0:T(8,128)(2,1)S(1)}, u32[]{:S(2)}, u32[]{:S(2)}) collective-permute-start(bf16[8,128,128]{2,1,0:T(8,128)(2,1)S(1)} %constant_dynamic-update-slice_fusion.2.rest_1_), channel_id=1, source_target_pairs={{0,2},{1,9},{2,4},{3,11},{4,6},{5,13},{6,0},{7,15},{8,10},{9,17},{... | collective-permute-start | bytes 786440 | tf_op jit(solution)/shard_map/ppermute | solution.py:47
  56.3 6.9 %collective-permute-start.22 = (bf16[8,128,128]{2,1,0:T(8,128)(2,1)S(1)}, bf16[8,128,128]{2,1,0:T(8,128)(2,1)S(1)}, u32[]{:S(2)}, u32[]{:S(2)}) collective-permute-start(bf16[8,128,128]{2,1,0:T(8,128)(2,1)S(1)} %pad_maximum_fusion.1.rest_0_), channel_id=1, source_target_pairs={{0,6},{1,25},{2,0},{3,27},{4,2},{5,29},{6,4},{7,31},{8,14},{9,1},{... | collective-permute-start | bytes 786440 | tf_op jit(solution)/shard_map/ppermute | solution.py:47
  59.1 6.1 %collective-permute-start.23 = (bf16[8,128,128]{2,1,0:T(8,128)(2,1)S(1)}, bf16[8,128,128]{2,1,0:T(8,128)(2,1)S(1)}, u32[]{:S(2)}, u32[]{:S(2)}) collective-permute-start(bf16[8,128,128]{2,1,0:T(8,128)(2,1)S(1)} %constant_dynamic-update-slice_fusion.2.rest_1_), channel_id=1, source_target_pairs={{0,6},{1,25},{2,0},{3,27},{4,2},{5,29},{6,4},{7,31},{8,14},{9,1},{... | collective-permute-start | bytes 786440 | tf_op jit(solution)/shard_map/ppermute | solution.py:47
  59.2 6.7 %collective-permute-start.24 = (bf16[8,128,128]{2,1,0:T(8,128)(2,1)S(1)}, bf16[8,128,128]{2,1,0:T(8,128)(2,1)S(1)}, u32[]{:S(2)}, u32[]{:S(2)}) collective-permute-start(bf16[8,128,128]{2,1,0:T(8,128)(2,1)S(1)} %pad_maximum_fusion.1.rest_0_), channel_id=1, source_target_pairs={{0,2},{1,9},{2,4},{3,11},{4,6},{5,13},{6,0},{7,15},{8,10},{9,17},{... | collective-permute-start | bytes 786440 | tf_op jit(solution)/shard_map/ppermute | solution.py:47
  60.5 8.1 %collective-permute-start.25 = (bf16[8,128,128]{2,1,0:T(8,128)(2,1)S(1)}, bf16[8,128,128]{2,1,0:T(8,128)(2,1)S(1)}, u32[]{:S(2)}, u32[]{:S(2)}) collective-permute-start(bf16[8,128,128]{2,1,0:T(8,128)(2,1)S(1)} %pad_maximum_fusion.1.rest_0_), channel_id=1, source_target_pairs={{0,1},{1,0},{2,3},{3,2},{4,5},{5,4},{6,7},{7,6},{8,9},{9,8},{10,11... | collective-permute-start | bytes 786440 | tf_op jit(solution)/shard_map/ppermute | solution.py:47
  62.9 5.8 %collective-permute-start.26 = (bf16[8,128,128]{2,1,0:T(8,128)(2,1)S(1)}, bf16[8,128,128]{2,1,0:T(8,128)(2,1)S(1)}, u32[]{:S(2)}, u32[]{:S(2)}) collective-permute-start(bf16[8,128,128]{2,1,0:T(8,128)(2,1)S(1)} %constant_dynamic-update-slice_fusion.2.rest_1_), channel_id=1, source_target_pairs={{0,1},{1,0},{2,3},{3,2},{4,5},{5,4},{6,7},{7,6},{8,9},{9,8},{10,11... | collective-permute-start | bytes 786440 | tf_op jit(solution)/shard_map/ppermute | solution.py:47
  63.3 17.6 %collective-permute-start = (bf16[1024,512]{1,0:T(8,128)(2,1)S(1)}, bf16[1024,512]{1,0:T(8,128)(2,1)S(1)}, u32[]{:S(2)}, u32[]{:S(2)}) collective-permute-start(bf16[1024,512]{1,0:T(8,128)(2,1)S(1)} %order.3), channel_id=1, source_target_pairs={{0,1},{1,0},{2,3},{3,2},{4,5},{5,4},{6,7},{7,6},{8,9},{9,8},{10,11... | collective-permute-start | bytes 3145736 | tf_op jit(solution)/shard_map/ppermute | solution.py:47
  65.2 4.0 %collective-permute-start.27 = (bf16[8,128,128]{2,1,0:T(8,128)(2,1)S(1)}, bf16[8,128,128]{2,1,0:T(8,128)(2,1)S(1)}, u32[]{:S(2)}, u32[]{:S(2)}) collective-permute-start(bf16[8,128,128]{2,1,0:T(8,128)(2,1)S(1)} %collective-permute-done.22.rest_2_), channel_id=1, source_target_pairs={{0,1},{1,0},{2,3},{3,2},{4,5},{5,4},{6,7},{7,6},{8,9},{9,8},{10,11... | collective-permute-start | bytes 786440 | tf_op jit(solution)/shard_map/ppermute | solution.py:47
  65.9 3.9 %collective-permute-start.28 = (bf16[8,128,128]{2,1,0:T(8,128)(2,1)S(1)}, bf16[8,128,128]{2,1,0:T(8,128)(2,1)S(1)}, u32[]{:S(2)}, u32[]{:S(2)}) collective-permute-start(bf16[8,128,128]{2,1,0:T(8,128)(2,1)S(1)} %collective-permute-done.23.rest_3_), channel_id=1, source_target_pairs={{0,1},{1,0},{2,3},{3,2},{4,5},{5,4},{6,7},{7,6},{8,9},{9,8},{10,11... | collective-permute-start | bytes 786440 | tf_op jit(solution)/shard_map/ppermute | solution.py:47
  68.6 3.2 %collective-permute-start.29 = (bf16[8,128,128]{2,1,0:T(8,128)(2,1)S(1)}, bf16[8,128,128]{2,1,0:T(8,128)(2,1)S(1)}, u32[]{:S(2)}, u32[]{:S(2)}) collective-permute-start(bf16[8,128,128]{2,1,0:T(8,128)(2,1)S(1)} %collective-permute-done.24.rest_4_), channel_id=1, source_target_pairs={{0,1},{1,0},{2,3},{3,2},{4,5},{5,4},{6,7},{7,6},{8,9},{9,8},{10,11... | collective-permute-start | bytes 786440 | tf_op jit(solution)/shard_map/ppermute | solution.py:47
  68.6 3.2 %collective-permute-start.30 = (bf16[8,128,128]{2,1,0:T(8,128)(2,1)S(1)}, bf16[8,128,128]{2,1,0:T(8,128)(2,1)S(1)}, u32[]{:S(2)}, u32[]{:S(2)}) collective-permute-start(bf16[8,128,128]{2,1,0:T(8,128)(2,1)S(1)} %collective-permute-done.21.rest_5_), channel_id=1, source_target_pairs={{0,1},{1,0},{2,3},{3,2},{4,5},{5,4},{6,7},{7,6},{8,9},{9,8},{10,11... | collective-permute-start | bytes 786440 | tf_op jit(solution)/shard_map/ppermute | solution.py:47
  69.2 6.7 %collective-permute-start.31 = (bf16[8,128,128]{2,1,0:T(8,128)(2,1)S(1)}, bf16[8,128,128]{2,1,0:T(8,128)(2,1)S(1)}, u32[]{:S(2)}, u32[]{:S(2)}) collective-permute-start(bf16[8,128,128]{2,1,0:T(8,128)(2,1)S(1)} %collective-permute-done.24.rest_4_), channel_id=1, source_target_pairs={{0,2},{1,9},{2,4},{3,11},{4,6},{5,13},{6,0},{7,15},{8,10},{9,17},{... | collective-permute-start | bytes 786440 | tf_op jit(solution)/shard_map/ppermute | solution.py:47
  69.8 6.1 %collective-permute-start.32 = (bf16[8,128,128]{2,1,0:T(8,128)(2,1)S(1)}, bf16[8,128,128]{2,1,0:T(8,128)(2,1)S(1)}, u32[]{:S(2)}, u32[]{:S(2)}) collective-permute-start(bf16[8,128,128]{2,1,0:T(8,128)(2,1)S(1)} %collective-permute-done.23.rest_3_), channel_id=1, source_target_pairs={{0,6},{1,25},{2,0},{3,27},{4,2},{5,29},{6,4},{7,31},{8,14},{9,1},{... | collective-permute-start | bytes 786440 | tf_op jit(solution)/shard_map/ppermute | solution.py:47
  75.9 2.3 %collective-permute-start.33 = (bf16[8,128,128]{2,1,0:T(8,128)(2,1)S(1)}, bf16[8,128,128]{2,1,0:T(8,128)(2,1)S(1)}, u32[]{:S(2)}, u32[]{:S(2)}) collective-permute-start(bf16[8,128,128]{2,1,0:T(8,128)(2,1)S(1)} %collective-permute-done.31.rest_0_), channel_id=1, source_target_pairs={{0,1},{1,0},{2,3},{3,2},{4,5},{5,4},{6,7},{7,6},{8,9},{9,8},{10,11... | collective-permute-start | bytes 786440 | tf_op jit(solution)/shard_map/ppermute | solution.py:47
  77.0 1.5 %collective-permute-start.34 = (bf16[8,128,128]{2,1,0:T(8,128)(2,1)S(1)}, bf16[8,128,128]{2,1,0:T(8,128)(2,1)S(1)}, u32[]{:S(2)}, u32[]{:S(2)}) collective-permute-start(bf16[8,128,128]{2,1,0:T(8,128)(2,1)S(1)} %collective-permute-done.32.rest_1_), channel_id=1, source_target_pairs={{0,1},{1,0},{2,3},{3,2},{4,5},{5,4},{6,7},{7,6},{8,9},{9,8},{10,11... | collective-permute-start | bytes 786440 | tf_op jit(solution)/shard_map/ppermute | solution.py:47
  80.4 1.4 %collective-permute-start.35 = (bf16[4,128,128]{2,1,0:T(8,128)(2,1)S(1)}, bf16[4,128,128]{2,1,0:T(8,128)(2,1)S(1)}, u32[]{:S(2)}, u32[]{:S(2)}) collective-permute-start(bf16[4,128,128]{2,1,0:T(8,128)(2,1)S(1)} %late.3), channel_id=1, source_target_pairs={{0,1},{1,0},{2,3},{3,2},{4,5},{5,4},{6,7},{7,6},{8,9},{9,8},{10,11... | collective-permute-start | bytes 393224 | tf_op jit(solution)/shard_map/ppermute | solution.py:47
  (4 other events, 6.0 us)

commit v4 on v3

--- a/solution.py
+++ b/solution.py
@@ -5,10 +5,10 @@
 from jax.experimental.pallas import tpu as pltpu
 from jax.sharding import PartitionSpec as P
 
+
 SIDE = 4
 OWN = 4
 SOURCES = 2 * SIDE * SIDE * OWN
-BLOCKS = 128
 PAIRS = 512
 TILE = 128
 JOIN = 8
@@ -20,6 +20,7 @@
 SMEM = pl.BlockSpec(memory_space=pltpu.SMEM)
 VMEM = pl.BlockSpec(memory_space=pltpu.VMEM)
 ANY = pl.BlockSpec(memory_space=pl.ANY)
+HBM = pl.BlockSpec(memory_space=pltpu.HBM)
 
 
 def device_of(x, y, core):
@@ -47,15 +48,19 @@
     return lax.ppermute(values, "dev", pairs)
 
 
+def stay(values):
+    return pltpu.with_memory_space_constraint(values, pltpu.HBM)
+
+
 def together(values, *fillers):
     return lax.optimization_barrier((values, fillers))[0]
 
 
-def spread(coeff, fill_first, fill_second):
+def spread(coeff, *fillers):
     first2 = send(coeff, along_first(2))
     first3 = send(coeff, along_first(1))
     first1 = send(coeff, along_first(-1))
-    first2, first3, first1 = together((first2, first3, first1), *fill_first)
+    first2, first3, first1 = together((first2, first3, first1), *fillers)
     low = jnp.concatenate([coeff, first1])
     high = jnp.concatenate([first2, first3])
     low3 = send(low, along_second(1))
@@ -64,10 +69,10 @@
     low1 = send(low, along_second(-1))
     low2 = send(low3, along_second(1))
     high2 = send(high1, along_second(-1))
-    high3, low1 = together((high3, low1), *fill_second)
     near = (low, high, low1, high1, low3, high3)
-    far = (low2, high2)
-    return near, tuple(send(piece, SWAP) for piece in near), far
+    other = (send(low, SWAP), send(high, SWAP))
+    other += tuple(send(piece, SWAP) for piece in near[2:])
+    return near, other, (low2, high2)
 
 
 def swapped(pieces, before):
@@ -93,9 +98,7 @@
     return lax.dot_general(left, right, (contract, ((), ())), preferred_element_type=jnp.float32)
 
 
-def plan_kernel(me, count, need, src, tgt, blk, blocks, words, groups, sizes, near, sem):
-    copy = pltpu.make_async_copy(blocks, near, sem)
-    copy.start()
+def plan_kernel(me, count, need, src, tgt, blk, words, groups, sizes):
     source = src[...]
     peer, request = source >> 2, source & 3
     from_peer = ones_where(counted((need.shape[0], PAIRS), 0) == peer)
@@ -147,70 +150,72 @@
         needed = (total.astype(jnp.int32) + (WIDE - 1)) // WIDE
         steps = jnp.where(lane == k, needed, steps)
     sizes[...] = steps
-    copy.wait()
-
-
-def plan(need, src, tgt, blk, count, blocks):
+
+
+def plan(need, src, tgt, blk, count):
     me = lax.axis_index("dev").reshape(1)
-    words, groups, sizes, near = pl.pallas_call(
+    return pl.pallas_call(
         plan_kernel,
         out_shape=(
             jax.ShapeDtypeStruct((1, GROUPS * JOIN), jnp.int32),
             jax.ShapeDtypeStruct((1, 2 * TILE), jnp.int32),
             jax.ShapeDtypeStruct((1, TILE), jnp.int32),
-            jax.ShapeDtypeStruct(blocks.shape, blocks.dtype),
         ),
-        in_specs=[SMEM] * 2 + [VMEM] * 4 + [ANY],
-        out_specs=(VMEM,) * 4,
-        scratch_shapes=[pltpu.SemaphoreType.DMA],
+        in_specs=[SMEM] * 2 + [VMEM] * 4,
+        out_specs=(VMEM,) * 3,
         compiler_params=LIMIT,
         cost_estimate=pl.CostEstimate(
-            flops=1_000_000_000, bytes_accessed=8_000_000, transcendentals=0
+            flops=1_000_000_000, bytes_accessed=1_000_000, transcendentals=0
         ),
         name="plan",
-    )(me, count, need, src, tgt, blk, blocks)
-    return (words, groups, sizes), near
+    )(me, count, need, src, tgt, blk)
 
 
 def add_pairs(part, lists, groups, sizes, blocks, sources, total):
-    def step(i, carry):
+    def several(count, first):
         made = []
-        for w in range(WIDE):
-            group = groups[0, part * LATE_GROUP + i * WIDE + w]
+        for w in range(count):
+            group = groups[0, part * LATE_GROUP + first + w]
             base = group & 0xFFFF
             left, right = [], []
             for u in range(JOIN):
                 word = lists[0, base + u]
                 left.append(blocks[word >> 8])
                 right.append(sources[word & 0xFF])
-            product = jnp.dot(
-                jnp.concatenate(left, axis=1),
-                jnp.concatenate(right, axis=0),
-                preferred_element_type=jnp.float32,
-            )
-            made.append((group >> 16, product))
+            made.append((group >> 16, dot(jnp.concatenate(left, 1), jnp.concatenate(right, 0))))
         for target, product in made:
             total[target] += product
+
+    def full(i, carry):
+        several(2 * WIDE, i * (2 * WIDE))
         return carry
 
-    lax.fori_loop(0, sizes[0, part], step, 0)
+    def rest(i, carry):
+        several(WIDE, i * WIDE)
+        return carry
+
+    steps = sizes[0, part]
+    lax.fori_loop(0, steps // 2, full, 0)
+    lax.fori_loop(steps // 2 * 2, steps, rest, 0)
 
 
 def fetch(pieces, places, sources, sems):
     copies = []
     for n, (piece, place) in enumerate(zip(pieces, places)):
-        copy = pltpu.make_async_copy(piece, sources.at[pl.ds(place, piece.shape[0])], sems.at[n])
+        there = sources.at[pl.ds(place, piece.shape[0])]
+        copies.append(pltpu.make_async_copy(piece, there, sems.at[n]))
+    for copy in copies:
         copy.start()
-        copies.append(copy)
     sources[SOURCES] = jnp.zeros((TILE, TILE), jnp.bfloat16)
+    return copies
+
+
+def early_kernel(lists, groups, sizes, blocks, incident, *rest):
+    pieces, (total, sources, sems) = rest[:-3], rest[-3:]
+    copies = fetch(pieces, EARLY_AT, sources, sems)
+    total[...] = incident[...].astype(jnp.float32)
     for copy in copies:
         copy.wait()
-
-
-def early_kernel(lists, groups, sizes, blocks, incident, *rest):
-    pieces, (total, sources, sems) = rest[:-3], rest[-3:]
-    fetch(pieces, EARLY_AT, sources, sems)
-    total[...] = incident[...].astype(jnp.float32)
     add_pairs(0, lists, groups, sizes, blocks, sources, total)
 
 
@@ -221,8 +226,10 @@
 
 def late_kernel(lists, groups, sizes, blocks, before, tmatrix, *rest):
     pieces, (coeff, sources, total, sems) = rest[:-4], rest[-4:]
-    fetch(pieces, LATE_AT, sources, sems)
+    copies = fetch(pieces, LATE_AT, sources, sems)
     total[...] = before[...]
+    for copy in copies:
+        copy.wait()
     add_pairs(1, lists, groups, sizes, blocks, sources, total)
     for t in range(OWN):
         coeff[t] = finish(tmatrix, total, t)
@@ -234,7 +241,8 @@
 def far_kernel(mine, other, coeff, arrived, far):
     def chunk(i, carry):
         rows = pl.ds(pl.multiple_of(i * FAR_ROWS, FAR_ROWS), FAR_ROWS)
-        far[rows, :] = dot(mine[rows, :], coeff[...]) + dot(other[rows, :], arrived[...])
+        made = dot(mine[rows, :], coeff[...]) + dot(other[rows, :], arrived[...])
+        far[rows, :] = made.astype(far.dtype)
         return carry
 
     lax.fori_loop(0, far.shape[0] // FAR_ROWS, chunk, 0)
@@ -243,7 +251,7 @@
 def far_field(mine, other, coeff, arrived):
     return pl.pallas_call(
         far_kernel,
-        out_shape=jax.ShapeDtypeStruct((mine.shape[0], TILE), jnp.float32),
+        out_shape=jax.ShapeDtypeStruct((mine.shape[0], TILE), jnp.bfloat16),
         in_specs=[VMEM] * 4,
         out_specs=VMEM,
         compiler_params=LIMIT,
@@ -251,58 +259,56 @@
     )(mine, other, coeff.reshape(-1, TILE), arrived.reshape(-1, TILE))
 
 
-def table_kernel(phases, harmonics, table):
+def order_kernel(order, factor_far, harmonics, ordered, right, factor, sems):
+    first = pltpu.make_async_copy(factor_far, factor, sems.at[0])
+    first.start()
+    copy = pltpu.make_async_copy(harmonics, right.at[:, pl.ds(0, TILE)], sems.at[1])
+    copy.start()
+    first.wait()
+    for i in range(right.shape[0] // FAR_ROWS):
+        rows = pl.ds(i * FAR_ROWS, FAR_ROWS)
+        phase = factor[:, rows]
+        high = phase.astype(jnp.bfloat16).astype(jnp.float32)
+        middle = (phase - high).astype(jnp.bfloat16).astype(jnp.float32)
+        parts = [high, middle, phase - high - middle, jnp.zeros_like(phase)]
+        parts = jnp.concatenate(parts, axis=0).T
+        parts = jnp.concatenate([parts, jnp.zeros((FAR_ROWS, TILE - 4 * OWN), jnp.float32)], axis=1)
+        right[rows, TILE:] = parts.astype(jnp.bfloat16)
+    copy.wait()
+
     def chunk(i, carry):
         rows = pl.ds(pl.multiple_of(i * FAR_ROWS, FAR_ROWS), FAR_ROWS)
-        modes = harmonics[rows, :].astype(jnp.float32)
+        wanted = jnp.broadcast_to(order[rows, :], (FAR_ROWS, right.shape[0]))
+        pick = ones_where(wanted == counted(wanted.shape, 1))
+        found = dot(pick, right[...])
+        mode, parts = found[:, :TILE], found[:, TILE:]
         for s in range(OWN):
-            phase = jnp.broadcast_to(phases[rows, s : s + 1], modes.shape)
-            table[rows, s * TILE : (s + 1) * TILE] = (phase * modes).astype(jnp.bfloat16)
+            phase = parts[:, s : s + 1] + parts[:, OWN + s : OWN + s + 1]
+            phase = phase + parts[:, 2 * OWN + s : 2 * OWN + s + 1]
+            made = jnp.broadcast_to(phase, mode.shape) * mode
+            ordered[rows, s * TILE : (s + 1) * TILE] = made.astype(jnp.bfloat16)
         return carry
 
-    lax.fori_loop(0, table.shape[0] // FAR_ROWS, chunk, 0)
-
-
-def order_kernel(order, table, ordered):
-    def chunk(i, carry):
-        rows = pl.ds(pl.multiple_of(i * FAR_ROWS, FAR_ROWS), FAR_ROWS)
-        wanted = jnp.broadcast_to(order[rows, :], (FAR_ROWS, table.shape[0]))
-        place = lax.broadcasted_iota(jnp.int32, wanted.shape, 1)
-        pick = jnp.where(wanted == place, 1.0, 0.0).astype(jnp.bfloat16)
-        ordered[rows, :] = jnp.dot(pick, table[...], preferred_element_type=jnp.float32).astype(
-            jnp.bfloat16
-        )
-        return carry
-
     lax.fori_loop(0, ordered.shape[0] // FAR_ROWS, chunk, 0)
 
 
-def make_table(factor, harmonics):
-    return pl.pallas_call(
-        table_kernel,
-        out_shape=jax.ShapeDtypeStruct((harmonics.shape[0], OWN * TILE), jnp.bfloat16),
-        in_specs=[VMEM] * 2,
-        out_specs=VMEM,
-        compiler_params=LIMIT,
-        cost_estimate=pl.CostEstimate(
-            flops=1_000_000_000, bytes_accessed=4_000_000, transcendentals=0
-        ),
-        name="table",
-    )(factor.T, harmonics)
-
-
-def in_order(order, table):
+def in_order(order, factor, harmonics):
     return pl.pallas_call(
         order_kernel,
         out_shape=jax.ShapeDtypeStruct((order.shape[0], OWN * TILE), jnp.bfloat16),
-        in_specs=[VMEM] * 2,
+        in_specs=[VMEM] + [HBM] * 2,
         out_specs=VMEM,
+        scratch_shapes=[
+            pltpu.VMEM((harmonics.shape[0], 2 * TILE), jnp.bfloat16),
+            pltpu.VMEM(factor.shape, factor.dtype),
+            pltpu.SemaphoreType.DMA((2,)),
+        ],
         compiler_params=LIMIT,
         cost_estimate=pl.CostEstimate(
             flops=2_000_000_000, bytes_accessed=4_000_000, transcendentals=0
         ),
         name="order",
-    )(order[:, None], table)
+    )(order, stay(factor), stay(harmonics))
 
 
 SCRATCH = pltpu.VMEM((SOURCES + 1, TILE, TILE), jnp.bfloat16)
@@ -360,30 +366,30 @@
 ):
     n_grp, n_dev = lax.axis_size("grp"), lax.axis_size("dev")
     coeff = apply_tmatrix(tmatrix, incident)
-    made, blocks = plan(need[0], pair_src, pair_tgt, pair_blk, pair_count, blocks)
-    table = make_table(factor, harmonics)
+    made = plan(need[0], pair_src, pair_tgt, pair_blk, pair_count)
 
     rows = owner.shape[0] // (n_grp * n_dev)
-    order = owner.reshape(n_grp, n_dev // 2, 2, rows).transpose(2, 1, 0, 3).reshape(2, -1)
+    order = owner.reshape(n_grp * n_dev // 2, 2, rows).transpose(1, 0, 2).reshape(2, -1)
     core = lax.axis_index("dev") % 2
     order_mine = jnp.where(core == 0, order[0], order[1])
     order_other = jnp.where(core == 0, order[1], order[0])
-    for_other = in_order(order_other, table)
-    near, other, far = spread(coeff, (made, table), (for_other,))
+    order_mine, order_other = lax.optimization_barrier((order_mine[:, None], order_other[:, None]))
+    for_other = in_order(order_other, factor, harmonics)
+    near, other, far = spread(coeff, made, for_other)
     before = early_pairs(made, blocks, incident, near + other)
     coeff = late_pairs(made, blocks, before, tmatrix, swapped(far, before))
 
-    mine = in_order(order_mine, table)
-    near, other, far = spread(coeff, (mine,), ())
+    mine = in_order(order_mine, factor, harmonics)
+    near, other, far = spread(coeff, mine)
     weighted_other = send(for_other, SWAP)
     before = early_pairs(made, blocks, incident, near + other)
     coeff = late_pairs(made, blocks, before, tmatrix, swapped(far, before))
 
     amplitude = far_field(mine, weighted_other, coeff, send(coeff, SWAP))
-    amplitude = amplitude.reshape(n_dev // 2, n_grp * rows, TILE)
-    amplitude = lax.all_to_all(amplitude, "dev", 0, 0, axis_index_groups=SAME_CORE).sum(axis=0)
-    amplitude = amplitude.reshape(n_grp, rows, TILE)
-    return lax.all_to_all(amplitude, "grp", 0, 0).sum(axis=0)
+    amplitude = amplitude.reshape(n_grp * n_dev // 2, rows, TILE)
+    groups = [[g * n_dev + d for g in range(n_grp) for d in same] for same in SAME_CORE]
+    amplitude = lax.all_to_all(amplitude, ("grp", "dev"), 0, 0, axis_index_groups=groups)
+    return amplitude.astype(jnp.float32).sum(axis=0)
 
 
 def solution(mesh):

time: 117 us -> 106 us (0.906); the launches traced: 115 us -> 106 us
  local copies, waits for them, and re-layouts: 12.3 us -> 3.94 us
  blocking collectives: 31.7 us -> 25 us
  starting transfers between devices: 38.3 us -> 42.2 us
  waiting for transfers between devices: 11.1 us -> 12.3 us
    unnamed x35 -> x20, local copies, waits for them, and re-layouts: 11.5 us -> 2.26 us
    all_to_all x2 -> x1, blocking collectives: 31.7 us -> 25 us  [body(): lax.all_to_all(amplitude, ('grp', 'dev'), 0, 0, axis_index_groups=groups)]
    ppermute x36, starting transfers between devices: 38.3 us -> 42.2 us  [send(): return lax.ppermute(values, 'dev', pairs)]
    pallas_call x2, Pallas kernels: 5.97 us -> 7.96 us  [in_order(): pl.pallas_call(order_kernel, out_shape=jax.ShapeDtypeStruct((order.shape[...]
    pallas_call x1 -> x0, Pallas kernels: 1.66 us -> none  [make_table(): pl.pallas_call(table_kernel, out_shape=jax.ShapeDtypeStruct((harmonics.sh...]
  transfers between devices with their start and end apart: 36 -> 36, of which waited for: 12 -> 12; matrix products, arithmetic and copies ran while one was open for 2% -> 2% of each run, Pallas kernels for 14% -> 15%
where the time goes in v4:
time: 106 us
  starting transfers between devices  42.2 us (40%)
  blocking collectives  25 us (24%)
  Pallas kernels  19 us (18%)
  waiting for transfers between devices  12.3 us (12%)
  local copies, waits for them, and re-layouts  3.94 us (4%)
  other arithmetic  1.17 us (1%)
  matrix products  1.14 us (1%)
  between operations  1.13 us (1%)
    ppermute x36, starting transfers between devices, send(): return lax.ppermute(values, 'dev', pairs)  42.2 us
    all_to_all x1, blocking collectives, body(): lax.all_to_all(amplitude, ('grp', 'dev'), 0, 0, axis_index_groups=groups)  25 us
    ppermute x36, waiting for transfers between devices, send(): return lax.ppermute(values, 'dev', pairs)  12.3 us
    pallas_call x2, Pallas kernels, in_order(): pl.pallas_call(order_kernel, out_shape=jax.ShapeDtypeStruct((order.shape[...  7.96 us
    pallas_call x2, Pallas kernels, early_pairs(): pl.pallas_call(early_kernel, out_shape=jax.ShapeDtypeStruct(TOTAL, jnp.fl...  5.75 us
    pallas_call x2, Pallas kernels, late_pairs(): pl.pallas_call(late_kernel, out_shape=jax.ShapeDtypeStruct(TOTAL, jnp.bfl...  3.34 us
    unnamed x20, local copies, waits for them, and re-layouts  2.26 us
  transfers between devices with their start and end apart: 36, of which 12 were waited for; matrix products, arithmetic and copies ran while one was open for 2% of the time, Pallas kernels for 15%

profile of v4, /device:TPU:1, one launch (start us, length us, event | category | flops | bytes accessed | tf_op | source)
XLA Modules:
  0.0 105.9 jit_solution(5073573682985385343)
XLA Ops:
  0.0 1.1 %convolution_convert_fusion = bf16[4,128,128]{2,1,0:T(8,128)(2,1)S(1)} fusion(bf16[4,128,128]{2,1,0:T(8,128)(2,1)} %tmatrix.3, bf16[4,128,128]{2,1,0:T(8,128)(2,1)} %incident.3), kind=kOutput, calls=%fused_computation | convolution fusion | flops 16842752 | bytes 393216 | tf_op jit(solution)/shard_map/skl,slq->skq/dot_general | solution.py:350
  1.1 3.8 %collective-permute-start.1 = (bf16[4,128,128]{2,1,0:T(8,128)(2,1)S(1)}, bf16[4,128,128]{2,1,0:T(8,128)(2,1)S(1)}, u32[]{:S(2)}, u32[]{:S(2)}) collective-permute-start(bf16[4,128,128]{2,1,0:T(8,128)(2,1)S(1)} %convolution_convert_fusion), channel_id=1, source_target_pairs={{0,16},{1,5},{2,18},{3,7},{4,20},{5,1},{6,22},{7,3},{8,24},{9,13},... | collective-permute-start | bytes 393224 | tf_op jit(solution)/shard_map/ppermute | solution.py:48
  5.0 0.4 collective-permute-start.2
  5.4 2.3 %collective-permute-start.3 = (bf16[4,128,128]{2,1,0:T(8,128)(2,1)S(1)}, bf16[4,128,128]{2,1,0:T(8,128)(2,1)S(1)}, u32[]{:S(2)}, u32[]{:S(2)}) collective-permute-start(bf16[4,128,128]{2,1,0:T(8,128)(2,1)S(1)} %convolution_convert_fusion), channel_id=1, source_target_pairs={{0,24},{1,7},{2,26},{3,1},{4,28},{5,3},{6,30},{7,5},{8,0},{9,15},{... | collective-permute-start | bytes 393224 | tf_op jit(solution)/shard_map/ppermute | solution.py:48
  7.6 0.9 reshape.58
  8.6 0.4 fusion.1
  9.4 4.0 %order.3 = bf16[1024,512]{1,0:T(8,128)(2,1)S(1)} custom-call(s32[1024,1]{1,0:T(8,128)S(1)} %copy.14.order, f32[4,2048]{1,0:T(4,128)} %factor_far.3, bf16[2048,128]{1,0:T(8,128)(2,1)} %harmonics.3), custom_call_target="tpu_custom_call" | custom-call | flops 2000000000 | bytes 4000000 | tf_op jit(solution)/shard_map/order/pallas_call | solution.py:296
  14.4 0.8 plan.1
  15.3 2.6 %collective-permute-start.5 = (bf16[8,128,128]{2,1,0:T(8,128)(2,1)S(1)}, bf16[8,128,128]{2,1,0:T(8,128)(2,1)S(1)}, u32[]{:S(2)}, u32[]{:S(2)}) collective-permute-start(bf16[8,128,128]{2,1,0:T(8,128)(2,1)S(1)} %constant_dynamic-update-slice_fusion.rest_1_), channel_id=1, source_target_pairs={{0,6},{1,25},{2,0},{3,27},{4,2},{5,29},{6,4},{7,31},{8,14},{9,1},{... | collective-permute-start | bytes 786440 | tf_op jit(solution)/shard_map/ppermute | solution.py:48
  17.8 1.9 %collective-permute-start.9 = (bf16[8,128,128]{2,1,0:T(8,128)(2,1)S(1)}, bf16[8,128,128]{2,1,0:T(8,128)(2,1)S(1)}, u32[]{:S(2)}, u32[]{:S(2)}) collective-permute-start(bf16[8,128,128]{2,1,0:T(8,128)(2,1)S(1)} %constant_dynamic-update-slice_fusion.rest_1_), channel_id=1, source_target_pairs={{0,1},{1,0},{2,3},{3,2},{4,5},{5,4},{6,7},{7,6},{8,9},{9,8},{10,11... | collective-permute-start | bytes 786440 | tf_op jit(solution)/shard_map/ppermute | solution.py:48
  19.8 0.9 collective-permute-start.4
  20.6 0.7 collective-permute-start.6
  21.3 2.3 %collective-permute-start.8 = (bf16[8,128,128]{2,1,0:T(8,128)(2,1)S(1)}, bf16[8,128,128]{2,1,0:T(8,128)(2,1)S(1)}, u32[]{:S(2)}, u32[]{:S(2)}) collective-permute-start(bf16[8,128,128]{2,1,0:T(8,128)(2,1)S(1)} %pad_maximum_fusion.rest_0_), channel_id=1, source_target_pairs={{0,1},{1,0},{2,3},{3,2},{4,5},{5,4},{6,7},{7,6},{8,9},{9,8},{10,11... | collective-permute-start | bytes 786440 | tf_op jit(solution)/shard_map/ppermute | solution.py:48
  23.6 1.0 collective-permute-done.7.rest_5_
  24.6 2.7 %collective-permute-start.11 = (bf16[8,128,128]{2,1,0:T(8,128)(2,1)S(1)}, bf16[8,128,128]{2,1,0:T(8,128)(2,1)S(1)}, u32[]{:S(2)}, u32[]{:S(2)}) collective-permute-start(bf16[8,128,128]{2,1,0:T(8,128)(2,1)S(1)} %collective-permute-done.5.rest_3_), channel_id=1, source_target_pairs={{0,1},{1,0},{2,3},{3,2},{4,5},{5,4},{6,7},{7,6},{8,9},{9,8},{10,11... | collective-permute-start | bytes 786440 | tf_op jit(solution)/shard_map/ppermute | solution.py:48
  27.3 0.5 collective-permute-start.10
  27.8 2.8 %collective-permute-start.12 = (bf16[8,128,128]{2,1,0:T(8,128)(2,1)S(1)}, bf16[8,128,128]{2,1,0:T(8,128)(2,1)S(1)}, u32[]{:S(2)}, u32[]{:S(2)}) collective-permute-start(bf16[8,128,128]{2,1,0:T(8,128)(2,1)S(1)} %collective-permute-done.6.rest_4_), channel_id=1, source_target_pairs={{0,1},{1,0},{2,3},{3,2},{4,5},{5,4},{6,7},{7,6},{8,9},{9,8},{10,11... | collective-permute-start | bytes 786440 | tf_op jit(solution)/shard_map/ppermute | solution.py:48
  30.7 1.5 %collective-permute-start.14 = (bf16[8,128,128]{2,1,0:T(8,128)(2,1)S(1)}, bf16[8,128,128]{2,1,0:T(8,128)(2,1)S(1)}, u32[]{:S(2)}, u32[]{:S(2)}) collective-permute-start(bf16[8,128,128]{2,1,0:T(8,128)(2,1)S(1)} %collective-permute-done.6.rest_4_), channel_id=1, source_target_pairs={{0,2},{1,9},{2,4},{3,11},{4,6},{5,13},{6,0},{7,15},{8,10},{9,17},{... | collective-permute-start | bytes 786440 | tf_op jit(solution)/shard_map/ppermute | solution.py:48
  32.2 2.9 %early.2.before = f32[4,128,128]{2,1,0:T(8,128)S(1)} custom-call(s32[1,1152]{1,0:T(1,128)S(1)} %get-tuple-element.22.lists, s32[1,256]{1,0:T(1,128)S(1)} %get-tuple-element.23.groups, s32[1,128]{1,0:T(1,128)S(1)} %get-tuple-element.24.sizes, bf16[128,128,128]{2,1,0:T(8,128)(2,1)S(1)} %copy-done, bf16[4,128,128]{2,1,0:T(8,128)(2,1)S(1)} %copy-done.3, ...), custom_call_target="tpu_custom_call" | custom-call | flops 2000000000 | bytes 8000000 | tf_op jit(solution)/shard_map/early/pallas_call | solution.py:319
  35.1 1.1 %collective-permute-done.15.rest_1_ = bf16[8,128,128]{2,1,0:T(8,128)(2,1)S(1)} collective-permute-done((bf16[8,128,128]{2,1,0:T(8,128)(2,1)S(1)}, bf16[8,128,128]{2,1,0:T(8,128)(2,1)S(1)}, u32[]{:S(2)}, u32[]{:S(2)}) %collective-permute-start.15) | collective-permute-done | bytes 262176 | tf_op jit(solution)/shard_map/ppermute | solution.py:48
  36.2 1.5 %collective-permute-done.14.rest_0_ = bf16[8,128,128]{2,1,0:T(8,128)(2,1)S(1)} collective-permute-done((bf16[8,128,128]{2,1,0:T(8,128)(2,1)S(1)}, bf16[8,128,128]{2,1,0:T(8,128)(2,1)S(1)}, u32[]{:S(2)}, u32[]{:S(2)}) %collective-permute-start.14) | collective-permute-done | bytes 262176 | tf_op jit(solution)/shard_map/ppermute | solution.py:48
  37.7 1.1 %collective-permute-start.16 = (bf16[8,128,128]{2,1,0:T(8,128)(2,1)S(1)}, bf16[8,128,128]{2,1,0:T(8,128)(2,1)S(1)}, u32[]{:S(2)}, u32[]{:S(2)}) collective-permute-start(bf16[8,128,128]{2,1,0:T(8,128)(2,1)S(1)} %collective-permute-done.14.rest_0_), channel_id=1, source_target_pairs={{0,1},{1,0},{2,3},{3,2},{4,5},{5,4},{6,7},{7,6},{8,9},{9,8},{10,11... | collective-permute-start | bytes 786440 | tf_op jit(solution)/shard_map/ppermute | solution.py:48
  39.0 0.9 collective-permute-done.16.rest_2_
  40.3 2.2 %copy-done.1 = bf16[128,128,128]{2,1,0:T(8,128)(2,1)S(1)} copy-done((bf16[128,128,128]{2,1,0:T(8,128)(2,1)S(1)}, bf16[128,128,128]{2,1,0:T(8,128)(2,1)}, u32[]{:S(2)}) %copy-start.1) | copy-done | bytes 4194328
  42.5 1.7 %late.2 = bf16[4,128,128]{2,1,0:T(8,128)(2,1)S(1)} custom-call(s32[1,1152]{1,0:T(1,128)S(1)} %get-tuple-element.22.lists, s32[1,256]{1,0:T(1,128)S(1)} %get-tuple-element.23.groups, s32[1,128]{1,0:T(1,128)S(1)} %get-tuple-element.24.sizes, bf16[128,128,128]{2,1,0:T(8,128)(2,1)S(1)} %copy-done.1, f32[4,128,128]{2,1,0:T(8,128)S(1)} %early.2.before, ...), custom_call_target="tpu_custom_call" | custom-call | tf_op jit(solution)/shard_map/late/pallas_call | solution.py:334
  44.3 0.5 collective-permute-start.19
  44.8 2.3 %collective-permute-start.20 = (bf16[4,128,128]{2,1,0:T(8,128)(2,1)S(1)}, bf16[4,128,128]{2,1,0:T(8,128)(2,1)S(1)}, u32[]{:S(2)}, u32[]{:S(2)}) collective-permute-start(bf16[4,128,128]{2,1,0:T(8,128)(2,1)S(1)} %late.2), channel_id=1, source_target_pairs={{0,24},{1,7},{2,26},{3,1},{4,28},{5,3},{6,30},{7,5},{8,0},{9,15},{... | collective-permute-start | bytes 393224 | tf_op jit(solution)/shard_map/ppermute | solution.py:48
  47.1 4.0 %order.2.mine = bf16[1024,512]{1,0:T(8,128)(2,1)S(1)} custom-call(s32[1024,1]{1,0:T(8,128)S(1)} %copy.13.order, f32[4,2048]{1,0:T(4,128)} %factor_far.3, bf16[2048,128]{1,0:T(8,128)(2,1)} %harmonics.3), custom_call_target="tpu_custom_call" | custom-call | flops 2000000000 | bytes 4000000 | tf_op jit(solution)/shard_map/order/pallas_call | solution.py:296
  51.3 1.5 %collective-permute-start.24 = (bf16[8,128,128]{2,1,0:T(8,128)(2,1)S(1)}, bf16[8,128,128]{2,1,0:T(8,128)(2,1)S(1)}, u32[]{:S(2)}, u32[]{:S(2)}) collective-permute-start(bf16[8,128,128]{2,1,0:T(8,128)(2,1)S(1)} %constant_dynamic-update-slice_fusion.2.rest_1_), channel_id=1, source_target_pairs={{0,2},{1,9},{2,4},{3,11},{4,6},{5,13},{6,0},{7,15},{8,10},{9,17},{... | collective-permute-start | bytes 786440 | tf_op jit(solution)/shard_map/ppermute | solution.py:48
  52.8 2.8 %collective-permute-start.26 = (bf16[8,128,128]{2,1,0:T(8,128)(2,1)S(1)}, bf16[8,128,128]{2,1,0:T(8,128)(2,1)S(1)}, u32[]{:S(2)}, u32[]{:S(2)}) collective-permute-start(bf16[8,128,128]{2,1,0:T(8,128)(2,1)S(1)} %constant_dynamic-update-slice_fusion.2.rest_1_), channel_id=1, source_target_pairs={{0,1},{1,0},{2,3},{3,2},{4,5},{5,4},{6,7},{7,6},{8,9},{9,8},{10,11... | collective-permute-start | bytes 786440 | tf_op jit(solution)/shard_map/ppermute | solution.py:48
  55.6 1.6 %collective-permute-start.21 = (bf16[8,128,128]{2,1,0:T(8,128)(2,1)S(1)}, bf16[8,128,128]{2,1,0:T(8,128)(2,1)S(1)}, u32[]{:S(2)}, u32[]{:S(2)}) collective-permute-start(bf16[8,128,128]{2,1,0:T(8,128)(2,1)S(1)} %pad_maximum_fusion.1.rest_0_), channel_id=1, source_target_pairs={{0,6},{1,25},{2,0},{3,27},{4,2},{5,29},{6,4},{7,31},{8,14},{9,1},{... | collective-permute-start | bytes 786440 | tf_op jit(solution)/shard_map/ppermute | solution.py:48
  57.3 2.7 %collective-permute-start.25 = (bf16[8,128,128]{2,1,0:T(8,128)(2,1)S(1)}, bf16[8,128,128]{2,1,0:T(8,128)(2,1)S(1)}, u32[]{:S(2)}, u32[]{:S(2)}) collective-permute-start(bf16[8,128,128]{2,1,0:T(8,128)(2,1)S(1)} %pad_maximum_fusion.1.rest_0_), channel_id=1, source_target_pairs={{0,1},{1,0},{2,3},{3,2},{4,5},{5,4},{6,7},{7,6},{8,9},{9,8},{10,11... | collective-permute-start | bytes 786440 | tf_op jit(solution)/shard_map/ppermute | solution.py:48
  60.0 1.3 %collective-permute-start = (bf16[1024,512]{1,0:T(8,128)(2,1)S(1)}, bf16[1024,512]{1,0:T(8,128)(2,1)S(1)}, u32[]{:S(2)}, u32[]{:S(2)}) collective-permute-start(bf16[1024,512]{1,0:T(8,128)(2,1)S(1)} %order.3), channel_id=1, source_target_pairs={{0,1},{1,0},{2,3},{3,2},{4,5},{5,4},{6,7},{7,6},{8,9},{9,8},{10,11... | collective-permute-start | bytes 3145736 | tf_op jit(solution)/shard_map/ppermute | solution.py:48
  61.3 1.5 %collective-permute-start.30 = (bf16[8,128,128]{2,1,0:T(8,128)(2,1)S(1)}, bf16[8,128,128]{2,1,0:T(8,128)(2,1)S(1)}, u32[]{:S(2)}, u32[]{:S(2)}) collective-permute-start(bf16[8,128,128]{2,1,0:T(8,128)(2,1)S(1)} %collective-permute-done.24.rest_5_), channel_id=1, source_target_pairs={{0,1},{1,0},{2,3},{3,2},{4,5},{5,4},{6,7},{7,6},{8,9},{9,8},{10,11... | collective-permute-start | bytes 786440 | tf_op jit(solution)/shard_map/ppermute | solution.py:48
  62.8 1.2 %collective-permute-done.23.rest_4_ = bf16[8,128,128]{2,1,0:T(8,128)(2,1)S(1)} collective-permute-done((bf16[8,128,128]{2,1,0:T(8,128)(2,1)S(1)}, bf16[8,128,128]{2,1,0:T(8,128)(2,1)S(1)}, u32[]{:S(2)}, u32[]{:S(2)}) %collective-permute-start.23) | collective-permute-done | bytes 262176 | tf_op jit(solution)/shard_map/ppermute | solution.py:48
  64.0 0.6 collective-permute-start.27
  64.6 1.6 %collective-permute-start.32 = (bf16[8,128,128]{2,1,0:T(8,128)(2,1)S(1)}, bf16[8,128,128]{2,1,0:T(8,128)(2,1)S(1)}, u32[]{:S(2)}, u32[]{:S(2)}) collective-permute-start(bf16[8,128,128]{2,1,0:T(8,128)(2,1)S(1)} %collective-permute-done.22.rest_3_), channel_id=1, source_target_pairs={{0,6},{1,25},{2,0},{3,27},{4,2},{5,29},{6,4},{7,31},{8,14},{9,1},{... | collective-permute-start | bytes 786440 | tf_op jit(solution)/shard_map/ppermute | solution.py:48
  66.3 2.9 %early.3.before = f32[4,128,128]{2,1,0:T(8,128)S(1)} custom-call(s32[1,1152]{1,0:T(1,128)S(1)} %get-tuple-element.22.lists, s32[1,256]{1,0:T(1,128)S(1)} %get-tuple-element.23.groups, s32[1,128]{1,0:T(1,128)S(1)} %get-tuple-element.24.sizes, bf16[128,128,128]{2,1,0:T(8,128)(2,1)S(1)} %copy-done.2, bf16[4,128,128]{2,1,0:T(8,128)(2,1)S(1)} %copy-done.3, ...), custom_call_target="tpu_custom_call" | custom-call | flops 2000000000 | bytes 8000000 | tf_op jit(solution)/shard_map/early/pallas_call | solution.py:319
  69.2 1.1 collective-permute-done.32.rest_1_
  70.2 2.6 %collective-permute-done.31.rest_0_ = bf16[8,128,128]{2,1,0:T(8,128)(2,1)S(1)} collective-permute-done((bf16[8,128,128]{2,1,0:T(8,128)(2,1)S(1)}, bf16[8,128,128]{2,1,0:T(8,128)(2,1)S(1)}, u32[]{:S(2)}, u32[]{:S(2)}) %collective-permute-start.31) | collective-permute-done | bytes 262176 | tf_op jit(solution)/shard_map/ppermute | solution.py:48
  72.8 0.4 collective-permute-start.33
  73.3 1.0 collective-permute-done.33.rest_2_
  74.7 1.7 %late.3 = bf16[4,128,128]{2,1,0:T(8,128)(2,1)S(1)} custom-call(s32[1,1152]{1,0:T(1,128)S(1)} %get-tuple-element.22.lists, s32[1,256]{1,0:T(1,128)S(1)} %get-tuple-element.23.groups, s32[1,128]{1,0:T(1,128)S(1)} %get-tuple-element.24.sizes, bf16[128,128,128]{2,1,0:T(8,128)(2,1)S(1)} %copy-done.2, f32[4,128,128]{2,1,0:T(8,128)S(1)} %early.3.before, ...), custom_call_target="tpu_custom_call" | custom-call | tf_op jit(solution)/shard_map/late/pallas_call | solution.py:334
  76.4 1.6 %collective-permute-start.35 = (bf16[4,128,128]{2,1,0:T(8,128)(2,1)S(1)}, bf16[4,128,128]{2,1,0:T(8,128)(2,1)S(1)}, u32[]{:S(2)}, u32[]{:S(2)}) collective-permute-start(bf16[4,128,128]{2,1,0:T(8,128)(2,1)S(1)} %late.3), channel_id=1, source_target_pairs={{0,1},{1,0},{2,3},{3,2},{4,5},{5,4},{6,7},{7,6},{8,9},{9,8},{10,11... | collective-permute-start | bytes 393224 | tf_op jit(solution)/shard_map/ppermute | solution.py:48
  78.0 1.0 collective-permute-done.35
  79.0 1.1 %far.1 = bf16[1024,128]{1,0:T(8,128)(2,1)S(1)} custom-call(bf16[1024,512]{1,0:T(8,128)(2,1)S(1)} %order.2.mine, bf16[1024,512]{1,0:T(8,128)(2,1)S(1)} %collective-permute-done.other, bf16[512,128]{1,0:T(8,128)(2,1)S(1)} %bitcast.9, bf16[512,128]{1,0:T(8,128)(2,1)S(1)} %bitcast.10), custom_call_target="tpu_custom_call" | custom-call | tf_op jit(solution)/shard_map/far/pallas_call | solution.py:252
  80.2 25.0 %all_to_all.5 = bf16[128,8,128]{2,1,0:T(8,128)(2,1)S(1)} all-to-all(bf16[128,8,128]{2,1,0:T(8,128)(2,1)S(1)} %bitcast.8), channel_id=1, replica_groups={{0,2,4,6,8,10,12,14,16,18,20,22,24,26,28,30,32,34,36,38,40,42,44,46,48,..., dimensions={0} | all-to-all | bytes 524288 | tf_op jit(solution)/shard_map/all_to_all | solution.py:391
  105.1 0.7 convert_reduce_fusion
  (66 shorter events, 2.1 us)
Async XLA Ops:
  1.1 14.1 %collective-permute-start.1 = (bf16[4,128,128]{2,1,0:T(8,128)(2,1)S(1)}, bf16[4,128,128]{2,1,0:T(8,128)(2,1)S(1)}, u32[]{:S(2)}, u32[]{:S(2)}) collective-permute-start(bf16[4,128,128]{2,1,0:T(8,128)(2,1)S(1)} %convolution_convert_fusion), channel_id=1, source_target_pairs={{0,16},{1,5},{2,18},{3,7},{4,20},{5,1},{6,22},{7,3},{8,24},{9,13},... | collective-permute-start | bytes 393224 | tf_op jit(solution)/shard_map/ppermute | solution.py:48
  5.0 10.3 %collective-permute-start.2 = (bf16[4,128,128]{2,1,0:T(8,128)(2,1)S(1)}, bf16[4,128,128]{2,1,0:T(8,128)(2,1)S(1)}, u32[]{:S(2)}, u32[]{:S(2)}) collective-permute-start(bf16[4,128,128]{2,1,0:T(8,128)(2,1)S(1)} %convolution_convert_fusion), channel_id=1, source_target_pairs={{0,8},{1,3},{2,10},{3,5},{4,12},{5,7},{6,14},{7,1},{8,16},{9,11},{... | collective-permute-start | bytes 393224 | tf_op jit(solution)/shard_map/ppermute | solution.py:48
  5.4 9.9 %collective-permute-start.3 = (bf16[4,128,128]{2,1,0:T(8,128)(2,1)S(1)}, bf16[4,128,128]{2,1,0:T(8,128)(2,1)S(1)}, u32[]{:S(2)}, u32[]{:S(2)}) collective-permute-start(bf16[4,128,128]{2,1,0:T(8,128)(2,1)S(1)} %convolution_convert_fusion), channel_id=1, source_target_pairs={{0,24},{1,7},{2,26},{3,1},{4,28},{5,3},{6,30},{7,5},{8,0},{9,15},{... | collective-permute-start | bytes 393224 | tf_op jit(solution)/shard_map/ppermute | solution.py:48
  8.6 4.9 %copy-start.8 = (s32[1,32,4]{1,2,0:T(4,128)S(1)}, s32[1,32,4]{1,2,0:T(4,128)}, u32[]{:S(2)}) copy-start(s32[1,32,4]{1,2,0:T(4,128)} %param.14) | copy-start | bytes 1540
  8.6 5.8 %copy-start.5 = (s32[1,512]{1,0:T(1,128)S(1)}, s32[1,512]{1,0:T(1,128)}, u32[]{:S(2)}) copy-start(s32[1,512]{1,0:T(1,128)} %src.1) | copy-start | bytes 6148
  8.6 5.8 %copy-start.6 = (s32[1,512]{1,0:T(1,128)S(1)}, s32[1,512]{1,0:T(1,128)}, u32[]{:S(2)}) copy-start(s32[1,512]{1,0:T(1,128)} %tgt.1) | copy-start | bytes 6148
  8.6 5.8 %copy-start.7 = (s32[1,512]{1,0:T(1,128)S(1)}, s32[1,512]{1,0:T(1,128)}, u32[]{:S(2)}) copy-start(s32[1,512]{1,0:T(1,128)} %blk.1) | copy-start | bytes 6148
  13.4 18.7 %copy-start.3 = (bf16[4,128,128]{2,1,0:T(8,128)(2,1)S(1)}, bf16[4,128,128]{2,1,0:T(8,128)(2,1)}, u32[]{:S(2)}) copy-start(bf16[4,128,128]{2,1,0:T(8,128)(2,1)} %incident.3) | copy-start | bytes 393220
  13.5 18.6 %copy-start = (bf16[128,128,128]{2,1,0:T(8,128)(2,1)S(1)}, bf16[128,128,128]{2,1,0:T(8,128)(2,1)}, u32[]{:S(2)}) copy-start(bf16[128,128,128]{2,1,0:T(8,128)(2,1)} %blocks.7) | copy-start | bytes 12582916
  15.3 6.0 %collective-permute-start.5 = (bf16[8,128,128]{2,1,0:T(8,128)(2,1)S(1)}, bf16[8,128,128]{2,1,0:T(8,128)(2,1)S(1)}, u32[]{:S(2)}, u32[]{:S(2)}) collective-permute-start(bf16[8,128,128]{2,1,0:T(8,128)(2,1)S(1)} %constant_dynamic-update-slice_fusion.rest_1_), channel_id=1, source_target_pairs={{0,6},{1,25},{2,0},{3,27},{4,2},{5,29},{6,4},{7,31},{8,14},{9,1},{... | collective-permute-start | bytes 786440 | tf_op jit(solution)/shard_map/ppermute | solution.py:48
  17.8 6.7 %collective-permute-start.7 = (bf16[8,128,128]{2,1,0:T(8,128)(2,1)S(1)}, bf16[8,128,128]{2,1,0:T(8,128)(2,1)S(1)}, u32[]{:S(2)}, u32[]{:S(2)}) collective-permute-start(bf16[8,128,128]{2,1,0:T(8,128)(2,1)S(1)} %constant_dynamic-update-slice_fusion.rest_1_), channel_id=1, source_target_pairs={{0,2},{1,9},{2,4},{3,11},{4,6},{5,13},{6,0},{7,15},{8,10},{9,17},{... | collective-permute-start | bytes 786440 | tf_op jit(solution)/shard_map/ppermute | solution.py:48
  17.8 9.5 %collective-permute-start.9 = (bf16[8,128,128]{2,1,0:T(8,128)(2,1)S(1)}, bf16[8,128,128]{2,1,0:T(8,128)(2,1)S(1)}, u32[]{:S(2)}, u32[]{:S(2)}) collective-permute-start(bf16[8,128,128]{2,1,0:T(8,128)(2,1)S(1)} %constant_dynamic-update-slice_fusion.rest_1_), channel_id=1, source_target_pairs={{0,1},{1,0},{2,3},{3,2},{4,5},{5,4},{6,7},{7,6},{8,9},{9,8},{10,11... | collective-permute-start | bytes 786440 | tf_op jit(solution)/shard_map/ppermute | solution.py:48
  19.8 20.6 %copy-start.4 = (bf16[4,128,128]{2,1,0:T(8,128)(2,1)S(1)}, bf16[4,128,128]{2,1,0:T(8,128)(2,1)}, u32[]{:S(2)}) copy-start(bf16[4,128,128]{2,1,0:T(8,128)(2,1)} %tmatrix.3) | copy-start | bytes 393220
  19.8 7.6 %collective-permute-start.4 = (bf16[8,128,128]{2,1,0:T(8,128)(2,1)S(1)}, bf16[8,128,128]{2,1,0:T(8,128)(2,1)S(1)}, u32[]{:S(2)}, u32[]{:S(2)}) collective-permute-start(bf16[8,128,128]{2,1,0:T(8,128)(2,1)S(1)} %pad_maximum_fusion.rest_0_), channel_id=1, source_target_pairs={{0,6},{1,25},{2,0},{3,27},{4,2},{5,29},{6,4},{7,31},{8,14},{9,1},{... | collective-permute-start | bytes 786440 | tf_op jit(solution)/shard_map/ppermute | solution.py:48
  20.6 7.2 %collective-permute-start.6 = (bf16[8,128,128]{2,1,0:T(8,128)(2,1)S(1)}, bf16[8,128,128]{2,1,0:T(8,128)(2,1)S(1)}, u32[]{:S(2)}, u32[]{:S(2)}) collective-permute-start(bf16[8,128,128]{2,1,0:T(8,128)(2,1)S(1)} %pad_maximum_fusion.rest_0_), channel_id=1, source_target_pairs={{0,2},{1,9},{2,4},{3,11},{4,6},{5,13},{6,0},{7,15},{8,10},{9,17},{... | collective-permute-start | bytes 786440 | tf_op jit(solution)/shard_map/ppermute | solution.py:48
  21.3 9.4 %collective-permute-start.8 = (bf16[8,128,128]{2,1,0:T(8,128)(2,1)S(1)}, bf16[8,128,128]{2,1,0:T(8,128)(2,1)S(1)}, u32[]{:S(2)}, u32[]{:S(2)}) collective-permute-start(bf16[8,128,128]{2,1,0:T(8,128)(2,1)S(1)} %pad_maximum_fusion.rest_0_), channel_id=1, source_target_pairs={{0,1},{1,0},{2,3},{3,2},{4,5},{5,4},{6,7},{7,6},{8,9},{9,8},{10,11... | collective-permute-start | bytes 786440 | tf_op jit(solution)/shard_map/ppermute | solution.py:48
  24.6 6.1 %collective-permute-start.11 = (bf16[8,128,128]{2,1,0:T(8,128)(2,1)S(1)}, bf16[8,128,128]{2,1,0:T(8,128)(2,1)S(1)}, u32[]{:S(2)}, u32[]{:S(2)}) collective-permute-start(bf16[8,128,128]{2,1,0:T(8,128)(2,1)S(1)} %collective-permute-done.5.rest_3_), channel_id=1, source_target_pairs={{0,1},{1,0},{2,3},{3,2},{4,5},{5,4},{6,7},{7,6},{8,9},{9,8},{10,11... | collective-permute-start | bytes 786440 | tf_op jit(solution)/shard_map/ppermute | solution.py:48
  27.3 4.8 %collective-permute-start.13 = (bf16[8,128,128]{2,1,0:T(8,128)(2,1)S(1)}, bf16[8,128,128]{2,1,0:T(8,128)(2,1)S(1)}, u32[]{:S(2)}, u32[]{:S(2)}) collective-permute-start(bf16[8,128,128]{2,1,0:T(8,128)(2,1)S(1)} %collective-permute-done.7.rest_5_), channel_id=1, source_target_pairs={{0,1},{1,0},{2,3},{3,2},{4,5},{5,4},{6,7},{7,6},{8,9},{9,8},{10,11... | collective-permute-start | bytes 786440 | tf_op jit(solution)/shard_map/ppermute | solution.py:48
  27.3 4.8 %collective-permute-start.10 = (bf16[8,128,128]{2,1,0:T(8,128)(2,1)S(1)}, bf16[8,128,128]{2,1,0:T(8,128)(2,1)S(1)}, u32[]{:S(2)}, u32[]{:S(2)}) collective-permute-start(bf16[8,128,128]{2,1,0:T(8,128)(2,1)S(1)} %collective-permute-done.4.rest_2_), channel_id=1, source_target_pairs={{0,1},{1,0},{2,3},{3,2},{4,5},{5,4},{6,7},{7,6},{8,9},{9,8},{10,11... | collective-permute-start | bytes 786440 | tf_op jit(solution)/shard_map/ppermute | solution.py:48
  27.8 4.3 %collective-permute-start.12 = (bf16[8,128,128]{2,1,0:T(8,128)(2,1)S(1)}, bf16[8,128,128]{2,1,0:T(8,128)(2,1)S(1)}, u32[]{:S(2)}, u32[]{:S(2)}) collective-permute-start(bf16[8,128,128]{2,1,0:T(8,128)(2,1)S(1)} %collective-permute-done.6.rest_4_), channel_id=1, source_target_pairs={{0,1},{1,0},{2,3},{3,2},{4,5},{5,4},{6,7},{7,6},{8,9},{9,8},{10,11... | collective-permute-start | bytes 786440 | tf_op jit(solution)/shard_map/ppermute | solution.py:48
  30.7 5.5 %collective-permute-start.15 = (bf16[8,128,128]{2,1,0:T(8,128)(2,1)S(1)}, bf16[8,128,128]{2,1,0:T(8,128)(2,1)S(1)}, u32[]{:S(2)}, u32[]{:S(2)}) collective-permute-start(bf16[8,128,128]{2,1,0:T(8,128)(2,1)S(1)} %collective-permute-done.5.rest_3_), channel_id=1, source_target_pairs={{0,6},{1,25},{2,0},{3,27},{4,2},{5,29},{6,4},{7,31},{8,14},{9,1},{... | collective-permute-start | bytes 786440 | tf_op jit(solution)/shard_map/ppermute | solution.py:48
  30.7 7.0 %collective-permute-start.14 = (bf16[8,128,128]{2,1,0:T(8,128)(2,1)S(1)}, bf16[8,128,128]{2,1,0:T(8,128)(2,1)S(1)}, u32[]{:S(2)}, u32[]{:S(2)}) collective-permute-start(bf16[8,128,128]{2,1,0:T(8,128)(2,1)S(1)} %collective-permute-done.6.rest_4_), channel_id=1, source_target_pairs={{0,2},{1,9},{2,4},{3,11},{4,6},{5,13},{6,0},{7,15},{8,10},{9,17},{... | collective-permute-start | bytes 786440 | tf_op jit(solution)/shard_map/ppermute | solution.py:48
  37.7 2.3 %collective-permute-start.16 = (bf16[8,128,128]{2,1,0:T(8,128)(2,1)S(1)}, bf16[8,128,128]{2,1,0:T(8,128)(2,1)S(1)}, u32[]{:S(2)}, u32[]{:S(2)}) collective-permute-start(bf16[8,128,128]{2,1,0:T(8,128)(2,1)S(1)} %collective-permute-done.14.rest_0_), channel_id=1, source_target_pairs={{0,1},{1,0},{2,3},{3,2},{4,5},{5,4},{6,7},{7,6},{8,9},{9,8},{10,11... | collective-permute-start | bytes 786440 | tf_op jit(solution)/shard_map/ppermute | solution.py:48
  38.8 1.5 %collective-permute-start.17 = (bf16[8,128,128]{2,1,0:T(8,128)(2,1)S(1)}, bf16[8,128,128]{2,1,0:T(8,128)(2,1)S(1)}, u32[]{:S(2)}, u32[]{:S(2)}) collective-permute-start(bf16[8,128,128]{2,1,0:T(8,128)(2,1)S(1)} %collective-permute-done.15.rest_1_), channel_id=1, source_target_pairs={{0,1},{1,0},{2,3},{3,2},{4,5},{5,4},{6,7},{7,6},{8,9},{9,8},{10,11... | collective-permute-start | bytes 786440 | tf_op jit(solution)/shard_map/ppermute | solution.py:48
  40.3 2.2 %copy-start.1 = (bf16[128,128,128]{2,1,0:T(8,128)(2,1)S(1)}, bf16[128,128,128]{2,1,0:T(8,128)(2,1)}, u32[]{:S(2)}) copy-start(bf16[128,128,128]{2,1,0:T(8,128)(2,1)} %blocks.7) | copy-start | bytes 12582916
  44.2 22.1 %copy-start.2 = (bf16[128,128,128]{2,1,0:T(8,128)(2,1)S(1)}, bf16[128,128,128]{2,1,0:T(8,128)(2,1)}, u32[]{:S(2)}) copy-start(bf16[128,128,128]{2,1,0:T(8,128)(2,1)} %blocks.7) | copy-start | bytes 12582916
  44.2 6.9 %collective-permute-start.18 = (bf16[4,128,128]{2,1,0:T(8,128)(2,1)S(1)}, bf16[4,128,128]{2,1,0:T(8,128)(2,1)S(1)}, u32[]{:S(2)}, u32[]{:S(2)}) collective-permute-start(bf16[4,128,128]{2,1,0:T(8,128)(2,1)S(1)} %late.2), channel_id=1, source_target_pairs={{0,16},{1,5},{2,18},{3,7},{4,20},{5,1},{6,22},{7,3},{8,24},{9,13},... | collective-permute-start | bytes 393224 | tf_op jit(solution)/shard_map/ppermute | solution.py:48
  44.3 6.8 %collective-permute-start.19 = (bf16[4,128,128]{2,1,0:T(8,128)(2,1)S(1)}, bf16[4,128,128]{2,1,0:T(8,128)(2,1)S(1)}, u32[]{:S(2)}, u32[]{:S(2)}) collective-permute-start(bf16[4,128,128]{2,1,0:T(8,128)(2,1)S(1)} %late.2), channel_id=1, source_target_pairs={{0,8},{1,3},{2,10},{3,5},{4,12},{5,7},{6,14},{7,1},{8,16},{9,11},{... | collective-permute-start | bytes 393224 | tf_op jit(solution)/shard_map/ppermute | solution.py:48
  44.8 6.4 %collective-permute-start.20 = (bf16[4,128,128]{2,1,0:T(8,128)(2,1)S(1)}, bf16[4,128,128]{2,1,0:T(8,128)(2,1)S(1)}, u32[]{:S(2)}, u32[]{:S(2)}) collective-permute-start(bf16[4,128,128]{2,1,0:T(8,128)(2,1)S(1)} %late.2), channel_id=1, source_target_pairs={{0,24},{1,7},{2,26},{3,1},{4,28},{5,3},{6,30},{7,5},{8,0},{9,15},{... | collective-permute-start | bytes 393224 | tf_op jit(solution)/shard_map/ppermute | solution.py:48
  51.2 6.1 %collective-permute-start.22 = (bf16[8,128,128]{2,1,0:T(8,128)(2,1)S(1)}, bf16[8,128,128]{2,1,0:T(8,128)(2,1)S(1)}, u32[]{:S(2)}, u32[]{:S(2)}) collective-permute-start(bf16[8,128,128]{2,1,0:T(8,128)(2,1)S(1)} %constant_dynamic-update-slice_fusion.2.rest_1_), channel_id=1, source_target_pairs={{0,6},{1,25},{2,0},{3,27},{4,2},{5,29},{6,4},{7,31},{8,14},{9,1},{... | collective-permute-start | bytes 786440 | tf_op jit(solution)/shard_map/ppermute | solution.py:48
  51.3 8.6 %collective-permute-start.24 = (bf16[8,128,128]{2,1,0:T(8,128)(2,1)S(1)}, bf16[8,128,128]{2,1,0:T(8,128)(2,1)S(1)}, u32[]{:S(2)}, u32[]{:S(2)}) collective-permute-start(bf16[8,128,128]{2,1,0:T(8,128)(2,1)S(1)} %constant_dynamic-update-slice_fusion.2.rest_1_), channel_id=1, source_target_pairs={{0,2},{1,9},{2,4},{3,11},{4,6},{5,13},{6,0},{7,15},{8,10},{9,17},{... | collective-permute-start | bytes 786440 | tf_op jit(solution)/shard_map/ppermute | solution.py:48
  52.8 8.5 %collective-permute-start.26 = (bf16[8,128,128]{2,1,0:T(8,128)(2,1)S(1)}, bf16[8,128,128]{2,1,0:T(8,128)(2,1)S(1)}, u32[]{:S(2)}, u32[]{:S(2)}) collective-permute-start(bf16[8,128,128]{2,1,0:T(8,128)(2,1)S(1)} %constant_dynamic-update-slice_fusion.2.rest_1_), channel_id=1, source_target_pairs={{0,1},{1,0},{2,3},{3,2},{4,5},{5,4},{6,7},{7,6},{8,9},{9,8},{10,11... | collective-permute-start | bytes 786440 | tf_op jit(solution)/shard_map/ppermute | solution.py:48
  55.6 5.6 %collective-permute-start.21 = (bf16[8,128,128]{2,1,0:T(8,128)(2,1)S(1)}, bf16[8,128,128]{2,1,0:T(8,128)(2,1)S(1)}, u32[]{:S(2)}, u32[]{:S(2)}) collective-permute-start(bf16[8,128,128]{2,1,0:T(8,128)(2,1)S(1)} %pad_maximum_fusion.1.rest_0_), channel_id=1, source_target_pairs={{0,6},{1,25},{2,0},{3,27},{4,2},{5,29},{6,4},{7,31},{8,14},{9,1},{... | collective-permute-start | bytes 786440 | tf_op jit(solution)/shard_map/ppermute | solution.py:48
  57.3 6.7 %collective-permute-start.23 = (bf16[8,128,128]{2,1,0:T(8,128)(2,1)S(1)}, bf16[8,128,128]{2,1,0:T(8,128)(2,1)S(1)}, u32[]{:S(2)}, u32[]{:S(2)}) collective-permute-start(bf16[8,128,128]{2,1,0:T(8,128)(2,1)S(1)} %pad_maximum_fusion.1.rest_0_), channel_id=1, source_target_pairs={{0,2},{1,9},{2,4},{3,11},{4,6},{5,13},{6,0},{7,15},{8,10},{9,17},{... | collective-permute-start | bytes 786440 | tf_op jit(solution)/shard_map/ppermute | solution.py:48
  57.3 7.3 %collective-permute-start.25 = (bf16[8,128,128]{2,1,0:T(8,128)(2,1)S(1)}, bf16[8,128,128]{2,1,0:T(8,128)(2,1)S(1)}, u32[]{:S(2)}, u32[]{:S(2)}) collective-permute-start(bf16[8,128,128]{2,1,0:T(8,128)(2,1)S(1)} %pad_maximum_fusion.1.rest_0_), channel_id=1, source_target_pairs={{0,1},{1,0},{2,3},{3,2},{4,5},{5,4},{6,7},{7,6},{8,9},{9,8},{10,11... | collective-permute-start | bytes 786440 | tf_op jit(solution)/shard_map/ppermute | solution.py:48
  60.0 18.1 %collective-permute-start = (bf16[1024,512]{1,0:T(8,128)(2,1)S(1)}, bf16[1024,512]{1,0:T(8,128)(2,1)S(1)}, u32[]{:S(2)}, u32[]{:S(2)}) collective-permute-start(bf16[1024,512]{1,0:T(8,128)(2,1)S(1)} %order.3), channel_id=1, source_target_pairs={{0,1},{1,0},{2,3},{3,2},{4,5},{5,4},{6,7},{7,6},{8,9},{9,8},{10,11... | collective-permute-start | bytes 3145736 | tf_op jit(solution)/shard_map/ppermute | solution.py:48
  61.3 3.4 %collective-permute-start.28 = (bf16[8,128,128]{2,1,0:T(8,128)(2,1)S(1)}, bf16[8,128,128]{2,1,0:T(8,128)(2,1)S(1)}, u32[]{:S(2)}, u32[]{:S(2)}) collective-permute-start(bf16[8,128,128]{2,1,0:T(8,128)(2,1)S(1)} %collective-permute-done.22.rest_3_), channel_id=1, source_target_pairs={{0,1},{1,0},{2,3},{3,2},{4,5},{5,4},{6,7},{7,6},{8,9},{9,8},{10,11... | collective-permute-start | bytes 786440 | tf_op jit(solution)/shard_map/ppermute | solution.py:48
  61.3 5.0 %collective-permute-start.30 = (bf16[8,128,128]{2,1,0:T(8,128)(2,1)S(1)}, bf16[8,128,128]{2,1,0:T(8,128)(2,1)S(1)}, u32[]{:S(2)}, u32[]{:S(2)}) collective-permute-start(bf16[8,128,128]{2,1,0:T(8,128)(2,1)S(1)} %collective-permute-done.24.rest_5_), channel_id=1, source_target_pairs={{0,1},{1,0},{2,3},{3,2},{4,5},{5,4},{6,7},{7,6},{8,9},{9,8},{10,11... | collective-permute-start | bytes 786440 | tf_op jit(solution)/shard_map/ppermute | solution.py:48
  64.0 2.3 %collective-permute-start.27 = (bf16[8,128,128]{2,1,0:T(8,128)(2,1)S(1)}, bf16[8,128,128]{2,1,0:T(8,128)(2,1)S(1)}, u32[]{:S(2)}, u32[]{:S(2)}) collective-permute-start(bf16[8,128,128]{2,1,0:T(8,128)(2,1)S(1)} %collective-permute-done.21.rest_2_), channel_id=1, source_target_pairs={{0,1},{1,0},{2,3},{3,2},{4,5},{5,4},{6,7},{7,6},{8,9},{9,8},{10,11... | collective-permute-start | bytes 786440 | tf_op jit(solution)/shard_map/ppermute | solution.py:48
  64.6 1.6 %collective-permute-start.29 = (bf16[8,128,128]{2,1,0:T(8,128)(2,1)S(1)}, bf16[8,128,128]{2,1,0:T(8,128)(2,1)S(1)}, u32[]{:S(2)}, u32[]{:S(2)}) collective-permute-start(bf16[8,128,128]{2,1,0:T(8,128)(2,1)S(1)} %collective-permute-done.23.rest_4_), channel_id=1, source_target_pairs={{0,1},{1,0},{2,3},{3,2},{4,5},{5,4},{6,7},{7,6},{8,9},{9,8},{10,11... | collective-permute-start | bytes 786440 | tf_op jit(solution)/shard_map/ppermute | solution.py:48
  64.6 5.6 %collective-permute-start.32 = (bf16[8,128,128]{2,1,0:T(8,128)(2,1)S(1)}, bf16[8,128,128]{2,1,0:T(8,128)(2,1)S(1)}, u32[]{:S(2)}, u32[]{:S(2)}) collective-permute-start(bf16[8,128,128]{2,1,0:T(8,128)(2,1)S(1)} %collective-permute-done.22.rest_3_), channel_id=1, source_target_pairs={{0,6},{1,25},{2,0},{3,27},{4,2},{5,29},{6,4},{7,31},{8,14},{9,1},{... | collective-permute-start | bytes 786440 | tf_op jit(solution)/shard_map/ppermute | solution.py:48
  66.3 6.5 %collective-permute-start.31 = (bf16[8,128,128]{2,1,0:T(8,128)(2,1)S(1)}, bf16[8,128,128]{2,1,0:T(8,128)(2,1)S(1)}, u32[]{:S(2)}, u32[]{:S(2)}) collective-permute-start(bf16[8,128,128]{2,1,0:T(8,128)(2,1)S(1)} %collective-permute-done.23.rest_4_), channel_id=1, source_target_pairs={{0,2},{1,9},{2,4},{3,11},{4,6},{5,13},{6,0},{7,15},{8,10},{9,17},{... | collective-permute-start | bytes 786440 | tf_op jit(solution)/shard_map/ppermute | solution.py:48
  72.8 1.6 %collective-permute-start.33 = (bf16[8,128,128]{2,1,0:T(8,128)(2,1)S(1)}, bf16[8,128,128]{2,1,0:T(8,128)(2,1)S(1)}, u32[]{:S(2)}, u32[]{:S(2)}) collective-permute-start(bf16[8,128,128]{2,1,0:T(8,128)(2,1)S(1)} %collective-permute-done.31.rest_0_), channel_id=1, source_target_pairs={{0,1},{1,0},{2,3},{3,2},{4,5},{5,4},{6,7},{7,6},{8,9},{9,8},{10,11... | collective-permute-start | bytes 786440 | tf_op jit(solution)/shard_map/ppermute | solution.py:48
  73.2 1.5 %collective-permute-start.34 = (bf16[8,128,128]{2,1,0:T(8,128)(2,1)S(1)}, bf16[8,128,128]{2,1,0:T(8,128)(2,1)S(1)}, u32[]{:S(2)}, u32[]{:S(2)}) collective-permute-start(bf16[8,128,128]{2,1,0:T(8,128)(2,1)S(1)} %collective-permute-done.32.rest_1_), channel_id=1, source_target_pairs={{0,1},{1,0},{2,3},{3,2},{4,5},{5,4},{6,7},{7,6},{8,9},{9,8},{10,11... | collective-permute-start | bytes 786440 | tf_op jit(solution)/shard_map/ppermute | solution.py:48
  76.4 2.6 %collective-permute-start.35 = (bf16[4,128,128]{2,1,0:T(8,128)(2,1)S(1)}, bf16[4,128,128]{2,1,0:T(8,128)(2,1)S(1)}, u32[]{:S(2)}, u32[]{:S(2)}) collective-permute-start(bf16[4,128,128]{2,1,0:T(8,128)(2,1)S(1)} %late.3), channel_id=1, source_target_pairs={{0,1},{1,0},{2,3},{3,2},{4,5},{5,4},{6,7},{7,6},{8,9},{9,8},{10,11... | collective-permute-start | bytes 393224 | tf_op jit(solution)/shard_map/ppermute | solution.py:48

commit v5 on v4

--- a/solution.py
+++ b/solution.py
@@ -56,11 +56,11 @@
     return lax.optimization_barrier((values, fillers))[0]
 
 
-def spread(coeff, *fillers):
+def spread(coeff, fill_first, fill_second):
     first2 = send(coeff, along_first(2))
     first3 = send(coeff, along_first(1))
     first1 = send(coeff, along_first(-1))
-    first2, first3, first1 = together((first2, first3, first1), *fillers)
+    first2, first3, first1 = together((first2, first3, first1), *fill_first)
     low = jnp.concatenate([coeff, first1])
     high = jnp.concatenate([first2, first3])
     low3 = send(low, along_second(1))
@@ -69,10 +69,9 @@
     low1 = send(low, along_second(-1))
     low2 = send(low3, along_second(1))
     high2 = send(high1, along_second(-1))
+    high3, low1 = together((high3, low1), *fill_second)
     near = (low, high, low1, high1, low3, high3)
-    other = (send(low, SWAP), send(high, SWAP))
-    other += tuple(send(piece, SWAP) for piece in near[2:])
-    return near, other, (low2, high2)
+    return near, tuple(send(piece, SWAP) for piece in near), (low2, high2)
 
 
 def swapped(pieces, before):
@@ -101,8 +100,8 @@
 def plan_kernel(me, count, need, src, tgt, blk, words, groups, sizes):
     source = src[...]
     peer, request = source >> 2, source & 3
-    from_peer = ones_where(counted((need.shape[0], PAIRS), 0) == peer)
-    choices = dot(need[...].astype(jnp.float32).astype(jnp.bfloat16), from_peer, ((0,), (0,)))
+    from_peer = ones_where(counted((need.shape[1], PAIRS), 0) == peer)
+    choices = dot(need[...].astype(jnp.float32).astype(jnp.bfloat16), from_peer)
     sphere = jnp.zeros((1, PAIRS), jnp.float32)
     for k in range(OWN):
         sphere = jnp.where(request == k, choices[k : k + 1, :], sphere)
@@ -165,7 +164,7 @@
         out_specs=(VMEM,) * 3,
         compiler_params=LIMIT,
         cost_estimate=pl.CostEstimate(
-            flops=1_000_000_000, bytes_accessed=1_000_000, transcendentals=0
+            flops=8_000_000_000, bytes_accessed=1_000_000, transcendentals=0
         ),
         name="plan",
     )(me, count, need, src, tgt, blk)
@@ -236,6 +235,7 @@
 
 
 FAR_ROWS = 256
+HALF = TILE // 2
 
 
 def far_kernel(mine, other, coeff, arrived, far):
@@ -259,11 +259,13 @@
     )(mine, other, coeff.reshape(-1, TILE), arrived.reshape(-1, TILE))
 
 
-def order_kernel(order, factor_far, harmonics, ordered, right, factor, sems):
+def order_kernel(which, owner_far, factor_far, harmonics, ordered, right, owner, factor, sems):
     first = pltpu.make_async_copy(factor_far, factor, sems.at[0])
     first.start()
     copy = pltpu.make_async_copy(harmonics, right.at[:, pl.ds(0, TILE)], sems.at[1])
     copy.start()
+    last = pltpu.make_async_copy(owner_far, owner, sems.at[2])
+    last.start()
     first.wait()
     for i in range(right.shape[0] // FAR_ROWS):
         rows = pl.ds(i * FAR_ROWS, FAR_ROWS)
@@ -275,12 +277,20 @@
         parts = jnp.concatenate([parts, jnp.zeros((FAR_ROWS, TILE - 4 * OWN), jnp.float32)], axis=1)
         right[rows, TILE:] = parts.astype(jnp.bfloat16)
     copy.wait()
+    last.wait()
 
     def chunk(i, carry):
         rows = pl.ds(pl.multiple_of(i * FAR_ROWS, FAR_ROWS), FAR_ROWS)
-        wanted = jnp.broadcast_to(order[rows, :], (FAR_ROWS, right.shape[0]))
-        pick = ones_where(wanted == counted(wanted.shape, 1))
-        found = dot(pick, right[...])
+        wanted = []
+        for n in range(FAR_ROWS // HALF):
+            line = owner[pl.ds(i * (FAR_ROWS // HALF) + n, 1), :]
+            both = jnp.broadcast_to(line, (TILE, TILE)).T.reshape(HALF // 8, 2, 8, TILE)
+            mine = jnp.where(which[0] == 0, both[:, 0], both[:, 1])
+            wanted.append(mine.reshape(HALF, TILE))
+        wanted = jnp.concatenate(wanted, axis=0)
+        place = counted(wanted.shape, 1)
+        pick = [ones_where(wanted == place + k) for k in range(0, right.shape[0], TILE)]
+        found = dot(jnp.concatenate(pick, axis=1), right[...])
         mode, parts = found[:, :TILE], found[:, TILE:]
         for s in range(OWN):
             phase = parts[:, s : s + 1] + parts[:, OWN + s : OWN + s + 1]
@@ -292,23 +302,24 @@
     lax.fori_loop(0, ordered.shape[0] // FAR_ROWS, chunk, 0)
 
 
-def in_order(order, factor, harmonics):
+def in_order(which, owner, factor, harmonics):
     return pl.pallas_call(
         order_kernel,
-        out_shape=jax.ShapeDtypeStruct((order.shape[0], OWN * TILE), jnp.bfloat16),
-        in_specs=[VMEM] + [HBM] * 2,
+        out_shape=jax.ShapeDtypeStruct((owner.shape[0] // 2, OWN * TILE), jnp.bfloat16),
+        in_specs=[SMEM] + [HBM] * 3,
         out_specs=VMEM,
         scratch_shapes=[
             pltpu.VMEM((harmonics.shape[0], 2 * TILE), jnp.bfloat16),
+            pltpu.VMEM((owner.shape[0] // TILE, TILE), owner.dtype),
             pltpu.VMEM(factor.shape, factor.dtype),
-            pltpu.SemaphoreType.DMA((2,)),
+            pltpu.SemaphoreType.DMA((3,)),
         ],
         compiler_params=LIMIT,
         cost_estimate=pl.CostEstimate(
             flops=2_000_000_000, bytes_accessed=4_000_000, transcendentals=0
         ),
         name="order",
-    )(order, stay(factor), stay(harmonics))
+    )(which.reshape(1), stay(owner.reshape(-1, TILE)), stay(factor), stay(harmonics))
 
 
 SCRATCH = pltpu.VMEM((SOURCES + 1, TILE, TILE), jnp.bfloat16)
@@ -366,22 +377,20 @@
 ):
     n_grp, n_dev = lax.axis_size("grp"), lax.axis_size("dev")
     coeff = apply_tmatrix(tmatrix, incident)
-    made = plan(need[0], pair_src, pair_tgt, pair_blk, pair_count)
+    made = plan(need[0].T, pair_src, pair_tgt, pair_blk, pair_count)
 
     rows = owner.shape[0] // (n_grp * n_dev)
-    order = owner.reshape(n_grp * n_dev // 2, 2, rows).transpose(1, 0, 2).reshape(2, -1)
-    core = lax.axis_index("dev") % 2
-    order_mine = jnp.where(core == 0, order[0], order[1])
-    order_other = jnp.where(core == 0, order[1], order[0])
-    order_mine, order_other = lax.optimization_barrier((order_mine[:, None], order_other[:, None]))
-    for_other = in_order(order_other, factor, harmonics)
-    near, other, far = spread(coeff, made, for_other)
+    core = lax.axis_index("dev") & 1
+    for_other = in_order(1 - core, owner, factor, harmonics)
+    near, other, far = spread(coeff, (for_other,), (made,))
+    near, other, for_other = lax.optimization_barrier((near, other, for_other))
+    weighted_other = send(for_other, SWAP)
     before = early_pairs(made, blocks, incident, near + other)
+    before = together(before, weighted_other)
     coeff = late_pairs(made, blocks, before, tmatrix, swapped(far, before))
 
-    mine = in_order(order_mine, factor, harmonics)
-    near, other, far = spread(coeff, mine)
-    weighted_other = send(for_other, SWAP)
+    mine = in_order(core, owner, factor, harmonics)
+    near, other, far = spread(coeff, (mine,), ())
     before = early_pairs(made, blocks, incident, near + other)
     coeff = late_pairs(made, blocks, before, tmatrix, swapped(far, before))
 

time: 106 us -> 104 us (0.981)
  waiting for transfers between devices: 12.3 us -> 16.2 us
  local copies, waits for them, and re-layouts: 3.94 us -> 0.1 us
  starting transfers between devices: 42.2 us -> 41.1 us
    ppermute x36, waiting for transfers between devices: 12.3 us -> 16.2 us  [send(): return lax.ppermute(values, 'dev', pairs)]
    unnamed x20 -> x16, local copies, waits for them, and re-layouts: 2.26 us -> 0.06 us
    ppermute x36, starting transfers between devices: 42.2 us -> 41.1 us  [send(): return lax.ppermute(values, 'dev', pairs)]
  transfers between devices with their start and end apart: 36 -> 36, of which waited for: 12 -> 13; matrix products, arithmetic and copies ran while one was open for 2% -> 0% of each run, Pallas kernels for 15% -> 13%
where the time goes in v5:
time: 104 us
  starting transfers between devices  41.1 us (40%)
  blocking collectives  25.1 us (24%)
  Pallas kernels  18.4 us (18%)
  waiting for transfers between devices  16.2 us (16%)
  matrix products  1.14 us (1%)
    ppermute x36, starting transfers between devices, send(): return lax.ppermute(values, 'dev', pairs)  41.1 us
    all_to_all x1, blocking collectives, body(): lax.all_to_all(amplitude, ('grp', 'dev'), 0, 0, axis_index_groups=groups)  25.1 us
    ppermute x36, waiting for transfers between devices, send(): return lax.ppermute(values, 'dev', pairs)  16.2 us
    pallas_call x2, Pallas kernels, in_order(): pl.pallas_call(order_kernel, out_shape=jax.ShapeDtypeStruct((owner.shape[...  8.14 us
    pallas_call x2, Pallas kernels, early_pairs(): pl.pallas_call(early_kernel, out_shape=jax.ShapeDtypeStruct(TOTAL, jnp.fl...  4.87 us
    pallas_call x2, Pallas kernels, late_pairs(): pl.pallas_call(late_kernel, out_shape=jax.ShapeDtypeStruct(TOTAL, jnp.bfl...  3.35 us
  transfers between devices with their start and end apart: 36, of which 13 were waited for; matrix products, arithmetic and copies ran while one was open for 0% of the time, Pallas kernels for 13%

profile of v5, /device:TPU:1, one launch (start us, length us, event | category | flops | bytes accessed | tf_op | source)
XLA Modules:
  0.0 103.7 jit_solution(13163962225300352599)
XLA Ops:
  0.0 1.1 %convolution_convert_fusion = bf16[4,128,128]{2,1,0:T(8,128)(2,1)S(1)} fusion(bf16[4,128,128]{2,1,0:T(8,128)(2,1)} %tmatrix.3, bf16[4,128,128]{2,1,0:T(8,128)(2,1)} %incident.3), kind=kOutput, calls=%fused_computation | convolution fusion | flops 16842752 | bytes 393216 | tf_op jit(solution)/shard_map/skl,slq->skq/dot_general | solution.py:361
  1.1 3.8 %collective-permute-start = (bf16[4,128,128]{2,1,0:T(8,128)(2,1)S(1)}, bf16[4,128,128]{2,1,0:T(8,128)(2,1)S(1)}, u32[]{:S(2)}, u32[]{:S(2)}) collective-permute-start(bf16[4,128,128]{2,1,0:T(8,128)(2,1)S(1)} %convolution_convert_fusion), channel_id=1, source_target_pairs={{0,16},{1,5},{2,18},{3,7},{4,20},{5,1},{6,22},{7,3},{8,24},{9,13},... | collective-permute-start | bytes 393224 | tf_op jit(solution)/shard_map/ppermute | solution.py:48
  5.0 0.4 collective-permute-start.1
  5.4 2.3 %collective-permute-start.2 = (bf16[4,128,128]{2,1,0:T(8,128)(2,1)S(1)}, bf16[4,128,128]{2,1,0:T(8,128)(2,1)S(1)}, u32[]{:S(2)}, u32[]{:S(2)}) collective-permute-start(bf16[4,128,128]{2,1,0:T(8,128)(2,1)S(1)} %convolution_convert_fusion), channel_id=1, source_target_pairs={{0,24},{1,7},{2,26},{3,1},{4,28},{5,3},{6,30},{7,5},{8,0},{9,15},{... | collective-permute-start | bytes 393224 | tf_op jit(solution)/shard_map/ppermute | solution.py:48
  8.3 4.1 %order.3 = bf16[1024,512]{1,0:T(8,128)(2,1)S(1)} custom-call(s32[1]{0:T(128)} %bitcast.2.which, s32[16,128]{1,0:T(8,128)} %bitcast.16, f32[4,2048]{1,0:T(4,128)} %factor_far.3, bf16[2048,128]{1,0:T(8,128)(2,1)} %harmonics.3), custom_call_target="tpu_custom_call" | custom-call | flops 2000000000 | bytes 4000000 | tf_op jit(solution)/shard_map/order/pallas_call | solution.py:306
  12.5 1.3 %collective-permute-start.3 = (bf16[8,128,128]{2,1,0:T(8,128)(2,1)S(1)}, bf16[8,128,128]{2,1,0:T(8,128)(2,1)S(1)}, u32[]{:S(2)}, u32[]{:S(2)}) collective-permute-start(bf16[8,128,128]{2,1,0:T(8,128)(2,1)S(1)} %constant_dynamic-update-slice_fusion.rest_1_), channel_id=1, source_target_pairs={{0,2},{1,9},{2,4},{3,11},{4,6},{5,13},{6,0},{7,15},{8,10},{9,17},{... | collective-permute-start | bytes 786440 | tf_op jit(solution)/shard_map/ppermute | solution.py:48
  13.8 1.5 %collective-permute-start.5 = (bf16[8,128,128]{2,1,0:T(8,128)(2,1)S(1)}, bf16[8,128,128]{2,1,0:T(8,128)(2,1)S(1)}, u32[]{:S(2)}, u32[]{:S(2)}) collective-permute-start(bf16[8,128,128]{2,1,0:T(8,128)(2,1)S(1)} %constant_dynamic-update-slice_fusion.rest_1_), channel_id=1, source_target_pairs={{0,6},{1,25},{2,0},{3,27},{4,2},{5,29},{6,4},{7,31},{8,14},{9,1},{... | collective-permute-start | bytes 786440 | tf_op jit(solution)/shard_map/ppermute | solution.py:48
  15.3 1.9 %collective-permute-start.8 = (bf16[8,128,128]{2,1,0:T(8,128)(2,1)S(1)}, bf16[8,128,128]{2,1,0:T(8,128)(2,1)S(1)}, u32[]{:S(2)}, u32[]{:S(2)}) collective-permute-start(bf16[8,128,128]{2,1,0:T(8,128)(2,1)S(1)} %constant_dynamic-update-slice_fusion.rest_1_), channel_id=1, source_target_pairs={{0,1},{1,0},{2,3},{3,2},{4,5},{5,4},{6,7},{7,6},{8,9},{9,8},{10,11... | collective-permute-start | bytes 786440 | tf_op jit(solution)/shard_map/ppermute | solution.py:48
  17.2 1.2 %collective-permute-start.4 = (bf16[8,128,128]{2,1,0:T(8,128)(2,1)S(1)}, bf16[8,128,128]{2,1,0:T(8,128)(2,1)S(1)}, u32[]{:S(2)}, u32[]{:S(2)}) collective-permute-start(bf16[8,128,128]{2,1,0:T(8,128)(2,1)S(1)} %pad_maximum_fusion.rest_0_), channel_id=1, source_target_pairs={{0,6},{1,25},{2,0},{3,27},{4,2},{5,29},{6,4},{7,31},{8,14},{9,1},{... | collective-permute-start | bytes 786440 | tf_op jit(solution)/shard_map/ppermute | solution.py:48
  18.3 0.4 collective-permute-start.6
  18.8 0.8 plan.1
  19.6 1.9 %collective-permute-start.7 = (bf16[8,128,128]{2,1,0:T(8,128)(2,1)S(1)}, bf16[8,128,128]{2,1,0:T(8,128)(2,1)S(1)}, u32[]{:S(2)}, u32[]{:S(2)}) collective-permute-start(bf16[8,128,128]{2,1,0:T(8,128)(2,1)S(1)} %pad_maximum_fusion.rest_0_), channel_id=1, source_target_pairs={{0,1},{1,0},{2,3},{3,2},{4,5},{5,4},{6,7},{7,6},{8,9},{9,8},{10,11... | collective-permute-start | bytes 786440 | tf_op jit(solution)/shard_map/ppermute | solution.py:48
  21.5 1.3 %collective-permute-done.4.rest_2_ = bf16[8,128,128]{2,1,0:T(8,128)(2,1)S(1)} collective-permute-done((bf16[8,128,128]{2,1,0:T(8,128)(2,1)S(1)}, bf16[8,128,128]{2,1,0:T(8,128)(2,1)S(1)}, u32[]{:S(2)}, u32[]{:S(2)}) %collective-permute-start.4) | collective-permute-done | bytes 262176 | tf_op jit(solution)/shard_map/ppermute | solution.py:48
  22.8 1.9 %collective-permute-start.12 = (bf16[8,128,128]{2,1,0:T(8,128)(2,1)S(1)}, bf16[8,128,128]{2,1,0:T(8,128)(2,1)S(1)}, u32[]{:S(2)}, u32[]{:S(2)}) collective-permute-start(bf16[8,128,128]{2,1,0:T(8,128)(2,1)S(1)} %collective-permute-done.3.rest_5_), channel_id=1, source_target_pairs={{0,1},{1,0},{2,3},{3,2},{4,5},{5,4},{6,7},{7,6},{8,9},{9,8},{10,11... | collective-permute-start | bytes 786440 | tf_op jit(solution)/shard_map/ppermute | solution.py:48
  24.7 0.5 collective-permute-start.10
  25.2 1.5 %collective-permute-start.11 = (bf16[8,128,128]{2,1,0:T(8,128)(2,1)S(1)}, bf16[8,128,128]{2,1,0:T(8,128)(2,1)S(1)}, u32[]{:S(2)}, u32[]{:S(2)}) collective-permute-start(bf16[8,128,128]{2,1,0:T(8,128)(2,1)S(1)} %collective-permute-done.6.rest_4_), channel_id=1, source_target_pairs={{0,1},{1,0},{2,3},{3,2},{4,5},{5,4},{6,7},{7,6},{8,9},{9,8},{10,11... | collective-permute-start | bytes 786440 | tf_op jit(solution)/shard_map/ppermute | solution.py:48
  26.7 1.1 %collective-permute-done.11.rest_10_ = bf16[8,128,128]{2,1,0:T(8,128)(2,1)S(1)} collective-permute-done((bf16[8,128,128]{2,1,0:T(8,128)(2,1)S(1)}, bf16[8,128,128]{2,1,0:T(8,128)(2,1)S(1)}, u32[]{:S(2)}, u32[]{:S(2)}) %collective-permute-start.11) | collective-permute-done | bytes 262176 | tf_op jit(solution)/shard_map/ppermute | solution.py:48
  28.2 1.1 %collective-permute-start.15 = (bf16[8,128,128]{2,1,0:T(8,128)(2,1)S(1)}, bf16[8,128,128]{2,1,0:T(8,128)(2,1)S(1)}, u32[]{:S(2)}, u32[]{:S(2)}) collective-permute-start(bf16[8,128,128]{2,1,0:T(8,128)(2,1)S(1)} %collective-permute-done.5.rest_3_), channel_id=1, source_target_pairs={{0,6},{1,25},{2,0},{3,27},{4,2},{5,29},{6,4},{7,31},{8,14},{9,1},{... | collective-permute-start | bytes 786440 | tf_op jit(solution)/shard_map/ppermute | solution.py:48
  29.3 0.4 collective-permute-start.14
  29.7 2.4 %early.2.before = f32[4,128,128]{2,1,0:T(8,128)S(1)} custom-call(s32[1,1152]{1,0:T(1,128)S(1)} %get-tuple-element.39.lists, s32[1,256]{1,0:T(1,128)S(1)} %get-tuple-element.40.groups, s32[1,128]{1,0:T(1,128)S(1)} %get-tuple-element.41.sizes, bf16[128,128,128]{2,1,0:T(8,128)(2,1)S(1)} %copy-done, bf16[4,128,128]{2,1,0:T(8,128)(2,1)S(1)} %copy-done.1, ...), custom_call_target="tpu_custom_call" | custom-call | flops 2000000000 | bytes 8000000 | tf_op jit(solution)/shard_map/early/pallas_call | solution.py:330
  32.1 1.6 %collective-permute-done.15.rest_1_ = bf16[8,128,128]{2,1,0:T(8,128)(2,1)S(1)} collective-permute-done((bf16[8,128,128]{2,1,0:T(8,128)(2,1)S(1)}, bf16[8,128,128]{2,1,0:T(8,128)(2,1)S(1)}, u32[]{:S(2)}, u32[]{:S(2)}) %collective-permute-start.15) | collective-permute-done | bytes 262176 | tf_op jit(solution)/shard_map/ppermute | solution.py:48
  33.7 2.3 %collective-permute-done.14.rest_0_ = bf16[8,128,128]{2,1,0:T(8,128)(2,1)S(1)} collective-permute-done((bf16[8,128,128]{2,1,0:T(8,128)(2,1)S(1)}, bf16[8,128,128]{2,1,0:T(8,128)(2,1)S(1)}, u32[]{:S(2)}, u32[]{:S(2)}) %collective-permute-start.14) | collective-permute-done | bytes 262176 | tf_op jit(solution)/shard_map/ppermute | solution.py:48
  36.0 1.9 %collective-permute-start.16 = (bf16[8,128,128]{2,1,0:T(8,128)(2,1)S(1)}, bf16[8,128,128]{2,1,0:T(8,128)(2,1)S(1)}, u32[]{:S(2)}, u32[]{:S(2)}) collective-permute-start(bf16[8,128,128]{2,1,0:T(8,128)(2,1)S(1)} %collective-permute-done.14.rest_0_), channel_id=1, source_target_pairs={{0,1},{1,0},{2,3},{3,2},{4,5},{5,4},{6,7},{7,6},{8,9},{9,8},{10,11... | collective-permute-start | bytes 786440 | tf_op jit(solution)/shard_map/ppermute | solution.py:48
  37.9 1.2 %collective-permute-done.16.rest_2_ = bf16[8,128,128]{2,1,0:T(8,128)(2,1)S(1)} collective-permute-done((bf16[8,128,128]{2,1,0:T(8,128)(2,1)S(1)}, bf16[8,128,128]{2,1,0:T(8,128)(2,1)S(1)}, u32[]{:S(2)}, u32[]{:S(2)}) %collective-permute-start.16) | collective-permute-done | bytes 262176 | tf_op jit(solution)/shard_map/ppermute | solution.py:48
  39.1 0.4 collective-permute-done.17.rest_3_
  39.5 1.7 %late.2 = bf16[4,128,128]{2,1,0:T(8,128)(2,1)S(1)} custom-call(s32[1,1152]{1,0:T(1,128)S(1)} %get-tuple-element.39.lists, s32[1,256]{1,0:T(1,128)S(1)} %get-tuple-element.40.groups, s32[1,128]{1,0:T(1,128)S(1)} %get-tuple-element.41.sizes, bf16[128,128,128]{2,1,0:T(8,128)(2,1)S(1)} %copy-done, f32[4,128,128]{2,1,0:T(8,128)S(1)} %early.2.before, ...), custom_call_target="tpu_custom_call" | custom-call | tf_op jit(solution)/shard_map/late/pallas_call | solution.py:345
  41.3 0.4 collective-permute-start.19
  41.7 2.3 %collective-permute-start.20 = (bf16[4,128,128]{2,1,0:T(8,128)(2,1)S(1)}, bf16[4,128,128]{2,1,0:T(8,128)(2,1)S(1)}, u32[]{:S(2)}, u32[]{:S(2)}) collective-permute-start(bf16[4,128,128]{2,1,0:T(8,128)(2,1)S(1)} %late.2), channel_id=1, source_target_pairs={{0,24},{1,7},{2,26},{3,1},{4,28},{5,3},{6,30},{7,5},{8,0},{9,15},{... | collective-permute-start | bytes 393224 | tf_op jit(solution)/shard_map/ppermute | solution.py:48
  44.0 4.1 %order.2.mine = bf16[1024,512]{1,0:T(8,128)(2,1)S(1)} custom-call(s32[1]{0:T(128)} %bitcast.which, s32[16,128]{1,0:T(8,128)} %bitcast.17, f32[4,2048]{1,0:T(4,128)} %factor_far.3, bf16[2048,128]{1,0:T(8,128)(2,1)} %harmonics.3), custom_call_target="tpu_custom_call" | custom-call | flops 2000000000 | bytes 4000000 | tf_op jit(solution)/shard_map/order/pallas_call | solution.py:306
  48.3 2.7 %collective-permute-start.22 = (bf16[8,128,128]{2,1,0:T(8,128)(2,1)S(1)}, bf16[8,128,128]{2,1,0:T(8,128)(2,1)S(1)}, u32[]{:S(2)}, u32[]{:S(2)}) collective-permute-start(bf16[8,128,128]{2,1,0:T(8,128)(2,1)S(1)} %pad_maximum_fusion.1.rest_0_), channel_id=1, source_target_pairs={{0,6},{1,25},{2,0},{3,27},{4,2},{5,29},{6,4},{7,31},{8,14},{9,1},{... | collective-permute-start | bytes 786440 | tf_op jit(solution)/shard_map/ppermute | solution.py:48
  51.3 2.2 %collective-permute-start.26 = (bf16[8,128,128]{2,1,0:T(8,128)(2,1)S(1)}, bf16[8,128,128]{2,1,0:T(8,128)(2,1)S(1)}, u32[]{:S(2)}, u32[]{:S(2)}) collective-permute-start(bf16[8,128,128]{2,1,0:T(8,128)(2,1)S(1)} %constant_dynamic-update-slice_fusion.2.rest_1_), channel_id=1, source_target_pairs={{0,1},{1,0},{2,3},{3,2},{4,5},{5,4},{6,7},{7,6},{8,9},{9,8},{10,11... | collective-permute-start | bytes 786440 | tf_op jit(solution)/shard_map/ppermute | solution.py:48
  53.6 1.4 %collective-permute-done.21.rest_5_ = bf16[8,128,128]{2,1,0:T(8,128)(2,1)S(1)} collective-permute-done((bf16[8,128,128]{2,1,0:T(8,128)(2,1)S(1)}, bf16[8,128,128]{2,1,0:T(8,128)(2,1)S(1)}, u32[]{:S(2)}, u32[]{:S(2)}) %collective-permute-start.21) | collective-permute-done | bytes 262176 | tf_op jit(solution)/shard_map/ppermute | solution.py:48
  55.0 2.7 %collective-permute-start.25 = (bf16[8,128,128]{2,1,0:T(8,128)(2,1)S(1)}, bf16[8,128,128]{2,1,0:T(8,128)(2,1)S(1)}, u32[]{:S(2)}, u32[]{:S(2)}) collective-permute-start(bf16[8,128,128]{2,1,0:T(8,128)(2,1)S(1)} %pad_maximum_fusion.1.rest_0_), channel_id=1, source_target_pairs={{0,1},{1,0},{2,3},{3,2},{4,5},{5,4},{6,7},{7,6},{8,9},{9,8},{10,11... | collective-permute-start | bytes 786440 | tf_op jit(solution)/shard_map/ppermute | solution.py:48
  57.7 2.4 %collective-permute-start.30 = (bf16[8,128,128]{2,1,0:T(8,128)(2,1)S(1)}, bf16[8,128,128]{2,1,0:T(8,128)(2,1)S(1)}, u32[]{:S(2)}, u32[]{:S(2)}) collective-permute-start(bf16[8,128,128]{2,1,0:T(8,128)(2,1)S(1)} %collective-permute-done.21.rest_5_), channel_id=1, source_target_pairs={{0,1},{1,0},{2,3},{3,2},{4,5},{5,4},{6,7},{7,6},{8,9},{9,8},{10,11... | collective-permute-start | bytes 786440 | tf_op jit(solution)/shard_map/ppermute | solution.py:48
  60.3 0.9 collective-permute-start.29
  61.1 1.8 %collective-permute-start.32 = (bf16[8,128,128]{2,1,0:T(8,128)(2,1)S(1)}, bf16[8,128,128]{2,1,0:T(8,128)(2,1)S(1)}, u32[]{:S(2)}, u32[]{:S(2)}) collective-permute-start(bf16[8,128,128]{2,1,0:T(8,128)(2,1)S(1)} %collective-permute-done.23.rest_3_), channel_id=1, source_target_pairs={{0,6},{1,25},{2,0},{3,27},{4,2},{5,29},{6,4},{7,31},{8,14},{9,1},{... | collective-permute-start | bytes 786440 | tf_op jit(solution)/shard_map/ppermute | solution.py:48
  62.9 2.4 %early.3.before = f32[4,128,128]{2,1,0:T(8,128)S(1)} custom-call(s32[1,1152]{1,0:T(1,128)S(1)} %get-tuple-element.39.lists, s32[1,256]{1,0:T(1,128)S(1)} %get-tuple-element.40.groups, s32[1,128]{1,0:T(1,128)S(1)} %get-tuple-element.41.sizes, bf16[128,128,128]{2,1,0:T(8,128)(2,1)S(1)} %copy-done, bf16[4,128,128]{2,1,0:T(8,128)(2,1)S(1)} %copy-done.1, ...), custom_call_target="tpu_custom_call" | custom-call | flops 2000000000 | bytes 8000000 | tf_op jit(solution)/shard_map/early/pallas_call | solution.py:330
  65.4 1.3 %collective-permute-done.32.rest_1_ = bf16[8,128,128]{2,1,0:T(8,128)(2,1)S(1)} collective-permute-done((bf16[8,128,128]{2,1,0:T(8,128)(2,1)S(1)}, bf16[8,128,128]{2,1,0:T(8,128)(2,1)S(1)}, u32[]{:S(2)}, u32[]{:S(2)}) %collective-permute-start.32) | collective-permute-done | bytes 262176 | tf_op jit(solution)/shard_map/ppermute | solution.py:48
  66.7 3.0 %collective-permute-done.31.rest_0_ = bf16[8,128,128]{2,1,0:T(8,128)(2,1)S(1)} collective-permute-done((bf16[8,128,128]{2,1,0:T(8,128)(2,1)S(1)}, bf16[8,128,128]{2,1,0:T(8,128)(2,1)S(1)}, u32[]{:S(2)}, u32[]{:S(2)}) %collective-permute-start.31) | collective-permute-done | bytes 262176 | tf_op jit(solution)/shard_map/ppermute | solution.py:48
  69.6 2.4 %collective-permute-start.33 = (bf16[8,128,128]{2,1,0:T(8,128)(2,1)S(1)}, bf16[8,128,128]{2,1,0:T(8,128)(2,1)S(1)}, u32[]{:S(2)}, u32[]{:S(2)}) collective-permute-start(bf16[8,128,128]{2,1,0:T(8,128)(2,1)S(1)} %collective-permute-done.31.rest_0_), channel_id=1, source_target_pairs={{0,1},{1,0},{2,3},{3,2},{4,5},{5,4},{6,7},{7,6},{8,9},{9,8},{10,11... | collective-permute-start | bytes 786440 | tf_op jit(solution)/shard_map/ppermute | solution.py:48
  72.1 1.2 %collective-permute-done.33.rest_2_ = bf16[8,128,128]{2,1,0:T(8,128)(2,1)S(1)} collective-permute-done((bf16[8,128,128]{2,1,0:T(8,128)(2,1)S(1)}, bf16[8,128,128]{2,1,0:T(8,128)(2,1)S(1)}, u32[]{:S(2)}, u32[]{:S(2)}) %collective-permute-start.33) | collective-permute-done | bytes 262176 | tf_op jit(solution)/shard_map/ppermute | solution.py:48
  73.2 0.4 collective-permute-done.34.rest_3_
  73.6 1.7 %late.3 = bf16[4,128,128]{2,1,0:T(8,128)(2,1)S(1)} custom-call(s32[1,1152]{1,0:T(1,128)S(1)} %get-tuple-element.39.lists, s32[1,256]{1,0:T(1,128)S(1)} %get-tuple-element.40.groups, s32[1,128]{1,0:T(1,128)S(1)} %get-tuple-element.41.sizes, bf16[128,128,128]{2,1,0:T(8,128)(2,1)S(1)} %copy-done, f32[4,128,128]{2,1,0:T(8,128)S(1)} %early.3.before, ...), custom_call_target="tpu_custom_call" | custom-call | tf_op jit(solution)/shard_map/late/pallas_call | solution.py:345
  75.3 0.5 collective-permute-start.35
  75.7 1.0 collective-permute-done.35
  76.7 1.2 %far.1 = bf16[1024,128]{1,0:T(8,128)(2,1)S(1)} custom-call(bf16[1024,512]{1,0:T(8,128)(2,1)S(1)} %order.2.mine, bf16[1024,512]{1,0:T(8,128)(2,1)S(1)} %collective-permute-done.13.other, bf16[512,128]{1,0:T(8,128)(2,1)S(1)} %bitcast.13, bf16[512,128]{1,0:T(8,128)(2,1)S(1)} %bitcast.14), custom_call_target="tpu_custom_call" | custom-call | tf_op jit(solution)/shard_map/far/pallas_call | solution.py:252
  77.9 25.1 %all_to_all.5 = bf16[128,8,128]{2,1,0:T(8,128)(2,1)S(1)} all-to-all(bf16[128,8,128]{2,1,0:T(8,128)(2,1)S(1)} %bitcast.12), channel_id=1, replica_groups={{0,2,4,6,8,10,12,14,16,18,20,22,24,26,28,30,32,34,36,38,40,42,44,46,48,..., dimensions={0} | all-to-all | bytes 524288 | tf_op jit(solution)/shard_map/all_to_all | solution.py:400
  103.0 0.7 convert_reduce_fusion
  (55 shorter events, 1.2 us)
Async XLA Ops:
  1.1 11.3 %collective-permute-start = (bf16[4,128,128]{2,1,0:T(8,128)(2,1)S(1)}, bf16[4,128,128]{2,1,0:T(8,128)(2,1)S(1)}, u32[]{:S(2)}, u32[]{:S(2)}) collective-permute-start(bf16[4,128,128]{2,1,0:T(8,128)(2,1)S(1)} %convolution_convert_fusion), channel_id=1, source_target_pairs={{0,16},{1,5},{2,18},{3,7},{4,20},{5,1},{6,22},{7,3},{8,24},{9,13},... | collective-permute-start | bytes 393224 | tf_op jit(solution)/shard_map/ppermute | solution.py:48
  5.0 7.5 %collective-permute-start.1 = (bf16[4,128,128]{2,1,0:T(8,128)(2,1)S(1)}, bf16[4,128,128]{2,1,0:T(8,128)(2,1)S(1)}, u32[]{:S(2)}, u32[]{:S(2)}) collective-permute-start(bf16[4,128,128]{2,1,0:T(8,128)(2,1)S(1)} %convolution_convert_fusion), channel_id=1, source_target_pairs={{0,8},{1,3},{2,10},{3,5},{4,12},{5,7},{6,14},{7,1},{8,16},{9,11},{... | collective-permute-start | bytes 393224 | tf_op jit(solution)/shard_map/ppermute | solution.py:48
  5.4 7.1 %collective-permute-start.2 = (bf16[4,128,128]{2,1,0:T(8,128)(2,1)S(1)}, bf16[4,128,128]{2,1,0:T(8,128)(2,1)S(1)}, u32[]{:S(2)}, u32[]{:S(2)}) collective-permute-start(bf16[4,128,128]{2,1,0:T(8,128)(2,1)S(1)} %convolution_convert_fusion), channel_id=1, source_target_pairs={{0,24},{1,7},{2,26},{3,1},{4,28},{5,3},{6,30},{7,5},{8,0},{9,15},{... | collective-permute-start | bytes 393224 | tf_op jit(solution)/shard_map/ppermute | solution.py:48
  8.3 10.4 %copy-start.3 = (s32[1,32,4]{1,2,0:T(4,128)S(1)}, s32[1,32,4]{1,2,0:T(4,128)}, u32[]{:S(2)}) copy-start(s32[1,32,4]{1,2,0:T(4,128)} %param.14) | copy-start | bytes 1540
  8.3 10.4 %copy-start.4 = (s32[1,512]{1,0:T(1,128)S(1)}, s32[1,512]{1,0:T(1,128)}, u32[]{:S(2)}) copy-start(s32[1,512]{1,0:T(1,128)} %src.1) | copy-start | bytes 6148
  8.3 10.4 %copy-start.5 = (s32[1,512]{1,0:T(1,128)S(1)}, s32[1,512]{1,0:T(1,128)}, u32[]{:S(2)}) copy-start(s32[1,512]{1,0:T(1,128)} %tgt.1) | copy-start | bytes 6148
  8.3 10.4 %copy-start.6 = (s32[1,512]{1,0:T(1,128)S(1)}, s32[1,512]{1,0:T(1,128)}, u32[]{:S(2)}) copy-start(s32[1,512]{1,0:T(1,128)} %blk.1) | copy-start | bytes 6148
  12.5 7.1 %collective-permute-start.3 = (bf16[8,128,128]{2,1,0:T(8,128)(2,1)S(1)}, bf16[8,128,128]{2,1,0:T(8,128)(2,1)S(1)}, u32[]{:S(2)}, u32[]{:S(2)}) collective-permute-start(bf16[8,128,128]{2,1,0:T(8,128)(2,1)S(1)} %constant_dynamic-update-slice_fusion.rest_1_), channel_id=1, source_target_pairs={{0,2},{1,9},{2,4},{3,11},{4,6},{5,13},{6,0},{7,15},{8,10},{9,17},{... | collective-permute-start | bytes 786440 | tf_op jit(solution)/shard_map/ppermute | solution.py:48
  13.8 10.9 %collective-permute-start.5 = (bf16[8,128,128]{2,1,0:T(8,128)(2,1)S(1)}, bf16[8,128,128]{2,1,0:T(8,128)(2,1)S(1)}, u32[]{:S(2)}, u32[]{:S(2)}) collective-permute-start(bf16[8,128,128]{2,1,0:T(8,128)(2,1)S(1)} %constant_dynamic-update-slice_fusion.rest_1_), channel_id=1, source_target_pairs={{0,6},{1,25},{2,0},{3,27},{4,2},{5,29},{6,4},{7,31},{8,14},{9,1},{... | collective-permute-start | bytes 786440 | tf_op jit(solution)/shard_map/ppermute | solution.py:48
  15.3 9.4 %collective-permute-start.8 = (bf16[8,128,128]{2,1,0:T(8,128)(2,1)S(1)}, bf16[8,128,128]{2,1,0:T(8,128)(2,1)S(1)}, u32[]{:S(2)}, u32[]{:S(2)}) collective-permute-start(bf16[8,128,128]{2,1,0:T(8,128)(2,1)S(1)} %constant_dynamic-update-slice_fusion.rest_1_), channel_id=1, source_target_pairs={{0,1},{1,0},{2,3},{3,2},{4,5},{5,4},{6,7},{7,6},{8,9},{9,8},{10,11... | collective-permute-start | bytes 786440 | tf_op jit(solution)/shard_map/ppermute | solution.py:48
  17.2 5.6 %collective-permute-start.4 = (bf16[8,128,128]{2,1,0:T(8,128)(2,1)S(1)}, bf16[8,128,128]{2,1,0:T(8,128)(2,1)S(1)}, u32[]{:S(2)}, u32[]{:S(2)}) collective-permute-start(bf16[8,128,128]{2,1,0:T(8,128)(2,1)S(1)} %pad_maximum_fusion.rest_0_), channel_id=1, source_target_pairs={{0,6},{1,25},{2,0},{3,27},{4,2},{5,29},{6,4},{7,31},{8,14},{9,1},{... | collective-permute-start | bytes 786440 | tf_op jit(solution)/shard_map/ppermute | solution.py:48
  18.3 6.9 %collective-permute-start.6 = (bf16[8,128,128]{2,1,0:T(8,128)(2,1)S(1)}, bf16[8,128,128]{2,1,0:T(8,128)(2,1)S(1)}, u32[]{:S(2)}, u32[]{:S(2)}) collective-permute-start(bf16[8,128,128]{2,1,0:T(8,128)(2,1)S(1)} %pad_maximum_fusion.rest_0_), channel_id=1, source_target_pairs={{0,2},{1,9},{2,4},{3,11},{4,6},{5,13},{6,0},{7,15},{8,10},{9,17},{... | collective-permute-start | bytes 786440 | tf_op jit(solution)/shard_map/ppermute | solution.py:48
  18.8 10.9 %copy-start = (bf16[128,128,128]{2,1,0:T(8,128)(2,1)S(1)}, bf16[128,128,128]{2,1,0:T(8,128)(2,1)}, u32[]{:S(2)}) copy-start(bf16[128,128,128]{2,1,0:T(8,128)(2,1)} %blocks.7) | copy-start | bytes 12582916
  18.8 10.9 %copy-start.1 = (bf16[4,128,128]{2,1,0:T(8,128)(2,1)S(1)}, bf16[4,128,128]{2,1,0:T(8,128)(2,1)}, u32[]{:S(2)}) copy-start(bf16[4,128,128]{2,1,0:T(8,128)(2,1)} %incident.3) | copy-start | bytes 393220
  19.6 19.9 %copy-start.2 = (bf16[4,128,128]{2,1,0:T(8,128)(2,1)S(1)}, bf16[4,128,128]{2,1,0:T(8,128)(2,1)}, u32[]{:S(2)}) copy-start(bf16[4,128,128]{2,1,0:T(8,128)(2,1)} %tmatrix.3) | copy-start | bytes 393220
  19.6 7.1 %collective-permute-start.7 = (bf16[8,128,128]{2,1,0:T(8,128)(2,1)S(1)}, bf16[8,128,128]{2,1,0:T(8,128)(2,1)S(1)}, u32[]{:S(2)}, u32[]{:S(2)}) collective-permute-start(bf16[8,128,128]{2,1,0:T(8,128)(2,1)S(1)} %pad_maximum_fusion.rest_0_), channel_id=1, source_target_pairs={{0,1},{1,0},{2,3},{3,2},{4,5},{5,4},{6,7},{7,6},{8,9},{9,8},{10,11... | collective-permute-start | bytes 786440 | tf_op jit(solution)/shard_map/ppermute | solution.py:48
  22.8 3.9 %collective-permute-start.12 = (bf16[8,128,128]{2,1,0:T(8,128)(2,1)S(1)}, bf16[8,128,128]{2,1,0:T(8,128)(2,1)S(1)}, u32[]{:S(2)}, u32[]{:S(2)}) collective-permute-start(bf16[8,128,128]{2,1,0:T(8,128)(2,1)S(1)} %collective-permute-done.3.rest_5_), channel_id=1, source_target_pairs={{0,1},{1,0},{2,3},{3,2},{4,5},{5,4},{6,7},{7,6},{8,9},{9,8},{10,11... | collective-permute-start | bytes 786440 | tf_op jit(solution)/shard_map/ppermute | solution.py:48
  24.7 2.0 %collective-permute-start.9 = (bf16[8,128,128]{2,1,0:T(8,128)(2,1)S(1)}, bf16[8,128,128]{2,1,0:T(8,128)(2,1)S(1)}, u32[]{:S(2)}, u32[]{:S(2)}) collective-permute-start(bf16[8,128,128]{2,1,0:T(8,128)(2,1)S(1)} %collective-permute-done.4.rest_2_), channel_id=1, source_target_pairs={{0,1},{1,0},{2,3},{3,2},{4,5},{5,4},{6,7},{7,6},{8,9},{9,8},{10,11... | collective-permute-start | bytes 786440 | tf_op jit(solution)/shard_map/ppermute | solution.py:48
  24.7 2.0 %collective-permute-start.10 = (bf16[8,128,128]{2,1,0:T(8,128)(2,1)S(1)}, bf16[8,128,128]{2,1,0:T(8,128)(2,1)S(1)}, u32[]{:S(2)}, u32[]{:S(2)}) collective-permute-start(bf16[8,128,128]{2,1,0:T(8,128)(2,1)S(1)} %collective-permute-done.5.rest_3_), channel_id=1, source_target_pairs={{0,1},{1,0},{2,3},{3,2},{4,5},{5,4},{6,7},{7,6},{8,9},{9,8},{10,11... | collective-permute-start | bytes 786440 | tf_op jit(solution)/shard_map/ppermute | solution.py:48
  25.2 2.6 %collective-permute-start.11 = (bf16[8,128,128]{2,1,0:T(8,128)(2,1)S(1)}, bf16[8,128,128]{2,1,0:T(8,128)(2,1)S(1)}, u32[]{:S(2)}, u32[]{:S(2)}) collective-permute-start(bf16[8,128,128]{2,1,0:T(8,128)(2,1)S(1)} %collective-permute-done.6.rest_4_), channel_id=1, source_target_pairs={{0,1},{1,0},{2,3},{3,2},{4,5},{5,4},{6,7},{7,6},{8,9},{9,8},{10,11... | collective-permute-start | bytes 786440 | tf_op jit(solution)/shard_map/ppermute | solution.py:48
  27.8 4.3 %collective-permute-start.13 = (bf16[1024,512]{1,0:T(8,128)(2,1)S(1)}, bf16[1024,512]{1,0:T(8,128)(2,1)S(1)}, u32[]{:S(2)}, u32[]{:S(2)}) collective-permute-start(bf16[1024,512]{1,0:T(8,128)(2,1)S(1)} %order.3), channel_id=1, source_target_pairs={{0,1},{1,0},{2,3},{3,2},{4,5},{5,4},{6,7},{7,6},{8,9},{9,8},{10,11... | collective-permute-start | bytes 3145736 | tf_op jit(solution)/shard_map/ppermute | solution.py:48
  28.2 5.5 %collective-permute-start.15 = (bf16[8,128,128]{2,1,0:T(8,128)(2,1)S(1)}, bf16[8,128,128]{2,1,0:T(8,128)(2,1)S(1)}, u32[]{:S(2)}, u32[]{:S(2)}) collective-permute-start(bf16[8,128,128]{2,1,0:T(8,128)(2,1)S(1)} %collective-permute-done.5.rest_3_), channel_id=1, source_target_pairs={{0,6},{1,25},{2,0},{3,27},{4,2},{5,29},{6,4},{7,31},{8,14},{9,1},{... | collective-permute-start | bytes 786440 | tf_op jit(solution)/shard_map/ppermute | solution.py:48
  29.3 6.7 %collective-permute-start.14 = (bf16[8,128,128]{2,1,0:T(8,128)(2,1)S(1)}, bf16[8,128,128]{2,1,0:T(8,128)(2,1)S(1)}, u32[]{:S(2)}, u32[]{:S(2)}) collective-permute-start(bf16[8,128,128]{2,1,0:T(8,128)(2,1)S(1)} %collective-permute-done.6.rest_4_), channel_id=1, source_target_pairs={{0,2},{1,9},{2,4},{3,11},{4,6},{5,13},{6,0},{7,15},{8,10},{9,17},{... | collective-permute-start | bytes 786440 | tf_op jit(solution)/shard_map/ppermute | solution.py:48
  36.0 3.1 %collective-permute-start.16 = (bf16[8,128,128]{2,1,0:T(8,128)(2,1)S(1)}, bf16[8,128,128]{2,1,0:T(8,128)(2,1)S(1)}, u32[]{:S(2)}, u32[]{:S(2)}) collective-permute-start(bf16[8,128,128]{2,1,0:T(8,128)(2,1)S(1)} %collective-permute-done.14.rest_0_), channel_id=1, source_target_pairs={{0,1},{1,0},{2,3},{3,2},{4,5},{5,4},{6,7},{7,6},{8,9},{9,8},{10,11... | collective-permute-start | bytes 786440 | tf_op jit(solution)/shard_map/ppermute | solution.py:48
  37.9 1.5 %collective-permute-start.17 = (bf16[8,128,128]{2,1,0:T(8,128)(2,1)S(1)}, bf16[8,128,128]{2,1,0:T(8,128)(2,1)S(1)}, u32[]{:S(2)}, u32[]{:S(2)}) collective-permute-start(bf16[8,128,128]{2,1,0:T(8,128)(2,1)S(1)} %collective-permute-done.15.rest_1_), channel_id=1, source_target_pairs={{0,1},{1,0},{2,3},{3,2},{4,5},{5,4},{6,7},{7,6},{8,9},{9,8},{10,11... | collective-permute-start | bytes 786440 | tf_op jit(solution)/shard_map/ppermute | solution.py:48
  41.2 6.9 %collective-permute-start.18 = (bf16[4,128,128]{2,1,0:T(8,128)(2,1)S(1)}, bf16[4,128,128]{2,1,0:T(8,128)(2,1)S(1)}, u32[]{:S(2)}, u32[]{:S(2)}) collective-permute-start(bf16[4,128,128]{2,1,0:T(8,128)(2,1)S(1)} %late.2), channel_id=1, source_target_pairs={{0,16},{1,5},{2,18},{3,7},{4,20},{5,1},{6,22},{7,3},{8,24},{9,13},... | collective-permute-start | bytes 393224 | tf_op jit(solution)/shard_map/ppermute | solution.py:48
  41.3 6.8 %collective-permute-start.19 = (bf16[4,128,128]{2,1,0:T(8,128)(2,1)S(1)}, bf16[4,128,128]{2,1,0:T(8,128)(2,1)S(1)}, u32[]{:S(2)}, u32[]{:S(2)}) collective-permute-start(bf16[4,128,128]{2,1,0:T(8,128)(2,1)S(1)} %late.2), channel_id=1, source_target_pairs={{0,8},{1,3},{2,10},{3,5},{4,12},{5,7},{6,14},{7,1},{8,16},{9,11},{... | collective-permute-start | bytes 393224 | tf_op jit(solution)/shard_map/ppermute | solution.py:48
  41.7 6.4 %collective-permute-start.20 = (bf16[4,128,128]{2,1,0:T(8,128)(2,1)S(1)}, bf16[4,128,128]{2,1,0:T(8,128)(2,1)S(1)}, u32[]{:S(2)}, u32[]{:S(2)}) collective-permute-start(bf16[4,128,128]{2,1,0:T(8,128)(2,1)S(1)} %late.2), channel_id=1, source_target_pairs={{0,24},{1,7},{2,26},{3,1},{4,28},{5,3},{6,30},{7,5},{8,0},{9,15},{... | collective-permute-start | bytes 393224 | tf_op jit(solution)/shard_map/ppermute | solution.py:48
  48.2 6.8 %collective-permute-start.21 = (bf16[8,128,128]{2,1,0:T(8,128)(2,1)S(1)}, bf16[8,128,128]{2,1,0:T(8,128)(2,1)S(1)}, u32[]{:S(2)}, u32[]{:S(2)}) collective-permute-start(bf16[8,128,128]{2,1,0:T(8,128)(2,1)S(1)} %constant_dynamic-update-slice_fusion.2.rest_1_), channel_id=1, source_target_pairs={{0,2},{1,9},{2,4},{3,11},{4,6},{5,13},{6,0},{7,15},{8,10},{9,17},{... | collective-permute-start | bytes 786440 | tf_op jit(solution)/shard_map/ppermute | solution.py:48
  48.3 9.4 %collective-permute-start.22 = (bf16[8,128,128]{2,1,0:T(8,128)(2,1)S(1)}, bf16[8,128,128]{2,1,0:T(8,128)(2,1)S(1)}, u32[]{:S(2)}, u32[]{:S(2)}) collective-permute-start(bf16[8,128,128]{2,1,0:T(8,128)(2,1)S(1)} %pad_maximum_fusion.1.rest_0_), channel_id=1, source_target_pairs={{0,6},{1,25},{2,0},{3,27},{4,2},{5,29},{6,4},{7,31},{8,14},{9,1},{... | collective-permute-start | bytes 786440 | tf_op jit(solution)/shard_map/ppermute | solution.py:48
  51.0 6.7 %collective-permute-start.23 = (bf16[8,128,128]{2,1,0:T(8,128)(2,1)S(1)}, bf16[8,128,128]{2,1,0:T(8,128)(2,1)S(1)}, u32[]{:S(2)}, u32[]{:S(2)}) collective-permute-start(bf16[8,128,128]{2,1,0:T(8,128)(2,1)S(1)} %constant_dynamic-update-slice_fusion.2.rest_1_), channel_id=1, source_target_pairs={{0,6},{1,25},{2,0},{3,27},{4,2},{5,29},{6,4},{7,31},{8,14},{9,1},{... | collective-permute-start | bytes 786440 | tf_op jit(solution)/shard_map/ppermute | solution.py:48
  51.3 8.8 %collective-permute-start.26 = (bf16[8,128,128]{2,1,0:T(8,128)(2,1)S(1)}, bf16[8,128,128]{2,1,0:T(8,128)(2,1)S(1)}, u32[]{:S(2)}, u32[]{:S(2)}) collective-permute-start(bf16[8,128,128]{2,1,0:T(8,128)(2,1)S(1)} %constant_dynamic-update-slice_fusion.2.rest_1_), channel_id=1, source_target_pairs={{0,1},{1,0},{2,3},{3,2},{4,5},{5,4},{6,7},{7,6},{8,9},{9,8},{10,11... | collective-permute-start | bytes 786440 | tf_op jit(solution)/shard_map/ppermute | solution.py:48
  53.6 6.7 %collective-permute-start.24 = (bf16[8,128,128]{2,1,0:T(8,128)(2,1)S(1)}, bf16[8,128,128]{2,1,0:T(8,128)(2,1)S(1)}, u32[]{:S(2)}, u32[]{:S(2)}) collective-permute-start(bf16[8,128,128]{2,1,0:T(8,128)(2,1)S(1)} %pad_maximum_fusion.1.rest_0_), channel_id=1, source_target_pairs={{0,2},{1,9},{2,4},{3,11},{4,6},{5,13},{6,0},{7,15},{8,10},{9,17},{... | collective-permute-start | bytes 786440 | tf_op jit(solution)/shard_map/ppermute | solution.py:48
  55.0 6.2 %collective-permute-start.25 = (bf16[8,128,128]{2,1,0:T(8,128)(2,1)S(1)}, bf16[8,128,128]{2,1,0:T(8,128)(2,1)S(1)}, u32[]{:S(2)}, u32[]{:S(2)}) collective-permute-start(bf16[8,128,128]{2,1,0:T(8,128)(2,1)S(1)} %pad_maximum_fusion.1.rest_0_), channel_id=1, source_target_pairs={{0,1},{1,0},{2,3},{3,2},{4,5},{5,4},{6,7},{7,6},{8,9},{9,8},{10,11... | collective-permute-start | bytes 786440 | tf_op jit(solution)/shard_map/ppermute | solution.py:48
  57.7 5.2 %collective-permute-start.27 = (bf16[8,128,128]{2,1,0:T(8,128)(2,1)S(1)}, bf16[8,128,128]{2,1,0:T(8,128)(2,1)S(1)}, u32[]{:S(2)}, u32[]{:S(2)}) collective-permute-start(bf16[8,128,128]{2,1,0:T(8,128)(2,1)S(1)} %collective-permute-done.22.rest_2_), channel_id=1, source_target_pairs={{0,1},{1,0},{2,3},{3,2},{4,5},{5,4},{6,7},{7,6},{8,9},{9,8},{10,11... | collective-permute-start | bytes 786440 | tf_op jit(solution)/shard_map/ppermute | solution.py:48
  57.7 5.2 %collective-permute-start.30 = (bf16[8,128,128]{2,1,0:T(8,128)(2,1)S(1)}, bf16[8,128,128]{2,1,0:T(8,128)(2,1)S(1)}, u32[]{:S(2)}, u32[]{:S(2)}) collective-permute-start(bf16[8,128,128]{2,1,0:T(8,128)(2,1)S(1)} %collective-permute-done.21.rest_5_), channel_id=1, source_target_pairs={{0,1},{1,0},{2,3},{3,2},{4,5},{5,4},{6,7},{7,6},{8,9},{9,8},{10,11... | collective-permute-start | bytes 786440 | tf_op jit(solution)/shard_map/ppermute | solution.py:48
  60.2 2.8 %collective-permute-start.28 = (bf16[8,128,128]{2,1,0:T(8,128)(2,1)S(1)}, bf16[8,128,128]{2,1,0:T(8,128)(2,1)S(1)}, u32[]{:S(2)}, u32[]{:S(2)}) collective-permute-start(bf16[8,128,128]{2,1,0:T(8,128)(2,1)S(1)} %collective-permute-done.23.rest_3_), channel_id=1, source_target_pairs={{0,1},{1,0},{2,3},{3,2},{4,5},{5,4},{6,7},{7,6},{8,9},{9,8},{10,11... | collective-permute-start | bytes 786440 | tf_op jit(solution)/shard_map/ppermute | solution.py:48
  60.3 2.7 %collective-permute-start.29 = (bf16[8,128,128]{2,1,0:T(8,128)(2,1)S(1)}, bf16[8,128,128]{2,1,0:T(8,128)(2,1)S(1)}, u32[]{:S(2)}, u32[]{:S(2)}) collective-permute-start(bf16[8,128,128]{2,1,0:T(8,128)(2,1)S(1)} %collective-permute-done.24.rest_4_), channel_id=1, source_target_pairs={{0,1},{1,0},{2,3},{3,2},{4,5},{5,4},{6,7},{7,6},{8,9},{9,8},{10,11... | collective-permute-start | bytes 786440 | tf_op jit(solution)/shard_map/ppermute | solution.py:48
  61.1 5.5 %collective-permute-start.32 = (bf16[8,128,128]{2,1,0:T(8,128)(2,1)S(1)}, bf16[8,128,128]{2,1,0:T(8,128)(2,1)S(1)}, u32[]{:S(2)}, u32[]{:S(2)}) collective-permute-start(bf16[8,128,128]{2,1,0:T(8,128)(2,1)S(1)} %collective-permute-done.23.rest_3_), channel_id=1, source_target_pairs={{0,6},{1,25},{2,0},{3,27},{4,2},{5,29},{6,4},{7,31},{8,14},{9,1},{... | collective-permute-start | bytes 786440 | tf_op jit(solution)/shard_map/ppermute | solution.py:48
  62.9 6.7 %collective-permute-start.31 = (bf16[8,128,128]{2,1,0:T(8,128)(2,1)S(1)}, bf16[8,128,128]{2,1,0:T(8,128)(2,1)S(1)}, u32[]{:S(2)}, u32[]{:S(2)}) collective-permute-start(bf16[8,128,128]{2,1,0:T(8,128)(2,1)S(1)} %collective-permute-done.24.rest_4_), channel_id=1, source_target_pairs={{0,2},{1,9},{2,4},{3,11},{4,6},{5,13},{6,0},{7,15},{8,10},{9,17},{... | collective-permute-start | bytes 786440 | tf_op jit(solution)/shard_map/ppermute | solution.py:48
  69.6 3.6 %collective-permute-start.33 = (bf16[8,128,128]{2,1,0:T(8,128)(2,1)S(1)}, bf16[8,128,128]{2,1,0:T(8,128)(2,1)S(1)}, u32[]{:S(2)}, u32[]{:S(2)}) collective-permute-start(bf16[8,128,128]{2,1,0:T(8,128)(2,1)S(1)} %collective-permute-done.31.rest_0_), channel_id=1, source_target_pairs={{0,1},{1,0},{2,3},{3,2},{4,5},{5,4},{6,7},{7,6},{8,9},{9,8},{10,11... | collective-permute-start | bytes 786440 | tf_op jit(solution)/shard_map/ppermute | solution.py:48
  72.1 1.5 %collective-permute-start.34 = (bf16[8,128,128]{2,1,0:T(8,128)(2,1)S(1)}, bf16[8,128,128]{2,1,0:T(8,128)(2,1)S(1)}, u32[]{:S(2)}, u32[]{:S(2)}) collective-permute-start(bf16[8,128,128]{2,1,0:T(8,128)(2,1)S(1)} %collective-permute-done.32.rest_1_), channel_id=1, source_target_pairs={{0,1},{1,0},{2,3},{3,2},{4,5},{5,4},{6,7},{7,6},{8,9},{9,8},{10,11... | collective-permute-start | bytes 786440 | tf_op jit(solution)/shard_map/ppermute | solution.py:48
  75.3 1.4 %collective-permute-start.35 = (bf16[4,128,128]{2,1,0:T(8,128)(2,1)S(1)}, bf16[4,128,128]{2,1,0:T(8,128)(2,1)S(1)}, u32[]{:S(2)}, u32[]{:S(2)}) collective-permute-start(bf16[4,128,128]{2,1,0:T(8,128)(2,1)S(1)} %late.3), channel_id=1, source_target_pairs={{0,1},{1,0},{2,3},{3,2},{4,5},{5,4},{6,7},{7,6},{8,9},{9,8},{10,11... | collective-permute-start | bytes 393224 | tf_op jit(solution)/shard_map/ppermute | solution.py:48
